TPU v7x, 32 devices: a whole 2x2x4 slice. The times are simulated.
32 devices in a mesh: bal: 8 (over z, x), seq: 4 (over y, core).
Axes of the slice: x: 2, y: 2, z: 4, core: 2. Of those that a mesh axis runs over, the one named last changes fastest.
Arguments:
- tokens: bfloat16 [128, 64, 5120], P('bal', 'seq'), may hold values from -6 to 6
- w_qkv: bfloat16 [5120, 24, 384], P('bal', 'seq')
- q_gain: float32 [24, 128], P('seq')
- k_gain: float32 [24, 128], P('seq')
- modulation: float32 [8, 4, 2, 5120], P('bal'), may hold values from -3 to 3
- tile_owner: int32 [128], P('bal'), may hold values from 0 to 7, as said below
- clip_dims: int32 [8, 4, 3], P('bal'), may hold values from 0 to 4, as said below
Outputs:
- attn_out: bfloat16 [128, 64, 3072], P('bal', 'seq')
Inputs may be any that keep to these rules, and one draw needn't show every extreme that they name: `tile_owner`: each owner is named by exactly 16 tiles. The 16 tiles of one bal index name any owner at most 2 times, and in every draw some owner exactly 2 times. `clip_dims`: for each owner the clips' products f h w add up to 16; entries after its last clip are 0; a clip spans at most 2 tile frames, 3 tile rows and 4 tile columns and has 4 tiles or more.
All inputs are finite; a program needn't handle non-finite values.
Results may differ from a plain program's by a relative error of at most 0.006.
Values may be sent and summed in bfloat16 or wider, within the bound.
No kernel may reach another device: no remote copies, remote signals or barrier semaphores. Data moves between devices by JAX's collectives and lax.ppermute only.
A program may use at most 128 MiB of HBM per device.

v0:
```python
import jax
import jax.numpy as jnp
from jax import lax
from jax.experimental import pallas as pl
from jax.experimental.pallas import tpu as pltpu
from jax.sharding import PartitionSpec as P


TILES_OWN = 16
AXES = ("bal", "seq")

eps_norm = 1e-06
score_fill = -1e30


def tile_layout(clip_shape):
    frames_of = clip_shape[:, 0]
    rows_of = clip_shape[:, 1]
    cols_of = clip_shape[:, 2]
    clip_sizes = frames_of * rows_of * cols_of
    clip_ends = jnp.cumsum(clip_sizes)
    clip_starts = clip_ends - clip_sizes
    local_index = jnp.arange(TILES_OWN, dtype=jnp.int32)
    member = jnp.sum((local_index[:, None] >= clip_ends[None, :]).astype(jnp.int32), axis=1)
    onehot = member[:, None] == jnp.arange(clip_shape.shape[0], dtype=jnp.int32)[None, :]

    def select_clip(values):
        return jnp.sum(jnp.where(onehot, values[None, :], 0), axis=1)

    offset = local_index - select_clip(clip_starts)
    height = jnp.maximum(select_clip(rows_of), 1)
    width_tiles = jnp.maximum(select_clip(cols_of), 1)
    frame_index = offset // (height * width_tiles)
    row_index = offset // width_tiles % height
    column = offset % width_tiles

    def within_one(coords):
        return jnp.abs(coords[:, None] - coords[None, :]) <= 1

    tile_mask = (
        (member[:, None] == member[None, :])
        & within_one(frame_index)
        & within_one(row_index)
        & within_one(column)
    )
    return (member.astype(jnp.int32), tile_mask)


def smem():
    return pl.BlockSpec(memory_space=pltpu.SMEM)


def vmem():
    return pl.BlockSpec(memory_space=pltpu.VMEM)


def pick_tiles(tokens, tile_owner, ids, groups, capacity):
    count = tokens.shape[0]

    def body(own_ref, ids_ref, tok_ref, *rest):
        outs, seen, index = rest[:groups], rest[groups], rest[groups + 1]
        for k in range(groups):
            seen[k] = 0
        for k in range(groups * capacity):
            index[k] = 0
        for i in range(count):
            k = lax.rem(own_ref[i] - ids_ref[0] + groups, groups)
            r = seen[k]
            seen[k] = r + 1
            index[k * capacity + r] = i
        for k in range(groups):
            for j in range(capacity):
                outs[k][j] = tok_ref[index[k * capacity + j]]

    shape = jax.ShapeDtypeStruct((capacity,) + tokens.shape[1:], tokens.dtype)
    return pl.pallas_call(
        body,
        out_shape=[shape] * groups,
        in_specs=[smem(), smem(), vmem()],
        out_specs=[vmem()] * groups,
        scratch_shapes=[
            pltpu.SMEM((groups,), jnp.int32),
            pltpu.SMEM((groups * capacity,), jnp.int32),
        ],
        name="pick_tiles",
    )(tile_owner, ids, tokens)


def norm_tiles(pieces, table, member, place, ids, groups):
    capacity, piece, width = pieces[0].shape
    tiles = TILES_OWN
    depth = width // groups

    def body(member_ref, place_ref, ids_ref, table_ref, *rest):
        ins, out_ref, held = rest[:groups], rest[groups], rest[groups + 1]
        for k in range(groups):
            source = lax.rem(ids_ref[1] - k + groups, groups)
            for j in range(capacity):
                held[place_ref[source * capacity + j]] = ins[k][j]

        def one(r, carry):
            values = held[r].astype(jnp.float32)
            center = jnp.mean(values, axis=-1, keepdims=True)
            values = values - center
            spread = jnp.mean(jnp.square(values), axis=-1, keepdims=True)
            values = values * lax.rsqrt(spread + eps_norm)
            rows = table_ref[member_ref[r]]
            done = (values * (1.0 + rows[1:2]) + rows[0:1]).astype(out_ref.dtype)
            at = pl.multiple_of(r * piece, piece)
            for g in range(groups):
                out_ref[g, pl.ds(at, piece), :] = done[:, g * depth : (g + 1) * depth]
            return carry

        lax.fori_loop(0, tiles, one, 0)

    return pl.pallas_call(
        body,
        out_shape=jax.ShapeDtypeStruct((groups, tiles * piece, depth), pieces[0].dtype),
        in_specs=[smem(), smem(), smem(), vmem()] + [vmem()] * groups,
        out_specs=vmem(),
        scratch_shapes=[pltpu.VMEM((tiles + 1, piece, width), pieces[0].dtype)],
        cost_estimate=pl.CostEstimate(
            flops=12 * tiles * piece * width,
            bytes_accessed=4 * tiles * piece * width,
            transcendentals=0,
        ),
        name="norm_tiles",
    )(member, place, ids, table, *pieces)


def project(xs, blocks, at, acc, sums):
    heads, depth, cols = blocks[0].shape
    sizes = [x.shape[1] for x in xs]
    total, m, n = sum(sizes), len(xs), len(blocks)

    def body(at_ref, *refs):
        x_refs, w_refs, rest = refs[: m * n], refs[m * n : (m + 1) * n], list(refs[(m + 1) * n :])
        acc_ref = rest.pop(0) if acc is not None else None
        out_ref = rest.pop(0)
        left = [jnp.concatenate([x_refs[i * n + j][0] for j in range(n)], axis=1) for i in range(m)]
        right = jnp.concatenate([ref[0] for ref in w_refs], axis=0)
        part = jnp.dot(jnp.concatenate(left, axis=0), right, preferred_element_type=jnp.float32)
        if acc is not None:
            part += acc_ref[0]
        out_ref[0] = part
        if sums:
            sums_ref, squares = rest
            head = pl.program_id(0)

            @pl.when(head == 0)
            def _():
                squares[...] = jnp.square(part)

            @pl.when(head > 0)
            def _():
                squares[...] += jnp.square(part)

            @pl.when(head == heads - 1)
            def _():
                lane = lax.broadcasted_iota(jnp.int32, (8, cols), 1)
                row = lax.broadcasted_iota(jnp.int32, (8, cols), 0)
                sums_ref[...] = lax.dot_general(
                    (lane // (cols // 2) == row).astype(jnp.float32),
                    squares[...],
                    (((1,), (1,)), ((), ())),
                    precision=lax.Precision.HIGHEST,
                    preferred_element_type=jnp.float32,
                )

    specs = [pl.BlockSpec((1, size, depth), lambda h, a, j=j: (a[j], 0, 0)) for size in sizes for j in range(n)]
    specs += [pl.BlockSpec((1, depth, cols), lambda h, a: (h, 0, 0))] * n
    args = [x for x in xs for _ in range(n)] + list(blocks)
    acc_spec = pl.BlockSpec((1, total, cols), lambda h, a: (h, 0, 0))
    aliases = {}
    if acc is not None:
        aliases = {1 + len(args): 0}
        specs.append(acc_spec)
        args.append(acc)
    out_shape = [jax.ShapeDtypeStruct((heads, total, cols), jnp.float32)]
    out_specs = [acc_spec]
    scratch = []
    if sums:
        out_shape.append(jax.ShapeDtypeStruct((8, total), jnp.float32))
        out_specs.append(pl.BlockSpec((8, total), lambda h, a: (0, 0)))
        scratch.append(pltpu.VMEM((total, cols), jnp.float32))
    return pl.pallas_call(
        body,
        out_shape=out_shape,
        grid_spec=pltpu.PrefetchScalarGridSpec(
            num_scalar_prefetch=1, grid=(heads,), in_specs=specs, out_specs=out_specs, scratch_shapes=scratch
        ),
        input_output_aliases=aliases,
        cost_estimate=pl.CostEstimate(
            flops=2 * n * total * depth * cols * heads,
            bytes_accessed=2 * n * (total + cols * heads) * depth + 8 * total * cols * heads,
            transcendentals=0,
        ),
        name="project",
    )(at, *args)


def soft_weights(qk, partial_sums, gains, mask, features, first, count):
    heads, total, cols = qk.shape
    dim = cols // 2
    rows = mask.shape[0]
    n = len(partial_sums)

    def body(*refs):
        q_ref, k_ref = refs[0], refs[1]
        sum_refs = refs[2 : 2 + n]
        qg_ref, kg_ref, mask_ref, out_ref, scales, keys = refs[2 + n :]
        head, block = pl.program_id(0), pl.program_id(1)

        @pl.when((head == 0) & (block == 0))
        def _():
            for p in range(n):
                whole = None
                for q in range(n):
                    there = (p // 2 - q // 2) % (n // 2) * 2 + (p % 2 ^ q % 2)
                    part = sum_refs[q][:, there * rows : (there + 1) * rows]
                    whole = part if whole is None else whole + part
                scales[p * rows : (p + 1) * rows] = jnp.transpose(lax.rsqrt(whole / features + eps_norm))

        @pl.when(block == 0)
        def _():
            keys[...] = (k_ref[0] * scales[:, 1:2] * kg_ref[pl.ds(first + head, 1), :]).astype(keys.dtype)

        at = pl.multiple_of(block * rows, rows)
        query = q_ref[0] * scales[pl.ds(at, rows), 0:1] * qg_ref[pl.ds(first + head, 1), :]
        scores = lax.dot_general(
            query.astype(keys.dtype),
            keys[...],
            (((1,), (1,)), ((), ())),
            preferred_element_type=jnp.float32,
        ) * dim ** (-0.5)
        scores = jnp.where(mask_ref[...] > 0.5, scores, score_fill)
        largest = jnp.max(scores, axis=-1, keepdims=True)
        powers = jnp.exp(scores - largest)
        share = 1.0 / jnp.sum(powers, axis=-1, keepdims=True)
        out_ref[0] = (powers * share).astype(out_ref.dtype)

    whole_sum = pl.BlockSpec((8, total), lambda h, b: (0, 0))
    gain = pl.BlockSpec((heads, dim), lambda h, b: (0, 0))
    return pl.pallas_call(
        body,
        out_shape=jax.ShapeDtypeStruct((count, total, total), jnp.bfloat16),
        grid=(count, total // rows),
        in_specs=[
            pl.BlockSpec((1, rows, dim), lambda h, b: (first + h, b, 0)),
            pl.BlockSpec((1, total, dim), lambda h, b: (first + h, 0, 1)),
        ]
        + [whole_sum] * n
        + [gain, gain, pl.BlockSpec(mask.shape, lambda h, b: (0, 0))],
        out_specs=pl.BlockSpec((1, rows, total), lambda h, b: (h, b, 0)),
        scratch_shapes=[pltpu.VMEM((total, 8), jnp.float32), pltpu.VMEM((total, dim), jnp.bfloat16)],
        cost_estimate=pl.CostEstimate(
            flops=(2 * dim + 8) * count * total * total,
            bytes_accessed=count * total * (2 * total + 4 * cols),
            transcendentals=count * total * total,
        ),
        name="soft_weights",
    )(qk, qk, *partial_sums, *gains, mask)


def mix_values(weights, values, order, place, groups, capacity, piece):
    parts, (count, total, _) = len(weights), weights[0].shape
    heads = parts * count
    packed, _, cols = values.shape
    dim = packed * cols // heads
    share = heads // packed
    n = order.shape[0]
    rows = total // n
    full = groups * capacity == TILES_OWN

    def body(order_ref, place_ref, *refs):
        w_refs, (v_ref, out_ref, *staged) = refs[:parts], refs[parts:]
        for i in range(parts):

            @pl.when(pl.program_id(0) // count == i)
            def _(w_ref=w_refs[i]):
                one_head(order_ref, place_ref, w_ref, v_ref, out_ref, staged)

    def one_head(order_ref, place_ref, w_ref, v_ref, out_ref, staged):
        held = v_ref[0].astype(w_ref.dtype)
        mixed = jnp.dot(w_ref[0], held, preferred_element_type=jnp.float32)
        for p in range(n):
            block = mixed[p * rows : (p + 1) * rows]
            if full:
                out_ref[:, order_ref[p]] = block.astype(out_ref.dtype).reshape(groups, capacity * piece, dim)
                continue
            staged[0][...] = block
            for slot in range(groups * capacity):
                tile = jnp.minimum(place_ref[slot], TILES_OWN - 1)
                tile_rows = staged[0][pl.ds(pl.multiple_of(tile * piece, piece), piece), :]
                at = slot % capacity * piece
                out_ref[slot // capacity, order_ref[p], at : at + piece] = tile_rows.astype(out_ref.dtype)

    return pl.pallas_call(
        body,
        out_shape=jax.ShapeDtypeStruct((groups, n, capacity * piece, heads * dim), jnp.bfloat16),
        grid_spec=pltpu.PrefetchScalarGridSpec(
            num_scalar_prefetch=2,
            grid=(heads,),
            in_specs=[
                pl.BlockSpec((1, total, total), lambda h, o, s, i=i: (jnp.clip(h - i * count, 0, count - 1), 0, 0))
                for i in range(parts)
            ]
            + [
                pl.BlockSpec((1, total, dim), lambda h, o, s: (h // share, 0, h % share)),
            ],
            out_specs=pl.BlockSpec((groups, n, capacity * piece, dim), lambda h, o, s: (0, 0, 0, h)),
            scratch_shapes=[pltpu.VMEM((rows, dim), jnp.float32)] * (not full),
        ),
        cost_estimate=pl.CostEstimate(
            flops=2 * heads * total * total * dim,
            bytes_accessed=heads * total * (2 * total + 6 * dim),
            transcendentals=0,
        ),
        name="mix_values",
    )(order, place, *weights, values)


def place_tiles(returned, tile_owner, groups, n, capacity):
    _, rows, width = returned.shape
    piece = rows // capacity
    count = tile_owner.shape[0]

    def body(own_ref, in_ref, out_ref, seen):
        for k in range(groups):
            seen[k] = 0
        for i in range(count):
            owner = own_ref[i]
            rank = seen[owner]
            seen[owner] = rank + 1
            at = pl.multiple_of(rank * piece, piece)
            for g in range(n):
                source = (owner // 2 * 2 + g % 2) * n + g // 2 * 2 + lax.rem(owner, 2)
                out_ref[i, :, g * width : (g + 1) * width] = in_ref[source, pl.ds(at, piece), :]

    return pl.pallas_call(
        body,
        out_shape=jax.ShapeDtypeStruct((count, piece, n * width), returned.dtype),
        in_specs=[smem(), vmem()],
        out_specs=vmem(),
        scratch_shapes=[pltpu.SMEM((groups,), jnp.int32)],
        name="place_tiles",
    )(tile_owner, returned)


def transposed(tokens, w_qkv, q_gain, k_gain, modulation, tile_owner, clip_dims):
    groups, n = lax.axis_size("bal"), lax.axis_size("seq")
    planes, lines = groups // 2, n // 2
    owned_tiles, piece, _ = tokens.shape
    capacity = owned_tiles // min(groups, owned_tiles)
    heads, dim = q_gain.shape
    features = heads * n * dim

    def send(value, to):
        pairs = []
        for b in range(groups):
            for s in range(n):
                z, x, y, c = to(b // 2, b % 2, s // 2, s % 2)
                pairs.append((b * n + s, (z * 2 + x) * n + y * 2 + c))
        return lax.ppermute(value, AXES, pairs)

    def swap(value):
        return send(value, lambda z, x, y, c: (z, c, y, x))

    def ring(value):
        return send(value, lambda z, x, y, c: ((z + 1) % planes, x, y, c))

    def other_core(value):
        return send(value, lambda z, x, y, c: (z, x, y, 1 - c))

    bal, seq = lax.axis_index("bal"), lax.axis_index("seq")
    z, x, y, c = bal // 2, bal % 2, seq // 2, seq % 2
    ids = jnp.stack([bal, z * 2 + c]).astype(jnp.int32)

    outgoing = pick_tiles(tokens, tile_owner, ids, groups, capacity)

    by_head = jnp.transpose(w_qkv, (1, 0, 2))
    pair = 2 if heads % 2 == 0 else 1
    v_columns = by_head[:, :, 2 * dim :]
    v_columns = jnp.concatenate([v_columns[i::pair] for i in range(pair)], axis=2)
    qk_own = [swap(by_head[:, :, : 2 * dim])]

    def to_owner(k):
        def to(z, x, y, c):
            owner = (z * 2 + x + k) % groups
            return owner // 2, c, y, owner % 2

        return to

    arrived = []
    for k in range(groups):
        arrived.append(send(outgoing[k], to_owner(k)))
    table = swap(modulation[0])
    clips = swap(clip_dims[0])
    gains = (swap(q_gain), swap(k_gain))
    member, tile_mask = tile_layout(clips)
    if groups * capacity == TILES_OWN:
        place = jnp.arange(TILES_OWN, dtype=jnp.int32)
    else:
        named = lax.all_gather(tile_owner, "bal", axis=0) == ids[1]
        live = jnp.arange(capacity)[None, :] < jnp.sum(named, axis=1, dtype=jnp.int32)[:, None]
        live = live.reshape(-1)
        place = jnp.where(live, jnp.cumsum(live.astype(jnp.int32)) - 1, TILES_OWN).astype(jnp.int32)
    gated = jnp.maximum(lax.optimization_barrier(member), 0)
    normed = norm_tiles(arrived, table, gated, place, ids, groups)

    def along_x(value):
        return send(value, lambda z, x, y, c: (z, x ^ 1, y, c))

    def along_y(value, py):
        return send(value, lambda z, x, y, c: (z, x, (y - py) % lines, c))

    across = along_x(normed)
    pieces = [normed, across]
    order = [y * 2 + x, y * 2 + (x ^ 1)]
    half = normed.shape[1] // 2
    for py in range(1, lines):
        beside = along_y(normed, py)
        corner = [along_x(beside[:, :half]), along_y(across[:, half:], py)]
        pieces += [beside, *corner]
        order += [(y + py) % lines * 2 + x, (y + py) % lines * 2 + (x ^ 1)]
    order = jnp.stack(order).astype(jnp.int32)

    def after(value, *others):
        return lax.optimization_barrier((value, *others))[0]

    def start_planes(own):
        if planes == 4:
            two = send(own, lambda z, x, y, c: (z ^ 2, x, y, c))
            return [own, send(own, lambda z, x, y, c: (z ^ 1, x, y, c)), two]
        got = [own]
        for _ in range(planes - 2):
            got.append(ring(got[-1]))
        return got

    def end_planes(got, *earlier):
        if planes == 4:
            own, _, two = got
            return [send_some(after(own, two, *earlier), {1: 2, 2: 1}), send_some(after(two, *earlier), {1: 0, 2: 3})]
        return [ring(after(got[-1], *earlier))]

    def last_plane(ends, *earlier):
        return sum(ends[1:], after(ends[0], *earlier))

    def send_some(value, hops):
        pairs = []
        for b in range(groups):
            for s in range(n):
                if b // 2 in hops:
                    pairs.append((b * n + s, (hops[b // 2] * 2 + b % 2) * n + s))
        return lax.ppermute(value, AXES, pairs)

    def plane_at(step):
        return z ^ step if planes == 4 else (z - step) % planes

    def blocks_of(own, steps):
        blocks, at = [], []
        for step in steps:
            blocks += [own[step], other_core(own[step])]
            at += [plane_at(step) * 2 + c, plane_at(step) * 2 + 1 - c]
        return blocks, jnp.stack(at).astype(jnp.int32)

    early, late = range(planes - 1), [planes - 1]
    qk_own = start_planes(after(qk_own[0], outgoing[0]))
    v_first = swap(after(v_columns, outgoing[0]))
    qk_ends = end_planes(qk_own)
    v_own = start_planes(after(v_first, *pieces[-2:]))

    blocks, at = blocks_of(qk_own, early)
    qk, *_ = project(pieces, blocks, at, None, False)
    qk_own.append(last_plane(qk_ends, qk))
    qk, sums = project(pieces, *blocks_of(qk_own, late), qk, True)
    partial_sums = [sums, along_x(sums)]
    for py in range(1, lines):
        partial_sums.append(along_y(sums, py))
        partial_sums.append(send(sums, lambda z, x, y, c: (z, x ^ 1, (y - py) % lines, c)))

    spread = jnp.repeat(jnp.repeat(tile_mask.astype(jnp.float32), piece, axis=0), piece, axis=1)
    mask = jnp.tile(spread, (1, n))
    parts = 2 if heads % 2 == 0 else 1
    weights = []
    for i in range(parts):
        part = soft_weights(qk, partial_sums, gains, mask, features, i * heads // parts, heads // parts)
        weights.append(part)
        if i == 0:
            v_ends = end_planes(v_own, weights[0])
    blocks, at = blocks_of(v_own, early)
    blocks[0] = after(blocks[0], weights[-1])
    values, *_ = project(pieces, blocks, at, None, False)
    v_own.append(last_plane(v_ends, values))
    values, *_ = project(pieces, *blocks_of(v_own, late), values, False)
    mixed = mix_values(weights, values, order, place, groups, capacity, piece)
    returned = lax.all_to_all(
        mixed.reshape(groups * n, capacity * piece, heads * dim), AXES, split_axis=0, concat_axis=0, tiled=True
    )
    return place_tiles(returned, tile_owner, groups, n, capacity)


def solution(mesh):
    return jax.shard_map(
        transposed,
        mesh=mesh,
        in_specs=(
            P("bal", "seq", None),
            P("bal", "seq", None),
            P("seq", None),
            P("seq", None),
            P("bal", None, None, None),
            P("bal"),
            P("bal", None, None),
        ),
        out_specs=P("bal", "seq", None),
        check_vma=False,
    )
```

profile of v0, /device:TPU:0, one launch (start us, length us, event | category | flops | bytes accessed | tf_op | source)
XLA Modules:
  0.0 438.1 jit_solution(13505973411985485841)
XLA Ops:
  0.0 3.0 slice.38
  3.0 2.3 collective-permute-start.14
  6.7 3.5 pick_tiles.1
  12.5 7.4 %collective-permute-start.3 = (bf16[2,16,5120]{2,1,0:T(8,128)(2,1)}, bf16[2,16,5120]{2,1,0:T(8,128)(2,1)S(1)}, u32[]{:S(2)}, u32[]{:S(2)}) collective-permute-start(bf16[2,16,5120]{2,1,0:T(8,128)(2,1)} %get-tuple-element.25), channel_id=1, source_target_pairs={{0,1},{1,5},{2,3},{3,7},{4,8},{5,12},{6,10},{7,14},{8,9},{9,13},{1... | collective-permute-start | bytes 983048 | tf_op jit(solution)/shard_map/ppermute | solution.py:364
  21.5 20.0 %collective-permute-start.5 = (bf16[2,16,5120]{2,1,0:T(8,128)(2,1)}, bf16[2,16,5120]{2,1,0:T(8,128)(2,1)S(1)}, u32[]{:S(2)}, u32[]{:S(2)}) collective-permute-start(bf16[2,16,5120]{2,1,0:T(8,128)(2,1)} %get-tuple-element.27), channel_id=1, source_target_pairs={{0,9},{1,13},{2,11},{3,15},{4,16},{5,20},{6,18},{7,22},{8,17},{9,2... | collective-permute-start | bytes 983048 | tf_op jit(solution)/shard_map/ppermute | solution.py:364
  44.6 2.2 collective-permute-start.8
  46.9 23.2 %collective-permute-done.5.rest_3_ = bf16[2,16,5120]{2,1,0:T(8,128)(2,1)S(1)} collective-permute-done((bf16[2,16,5120]{2,1,0:T(8,128)(2,1)}, bf16[2,16,5120]{2,1,0:T(8,128)(2,1)S(1)}, u32[]{:S(2)}, u32[]{:S(2)}) %collective-permute-start.5) | collective-permute-done | bytes 327712 | tf_op jit(solution)/shard_map/ppermute | solution.py:364
  70.7 5.2 %collective-permute-done.6.rest_4_ = bf16[2,16,5120]{2,1,0:T(8,128)(2,1)} collective-permute-done((bf16[2,16,5120]{2,1,0:T(8,128)(2,1)}, bf16[2,16,5120]{2,1,0:T(8,128)(2,1)}, u32[]{:S(2)}, u32[]{:S(2)}) %collective-permute-start.6) | collective-permute-done | bytes 327712 | tf_op jit(solution)/shard_map/ppermute | solution.py:364
  75.9 3.2 collective-permute-done.9.rest_7_
  79.7 8.5 %norm_tiles.1.refs_0_.refs_1_.refs_2_.refs_3_.refs_4_.refs_5_ = bf16[8,256,640]{2,1,0:T(8,128)(2,1)} custom-call(s32[16]{0:T(128)} %broadcast_maximum_fusion.1.member_ref, s32[16]{0:T(128)} %iota.28.place_ref, s32[2]{0:T(128)} %pad_add_fusion.2.ids_ref, f32[4,2,5120]{2,1,0:T(2,128)} %copy-done.11, bf16[2,16,5120]{2,1,0:T(8,128)(2,1)} %copy-done.7, ...), custom_call_target="tpu_custom_call" | custom-call | flops 15728640 | bytes 5242880 | tf_op jit(solution)/shard_map/norm_tiles/pallas_call | solution.py:116
  89.8 14.6 %collective-permute-start.18 = (bf16[6,640,256]{2,1,0:T(8,128)(2,1)S(1)}, bf16[6,640,256]{2,1,0:T(8,128)(2,1)}, u32[]{:S(2)}, u32[]{:S(2)}) collective-permute-start(bf16[6,640,256]{2,1,0:T(8,128)(2,1)S(1)} %collective-permute-done.14.refs_30_), channel_id=1, source_target_pairs={{0,8},{1,9},{2,10},{3,11},{4,12},{5,13},{6,14},{7,15},{8,0},{9,1},... | collective-permute-start | bytes 5898248 | tf_op jit(solution)/shard_map/ppermute | solution.py:364
  104.4 3.3 collective-permute-start.15
  109.5 34.6 %collective-permute-done.11.refs_12_.refs_13_.refs_14_.refs_15_.refs_16_.refs_17_.refs_4_.refs_5_ = bf16[8,256,640]{2,1,0:T(8,128)(2,1)S(1)} collective-permute-done((bf16[8,256,640]{2,1,0:T(8,128)(2,1)}, bf16[8,256,640]{2,1,0:T(8,128)(2,1)S(1)}, u32[]{:S(2)}, u32[]{:S(2)}) %collective-permute-start.11) | collective-permute-done | bytes 2621472 | tf_op jit(solution)/shard_map/ppermute | solution.py:364
  144.4 42.5 %collective-permute-done.18.refs_32_ = bf16[6,640,256]{2,1,0:T(8,128)(2,1)} collective-permute-done((bf16[6,640,256]{2,1,0:T(8,128)(2,1)S(1)}, bf16[6,640,256]{2,1,0:T(8,128)(2,1)}, u32[]{:S(2)}, u32[]{:S(2)}) %collective-permute-start.18) | collective-permute-done | bytes 1966112 | tf_op jit(solution)/shard_map/ppermute | solution.py:364
  186.9 3.3 collective-permute-start.19
  193.4 1.9 collective-permute-start.16
  199.7 23.2 %collective-permute-done.13.refs_24_.refs_25_.refs_26_.refs_27_.refs_28_.refs_29_.refs_8_.refs_9_ = bf16[8,128,640]{2,1,0:T(8,128)(2,1)} collective-permute-done((bf16[8,128,640]{2,1,0:T(8,128)(2,1)}, bf16[8,128,640]{2,1,0:T(8,128)(2,1)}, u32[]{:S(2)}, u32[]{:S(2)}) %collective-permute-start.13) | collective-permute-done | bytes 1310752 | tf_op jit(solution)/shard_map/ppermute | solution.py:364
  222.9 8.9 %collective-permute-start.28 = (bf16[3,640,256]{2,1,0:T(8,128)(2,1)}, bf16[3,640,256]{2,1,0:T(8,128)(2,1)}, u32[]{:S(2)}, u32[]{:S(2)}) collective-permute-start(bf16[3,640,256]{2,1,0:T(8,128)(2,1)} %pad_maximum_fusion), channel_id=1, source_target_pairs={{0,0},{1,4},{2,2},{3,6},{4,1},{5,5},{6,3},{7,7},{8,8},{9,12},{10,1... | collective-permute-start | bytes 2949128 | tf_op jit(solution)/shard_map/ppermute | solution.py:364
  231.8 20.5 %project.4.refs_12_ = f32[6,1024,256]{2,1,0:T(8,128)} custom-call(s32[6]{0:T(128)} %stack.78.at_ref, bf16[8,256,640]{2,1,0:T(8,128)(2,1)} %norm_tiles.1.refs_0_.refs_1_.refs_2_.refs_3_.refs_4_.refs_5_, bf16[8,256,640]{2,1,0:T(8,128)(2,1)} %norm_tiles.1.refs_0_.refs_1_.refs_2_.refs_3_.refs_4_.refs_5_, ...), custom_call_target="tpu_custom_call" | custom-call | flops 12079595520 | bytes 32243712 | tf_op jit(solution)/shard_map/project/pallas_call | solution.py:186
  252.3 2.6 add.125.refs_10_
  255.1 2.6 collective-permute-start.29
  257.6 5.4 %collective-permute-start.32 = (bf16[3,640,256]{2,1,0:T(8,128)(2,1)}, bf16[3,640,256]{2,1,0:T(8,128)(2,1)}, u32[]{:S(2)}, u32[]{:S(2)}) collective-permute-start(bf16[3,640,256]{2,1,0:T(8,128)(2,1)} %collective-permute-done.28.refs_30_), channel_id=1, source_target_pairs={{0,8},{1,9},{2,10},{3,11},{4,12},{5,13},{6,14},{7,15},{8,0},{9,1},... | collective-permute-start | bytes 2949128 | tf_op jit(solution)/shard_map/ppermute | solution.py:364
  265.1 36.5 %collective-permute-done.29.refs_34_ = bf16[3,640,256]{2,1,0:T(8,128)(2,1)} collective-permute-done((bf16[3,640,256]{2,1,0:T(8,128)(2,1)}, bf16[3,640,256]{2,1,0:T(8,128)(2,1)}, u32[]{:S(2)}, u32[]{:S(2)}) %collective-permute-start.29) | collective-permute-done | bytes 983072 | tf_op jit(solution)/shard_map/ppermute | solution.py:364
  302.2 12.7 %project.5 = (f32[6,1024,256]{2,1,0:T(8,128)}, f32[8,1024]{1,0:T(8,128)}) custom-call(s32[2]{0:T(128)} %pad_add_fusion.1.at_ref, bf16[8,256,640]{2,1,0:T(8,128)(2,1)} %norm_tiles.1.refs_0_.refs_1_.refs_2_.refs_3_.refs_4_.refs_5_, bf16[8,256,640]{2,1,0:T(8,128)(2,1)} %norm_tiles.1.refs_0_.refs_1_.refs_2_.refs_3_.refs_4_.refs_5_, ...), custom_call_target="tpu_custom_call", output_to_operand_aliasing={{0}: (13, {})} | custom-call | flops 4026531840 | bytes 19136512 | tf_op jit(solution)/shard_map/project/pallas_call | solution.py:186
  314.9 3.6 collective-permute-start.23
  326.4 13.5 %soft_weights.2.refs_0_ = bf16[3,1024,1024]{2,1,0:T(8,128)(2,1)} custom-call(f32[6,1024,256]{2,1,0:T(8,128)} %get-tuple-element.35.refs_0_.refs_1_, f32[6,1024,256]{2,1,0:T(8,128)} %get-tuple-element.35.refs_0_.refs_1_, f32[8,1024]{1,0:T(8,128)} %get-tuple-element.36.refs_2_, f32[8,1024]{1,0:T(8,128)} %copy-done.12, f32[8,1024]{1,0:T(8,128)} %copy-done.13, ...), custom_call_target="tpu_custom_call" | custom-call | flops 830472192 | bytes 9437184 | tf_op jit(solution)/shard_map/soft_weights/pallas_call | solution.py:244
  342.0 13.6 %soft_weights.3.refs_1_ = bf16[3,1024,1024]{2,1,0:T(8,128)(2,1)} custom-call(f32[6,1024,256]{2,1,0:T(8,128)} %get-tuple-element.35.refs_0_.refs_1_, f32[6,1024,256]{2,1,0:T(8,128)} %get-tuple-element.35.refs_0_.refs_1_, f32[8,1024]{1,0:T(8,128)} %get-tuple-element.36.refs_2_, f32[8,1024]{1,0:T(8,128)} %copy-done.12, f32[8,1024]{1,0:T(8,128)} %copy-done.13, ...), custom_call_target="tpu_custom_call" | custom-call | flops 830472192 | bytes 9437184 | tf_op jit(solution)/shard_map/soft_weights/pallas_call | solution.py:244
  355.6 12.9 %project.6.refs_12_ = f32[3,1024,256]{2,1,0:T(8,128)} custom-call(s32[6]{0:T(128)} %stack.78.at_ref, bf16[8,256,640]{2,1,0:T(8,128)(2,1)} %norm_tiles.1.refs_0_.refs_1_.refs_2_.refs_3_.refs_4_.refs_5_, bf16[8,256,640]{2,1,0:T(8,128)(2,1)} %norm_tiles.1.refs_0_.refs_1_.refs_2_.refs_3_.refs_4_.refs_5_, ...), custom_call_target="tpu_custom_call" | custom-call | flops 6039797760 | bytes 20054016 | tf_op jit(solution)/shard_map/project/pallas_call | solution.py:186
  372.4 7.5 %project.7.refs_2_ = f32[3,1024,256]{2,1,0:T(8,128)} custom-call(s32[2]{0:T(128)} %pad_add_fusion.1.at_ref, bf16[8,256,640]{2,1,0:T(8,128)(2,1)} %norm_tiles.1.refs_0_.refs_1_.refs_2_.refs_3_.refs_4_.refs_5_, bf16[8,256,640]{2,1,0:T(8,128)(2,1)} %norm_tiles.1.refs_0_.refs_1_.refs_2_.refs_3_.refs_4_.refs_5_, ...), custom_call_target="tpu_custom_call", output_to_operand_aliasing={{}: (13, {})} | custom-call | flops 2013265920 | bytes 10878976 | tf_op jit(solution)/shard_map/project/pallas_call | solution.py:186
  380.4 10.5 %mix_values.1 = bf16[8,4,32,768]{3,2,1,0:T(8,128)(2,1)} custom-call(s32[4]{0:T(128)} %pad_add_fusion.order_ref, s32[16]{0:T(128)} %iota.27.place_ref, bf16[3,1024,1024]{2,1,0:T(8,128)(2,1)} %soft_weights.2.refs_0_, bf16[3,1024,1024]{2,1,0:T(8,128)(2,1)} %soft_weights.3.refs_1_, f32[3,1024,256]{2,1,0:T(8,128)} %project.7.refs_2_), custom_call_target="tpu_custom_call" | custom-call | flops 1610612736 | bytes 17301504 | tf_op jit(solution)/shard_map/mix_values/pallas_call | solution.py:298
  390.9 44.4 %all_to_all.5.in_ref = bf16[32,32,768]{2,1,0:T(8,128)(2,1)} all-to-all(bf16[32,32,768]{2,1,0:T(8,128)(2,1)} %bitcast.24), channel_id=1, replica_groups=mesh['bal'=8,'seq'=4] {'bal','seq'}, dimensions={0} | all-to-all | bytes 3145728 | tf_op jit(solution)/shard_map/all_to_all | solution.py:497
  435.4 2.7 place_tiles.1
  (125 shorter events, 37.6 us)
Async XLA Ops:
  3.0 86.8 %collective-permute-start.14 = (bf16[6,640,256]{2,1,0:T(8,128)(2,1)}, bf16[6,640,256]{2,1,0:T(8,128)(2,1)S(1)}, u32[]{:S(2)}, u32[]{:S(2)}) collective-permute-start(bf16[6,640,256]{2,1,0:T(8,128)(2,1)} %slice.38), channel_id=1, source_target_pairs={{0,0},{1,4},{2,2},{3,6},{4,1},{5,5},{6,3},{7,7},{8,8},{9,12},{10,1... | collective-permute-start | bytes 5898248 | tf_op jit(solution)/shard_map/ppermute | solution.py:364
  5.3 16.2 %collective-permute-start.1 = (f32[4,2,5120]{2,1,0:T(2,128)S(1)}, f32[4,2,5120]{2,1,0:T(2,128)S(1)}, u32[]{:S(2)}, u32[]{:S(2)}) collective-permute-start(f32[4,2,5120]{2,1,0:T(2,128)S(1)} %bitcast.30), channel_id=1, source_target_pairs={{0,0},{1,4},{2,2},{3,6},{4,1},{5,5},{6,3},{7,7},{8,8},{9,12},{10,1... | collective-permute-start | bytes 491528 | tf_op jit(solution)/shard_map/ppermute | solution.py:364
  10.2 31.8 %collective-permute-start.2 = (bf16[2,16,5120]{2,1,0:T(8,128)(2,1)}, bf16[2,16,5120]{2,1,0:T(8,128)(2,1)S(1)}, u32[]{:S(2)}, u32[]{:S(2)}) collective-permute-start(bf16[2,16,5120]{2,1,0:T(8,128)(2,1)} %get-tuple-element.24), channel_id=1, source_target_pairs={{0,0},{1,4},{2,2},{3,6},{4,1},{5,5},{6,3},{7,7},{8,8},{9,12},{10,1... | collective-permute-start | bytes 983048 | tf_op jit(solution)/shard_map/ppermute | solution.py:364
  12.5 31.2 %collective-permute-start.3 = (bf16[2,16,5120]{2,1,0:T(8,128)(2,1)}, bf16[2,16,5120]{2,1,0:T(8,128)(2,1)S(1)}, u32[]{:S(2)}, u32[]{:S(2)}) collective-permute-start(bf16[2,16,5120]{2,1,0:T(8,128)(2,1)} %get-tuple-element.25), channel_id=1, source_target_pairs={{0,1},{1,5},{2,3},{3,7},{4,8},{5,12},{6,10},{7,14},{8,9},{9,13},{1... | collective-permute-start | bytes 983048 | tf_op jit(solution)/shard_map/ppermute | solution.py:364
  19.9 24.7 %collective-permute-start.4 = (bf16[2,16,5120]{2,1,0:T(8,128)(2,1)}, bf16[2,16,5120]{2,1,0:T(8,128)(2,1)S(1)}, u32[]{:S(2)}, u32[]{:S(2)}) collective-permute-start(bf16[2,16,5120]{2,1,0:T(8,128)(2,1)} %get-tuple-element.26), channel_id=1, source_target_pairs={{0,8},{1,12},{2,10},{3,14},{4,9},{5,13},{6,11},{7,15},{8,16},{9,20... | collective-permute-start | bytes 983048 | tf_op jit(solution)/shard_map/ppermute | solution.py:364
  21.5 48.6 %collective-permute-start.5 = (bf16[2,16,5120]{2,1,0:T(8,128)(2,1)}, bf16[2,16,5120]{2,1,0:T(8,128)(2,1)S(1)}, u32[]{:S(2)}, u32[]{:S(2)}) collective-permute-start(bf16[2,16,5120]{2,1,0:T(8,128)(2,1)} %get-tuple-element.27), channel_id=1, source_target_pairs={{0,9},{1,13},{2,11},{3,15},{4,16},{5,20},{6,18},{7,22},{8,17},{9,2... | collective-permute-start | bytes 983048 | tf_op jit(solution)/shard_map/ppermute | solution.py:364
  42.0 34.0 %collective-permute-start.6 = (bf16[2,16,5120]{2,1,0:T(8,128)(2,1)}, bf16[2,16,5120]{2,1,0:T(8,128)(2,1)}, u32[]{:S(2)}, u32[]{:S(2)}) collective-permute-start(bf16[2,16,5120]{2,1,0:T(8,128)(2,1)} %get-tuple-element.28), channel_id=1, source_target_pairs={{0,16},{1,20},{2,18},{3,22},{4,17},{5,21},{6,19},{7,23},{8,24},{9,... | collective-permute-start | bytes 983048 | tf_op jit(solution)/shard_map/ppermute | solution.py:364
  43.7 32.2 %collective-permute-start.7 = (bf16[2,16,5120]{2,1,0:T(8,128)(2,1)}, bf16[2,16,5120]{2,1,0:T(8,128)(2,1)}, u32[]{:S(2)}, u32[]{:S(2)}) collective-permute-start(bf16[2,16,5120]{2,1,0:T(8,128)(2,1)} %get-tuple-element.29), channel_id=1, source_target_pairs={{0,17},{1,21},{2,19},{3,23},{4,24},{5,28},{6,26},{7,30},{8,25},{9,... | collective-permute-start | bytes 983048 | tf_op jit(solution)/shard_map/ppermute | solution.py:364
  44.6 31.3 %collective-permute-start.8 = (bf16[2,16,5120]{2,1,0:T(8,128)(2,1)}, bf16[2,16,5120]{2,1,0:T(8,128)(2,1)}, u32[]{:S(2)}, u32[]{:S(2)}) collective-permute-start(bf16[2,16,5120]{2,1,0:T(8,128)(2,1)} %get-tuple-element.30), channel_id=1, source_target_pairs={{0,24},{1,28},{2,26},{3,30},{4,25},{5,29},{6,27},{7,31},{8,0},{9,4... | collective-permute-start | bytes 983048 | tf_op jit(solution)/shard_map/ppermute | solution.py:364
  70.1 9.0 %collective-permute-start.9 = (bf16[2,16,5120]{2,1,0:T(8,128)(2,1)}, bf16[2,16,5120]{2,1,0:T(8,128)(2,1)}, u32[]{:S(2)}, u32[]{:S(2)}) collective-permute-start(bf16[2,16,5120]{2,1,0:T(8,128)(2,1)} %get-tuple-element.31), channel_id=1, source_target_pairs={{0,25},{1,29},{2,27},{3,31},{4,0},{5,4},{6,2},{7,6},{8,1},{9,5},{1... | collective-permute-start | bytes 983048 | tf_op jit(solution)/shard_map/ppermute | solution.py:364
  88.3 55.9 %collective-permute-start.11 = (bf16[8,256,640]{2,1,0:T(8,128)(2,1)}, bf16[8,256,640]{2,1,0:T(8,128)(2,1)S(1)}, u32[]{:S(2)}, u32[]{:S(2)}) collective-permute-start(bf16[8,256,640]{2,1,0:T(8,128)(2,1)} %norm_tiles.1.refs_0_.refs_1_.refs_2_.refs_3_.refs_4_.refs_5_), channel_id=1, source_target_pairs={{0,2},{1,3},{2,0},{3,1},{4,6},{5,7},{6,4},{7,5},{8,10},{9,11},{10,... | collective-permute-start | bytes 7864328 | tf_op jit(solution)/shard_map/ppermute | solution.py:364
  89.8 100.4 %collective-permute-start.10 = (bf16[8,256,640]{2,1,0:T(8,128)(2,1)}, bf16[8,256,640]{2,1,0:T(8,128)(2,1)S(1)}, u32[]{:S(2)}, u32[]{:S(2)}) collective-permute-start(bf16[8,256,640]{2,1,0:T(8,128)(2,1)} %norm_tiles.1.refs_0_.refs_1_.refs_2_.refs_3_.refs_4_.refs_5_), channel_id=1, source_target_pairs={{0,4},{1,5},{2,6},{3,7},{4,0},{5,1},{6,2},{7,3},{8,12},{9,13},{10,... | collective-permute-start | bytes 7864328 | tf_op jit(solution)/shard_map/ppermute | solution.py:364
  89.8 97.1 %collective-permute-start.18 = (bf16[6,640,256]{2,1,0:T(8,128)(2,1)S(1)}, bf16[6,640,256]{2,1,0:T(8,128)(2,1)}, u32[]{:S(2)}, u32[]{:S(2)}) collective-permute-start(bf16[6,640,256]{2,1,0:T(8,128)(2,1)S(1)} %collective-permute-done.14.refs_30_), channel_id=1, source_target_pairs={{0,8},{1,9},{2,10},{3,11},{4,12},{5,13},{6,14},{7,15},{8,0},{9,1},... | collective-permute-start | bytes 5898248 | tf_op jit(solution)/shard_map/ppermute | solution.py:364
  104.4 85.7 %collective-permute-start.15 = (bf16[6,640,256]{2,1,0:T(8,128)(2,1)S(1)}, bf16[6,640,256]{2,1,0:T(8,128)(2,1)}, u32[]{:S(2)}, u32[]{:S(2)}) collective-permute-start(bf16[6,640,256]{2,1,0:T(8,128)(2,1)S(1)} %collective-permute-done.14.refs_30_), channel_id=1, source_target_pairs={{0,16},{1,17},{2,18},{3,19},{4,20},{5,21},{6,22},{7,23},{8,24},{9,... | collective-permute-start | bytes 5898248 | tf_op jit(solution)/shard_map/ppermute | solution.py:364
  107.8 84.3 %collective-permute-start.17 = (bf16[6,640,256]{2,1,0:T(8,128)(2,1)S(1)}, bf16[6,640,256]{2,1,0:T(8,128)(2,1)S(1)}, u32[]{:S(2)}, u32[]{:S(2)}) collective-permute-start(bf16[6,640,256]{2,1,0:T(8,128)(2,1)S(1)} %collective-permute-done.14.refs_30_), channel_id=1, source_target_pairs={{0,1},{1,0},{2,3},{3,2},{4,5},{5,4},{6,7},{7,6},{8,9},{9,8},{10,11... | collective-permute-start | bytes 5898248 | tf_op jit(solution)/shard_map/ppermute | solution.py:364
  144.3 51.0 %collective-permute-start.12 = (bf16[8,128,640]{2,1,0:T(8,128)(2,1)S(1)}, bf16[8,128,640]{2,1,0:T(8,128)(2,1)}, u32[]{:S(2)}, u32[]{:S(2)}) collective-permute-start(bf16[8,128,640]{2,1,0:T(8,128)(2,1)S(1)} %slice.36), channel_id=1, source_target_pairs={{0,4},{1,5},{2,6},{3,7},{4,0},{5,1},{6,2},{7,3},{8,12},{9,13},{10,... | collective-permute-start | bytes 3932168 | tf_op jit(solution)/shard_map/ppermute | solution.py:364
  186.9 44.9 %collective-permute-start.19 = (bf16[6,640,256]{2,1,0:T(8,128)(2,1)}, bf16[6,640,256]{2,1,0:T(8,128)(2,1)}, u32[]{:S(2)}, u32[]{:S(2)}) collective-permute-start(bf16[6,640,256]{2,1,0:T(8,128)(2,1)} %collective-permute-done.18.refs_32_), channel_id=1, source_target_pairs={{0,1},{1,0},{2,3},{3,2},{4,5},{5,4},{6,7},{7,6},{8,9},{9,8},{10,11... | collective-permute-start | bytes 5898248 | tf_op jit(solution)/shard_map/ppermute | solution.py:364
  190.2 41.7 %collective-permute-start.20 = (bf16[6,640,256]{2,1,0:T(8,128)(2,1)}, bf16[6,640,256]{2,1,0:T(8,128)(2,1)}, u32[]{:S(2)}, u32[]{:S(2)}) collective-permute-start(bf16[6,640,256]{2,1,0:T(8,128)(2,1)} %collective-permute-done.15.refs_34_), channel_id=1, source_target_pairs={{0,1},{1,0},{2,3},{3,2},{4,5},{5,4},{6,7},{7,6},{8,9},{9,8},{10,11... | collective-permute-start | bytes 5898248 | tf_op jit(solution)/shard_map/ppermute | solution.py:364
  191.5 31.5 %collective-permute-start.13 = (bf16[8,128,640]{2,1,0:T(8,128)(2,1)}, bf16[8,128,640]{2,1,0:T(8,128)(2,1)}, u32[]{:S(2)}, u32[]{:S(2)}) collective-permute-start(bf16[8,128,640]{2,1,0:T(8,128)(2,1)} %slice.37), channel_id=1, source_target_pairs={{0,2},{1,3},{2,0},{3,1},{4,6},{5,7},{6,4},{7,5},{8,10},{9,11},{10,... | collective-permute-start | bytes 3932168 | tf_op jit(solution)/shard_map/ppermute | solution.py:364
  193.4 58.9 %collective-permute-start.16 = (bf16[6,640,256]{2,1,0:T(8,128)(2,1)S(1)}, bf16[6,640,256]{2,1,0:T(8,128)(2,1)}, u32[]{:S(2)}, u32[]{:S(2)}) collective-permute-start(bf16[6,640,256]{2,1,0:T(8,128)(2,1)S(1)} %collective-permute-done.14.refs_30_), channel_id=1, source_target_pairs={{8,16},{9,17},{10,18},{11,19},{12,20},{13,21},{14,22},{15,23},{16,... | collective-permute-start | bytes 5898248 | tf_op jit(solution)/shard_map/ppermute | solution.py:455
  195.3 57.0 %collective-permute-start.21 = (bf16[6,640,256]{2,1,0:T(8,128)(2,1)}, bf16[6,640,256]{2,1,0:T(8,128)(2,1)}, u32[]{:S(2)}, u32[]{:S(2)}) collective-permute-start(bf16[6,640,256]{2,1,0:T(8,128)(2,1)} %collective-permute-done.15.refs_34_), channel_id=1, source_target_pairs={{8,0},{9,1},{10,2},{11,3},{12,4},{13,5},{14,6},{15,7},{16,24},{17,... | collective-permute-start | bytes 5898248 | tf_op jit(solution)/shard_map/ppermute | solution.py:455
  222.9 32.1 %collective-permute-start.28 = (bf16[3,640,256]{2,1,0:T(8,128)(2,1)}, bf16[3,640,256]{2,1,0:T(8,128)(2,1)}, u32[]{:S(2)}, u32[]{:S(2)}) collective-permute-start(bf16[3,640,256]{2,1,0:T(8,128)(2,1)} %pad_maximum_fusion), channel_id=1, source_target_pairs={{0,0},{1,4},{2,2},{3,6},{4,1},{5,5},{6,3},{7,7},{8,8},{9,12},{10,1... | collective-permute-start | bytes 2949128 | tf_op jit(solution)/shard_map/ppermute | solution.py:364
  255.0 47.1 %collective-permute-start.22 = (bf16[6,640,256]{2,1,0:T(8,128)(2,1)S(1)}, bf16[6,640,256]{2,1,0:T(8,128)(2,1)}, u32[]{:S(2)}, u32[]{:S(2)}) collective-permute-start(bf16[6,640,256]{2,1,0:T(8,128)(2,1)S(1)} %add.125.refs_10_), channel_id=1, source_target_pairs={{0,1},{1,0},{2,3},{3,2},{4,5},{5,4},{6,7},{7,6},{8,9},{9,8},{10,11... | collective-permute-start | bytes 5898248 | tf_op jit(solution)/shard_map/ppermute | solution.py:364
  255.1 46.5 %collective-permute-start.29 = (bf16[3,640,256]{2,1,0:T(8,128)(2,1)}, bf16[3,640,256]{2,1,0:T(8,128)(2,1)}, u32[]{:S(2)}, u32[]{:S(2)}) collective-permute-start(bf16[3,640,256]{2,1,0:T(8,128)(2,1)} %collective-permute-done.28.refs_30_), channel_id=1, source_target_pairs={{0,16},{1,17},{2,18},{3,19},{4,20},{5,21},{6,22},{7,23},{8,24},{9,... | collective-permute-start | bytes 2949128 | tf_op jit(solution)/shard_map/ppermute | solution.py:364
  257.6 44.1 %collective-permute-start.32 = (bf16[3,640,256]{2,1,0:T(8,128)(2,1)}, bf16[3,640,256]{2,1,0:T(8,128)(2,1)}, u32[]{:S(2)}, u32[]{:S(2)}) collective-permute-start(bf16[3,640,256]{2,1,0:T(8,128)(2,1)} %collective-permute-done.28.refs_30_), channel_id=1, source_target_pairs={{0,8},{1,9},{2,10},{3,11},{4,12},{5,13},{6,14},{7,15},{8,0},{9,1},... | collective-permute-start | bytes 2949128 | tf_op jit(solution)/shard_map/ppermute | solution.py:364
  263.0 51.9 %collective-permute-start.26 = (f32[6,128]{1,0:T(8,128)S(1)}, f32[6,128]{1,0:T(8,128)S(1)}, u32[]{:S(2)}, u32[]{:S(2)}) collective-permute-start(f32[6,128]{1,0:T(8,128)S(1)} %copy-done.19), channel_id=1, source_target_pairs={{0,0},{1,4},{2,2},{3,6},{4,1},{5,5},{6,3},{7,7},{8,8},{9,12},{10,1... | collective-permute-start | bytes 9224 | tf_op jit(solution)/shard_map/ppermute | solution.py:364
  263.7 55.1 %collective-permute-start.27 = (f32[6,128]{1,0:T(8,128)S(1)}, f32[6,128]{1,0:T(8,128)S(1)}, u32[]{:S(2)}, u32[]{:S(2)}) collective-permute-start(f32[6,128]{1,0:T(8,128)S(1)} %copy-done.20), channel_id=1, source_target_pairs={{0,0},{1,4},{2,2},{3,6},{4,1},{5,5},{6,3},{7,7},{8,8},{9,12},{10,1... | collective-permute-start | bytes 9224 | tf_op jit(solution)/shard_map/ppermute | solution.py:364
  301.6 54.0 %collective-permute-start.31 = (bf16[3,640,256]{2,1,0:T(8,128)(2,1)}, bf16[3,640,256]{2,1,0:T(8,128)(2,1)}, u32[]{:S(2)}, u32[]{:S(2)}) collective-permute-start(bf16[3,640,256]{2,1,0:T(8,128)(2,1)} %collective-permute-done.28.refs_30_), channel_id=1, source_target_pairs={{0,1},{1,0},{2,3},{3,2},{4,5},{5,4},{6,7},{7,6},{8,9},{9,8},{10,11... | collective-permute-start | bytes 2949128 | tf_op jit(solution)/shard_map/ppermute | solution.py:364
  301.7 53.9 %collective-permute-start.33 = (bf16[3,640,256]{2,1,0:T(8,128)(2,1)}, bf16[3,640,256]{2,1,0:T(8,128)(2,1)}, u32[]{:S(2)}, u32[]{:S(2)}) collective-permute-start(bf16[3,640,256]{2,1,0:T(8,128)(2,1)} %collective-permute-done.32.refs_32_), channel_id=1, source_target_pairs={{0,1},{1,0},{2,3},{3,2},{4,5},{5,4},{6,7},{7,6},{8,9},{9,8},{10,11... | collective-permute-start | bytes 2949128 | tf_op jit(solution)/shard_map/ppermute | solution.py:364
  302.1 53.5 %collective-permute-start.34 = (bf16[3,640,256]{2,1,0:T(8,128)(2,1)}, bf16[3,640,256]{2,1,0:T(8,128)(2,1)}, u32[]{:S(2)}, u32[]{:S(2)}) collective-permute-start(bf16[3,640,256]{2,1,0:T(8,128)(2,1)} %collective-permute-done.29.refs_34_), channel_id=1, source_target_pairs={{0,1},{1,0},{2,3},{3,2},{4,5},{5,4},{6,7},{7,6},{8,9},{9,8},{10,11... | collective-permute-start | bytes 2949128 | tf_op jit(solution)/shard_map/ppermute | solution.py:364
  339.8 28.7 %collective-permute-start.30 = (bf16[3,640,256]{2,1,0:T(8,128)(2,1)}, bf16[3,640,256]{2,1,0:T(8,128)(2,1)S(1)}, u32[]{:S(2)}, u32[]{:S(2)}) collective-permute-start(bf16[3,640,256]{2,1,0:T(8,128)(2,1)} %collective-permute-done.28.refs_30_), channel_id=1, source_target_pairs={{8,16},{9,17},{10,18},{11,19},{12,20},{13,21},{14,22},{15,23},{16,... | collective-permute-start | bytes 2949128 | tf_op jit(solution)/shard_map/ppermute | solution.py:455
  340.6 28.0 %collective-permute-start.35 = (bf16[3,640,256]{2,1,0:T(8,128)(2,1)}, bf16[3,640,256]{2,1,0:T(8,128)(2,1)S(1)}, u32[]{:S(2)}, u32[]{:S(2)}) collective-permute-start(bf16[3,640,256]{2,1,0:T(8,128)(2,1)} %collective-permute-done.29.refs_34_), channel_id=1, source_target_pairs={{8,0},{9,1},{10,2},{11,3},{12,4},{13,5},{14,6},{15,7},{16,24},{17,... | collective-permute-start | bytes 2949128 | tf_op jit(solution)/shard_map/ppermute | solution.py:455
  (26 other events, 504.3 us)
where the time goes:
time: 440 us; the launch traced here: 438 us
  waiting for transfers between devices  173 us (39%)
  Pallas kernels  106 us (24%)
  starting transfers between devices  94.6 us (22%)
  blocking collectives  44.4 us (10%)
  local copies, waits for them, and re-layouts  12.4 us (3%)
  other arithmetic  7.25 us (2%)
    ppermute x33, waiting for transfers between devices, send(): return lax.ppermute(value, AXES, pairs)  173 us
    ppermute x33, starting transfers between devices, send(): return lax.ppermute(value, AXES, pairs)  89.2 us
    pallas_call x4, Pallas kernels, project(): pl.pallas_call(body, out_shape=out_shape, grid_spec=pltpu.PrefetchScalarG...  53.5 us
    all_to_all x1, blocking collectives, transposed(): lax.all_to_all(mixed.reshape(groups * n, capacity * piece, heads * dim),...  44.4 us
    pallas_call x2, Pallas kernels, soft_weights(): pl.pallas_call(body, out_shape=jax.ShapeDtypeStruct((count, total, total)...  27 us
    pallas_call x1, Pallas kernels, mix_values(): pl.pallas_call(body, out_shape=jax.ShapeDtypeStruct((groups, n, capacity...  10.5 us
  transfers between devices with their start and end apart: 37, of which 11 were waited for; matrix products, arithmetic and copies ran while one was open for 3% of the time, Pallas kernels for 19%

commit v1 on v0

--- a/solution.py
+++ b/solution.py
@@ -428,10 +428,10 @@
     def after(value, *others):
         return lax.optimization_barrier((value, *others))[0]
 
-    def start_planes(own):
+    def start_planes(own, *earlier):
         if planes == 4:
-            two = send(own, lambda z, x, y, c: (z ^ 2, x, y, c))
-            return [own, send(own, lambda z, x, y, c: (z ^ 1, x, y, c)), two]
+            one = send(own, lambda z, x, y, c: (z ^ 1, x, y, c))
+            return [own, one, send(after(own, *earlier), lambda z, x, y, c: (z ^ 2, x, y, c))]
         got = [own]
         for _ in range(planes - 2):
             got.append(ring(got[-1]))
@@ -465,7 +465,7 @@
         return blocks, jnp.stack(at).astype(jnp.int32)
 
     early, late = range(planes - 1), [planes - 1]
-    qk_own = start_planes(after(qk_own[0], outgoing[0]))
+    qk_own = start_planes(after(qk_own[0], outgoing[0]), *arrived)
     v_first = swap(after(v_columns, outgoing[0]))
     qk_ends = end_planes(qk_own)
     v_own = start_planes(after(v_first, *pieces[-2:]))

time: 440 us -> 440 us (level)
  no operation moved by 1% of the time
where the time goes in v1:
time: 440 us; the launch traced here: 438 us
  waiting for transfers between devices  173 us (39%)
  Pallas kernels  106 us (24%)
  starting transfers between devices  94.6 us (22%)
  blocking collectives  44.4 us (10%)
  local copies, waits for them, and re-layouts  12.4 us (3%)
  other arithmetic  7.25 us (2%)
    ppermute x33, waiting for transfers between devices, send(): return lax.ppermute(value, AXES, pairs)  173 us
    ppermute x33, starting transfers between devices, send(): return lax.ppermute(value, AXES, pairs)  89.2 us
    pallas_call x4, Pallas kernels, project(): pl.pallas_call(body, out_shape=out_shape, grid_spec=pltpu.PrefetchScalarG...  53.5 us
    all_to_all x1, blocking collectives, transposed(): lax.all_to_all(mixed.reshape(groups * n, capacity * piece, heads * dim),...  44.4 us
    pallas_call x2, Pallas kernels, soft_weights(): pl.pallas_call(body, out_shape=jax.ShapeDtypeStruct((count, total, total)...  27 us
    pallas_call x1, Pallas kernels, mix_values(): pl.pallas_call(body, out_shape=jax.ShapeDtypeStruct((groups, n, capacity...  10.5 us
  transfers between devices with their start and end apart: 37, of which 11 were waited for; matrix products, arithmetic and copies ran while one was open for 3% of the time, Pallas kernels for 19%

profile of v1, /device:TPU:0, one launch (start us, length us, event | category | flops | bytes accessed | tf_op | source)
XLA Modules:
  0.0 438.1 jit_solution(13505973411985485841)
XLA Ops:
  0.0 3.0 slice.38
  3.0 2.3 collective-permute-start.14
  6.7 3.5 pick_tiles.1
  12.5 7.4 %collective-permute-start.3 = (bf16[2,16,5120]{2,1,0:T(8,128)(2,1)}, bf16[2,16,5120]{2,1,0:T(8,128)(2,1)S(1)}, u32[]{:S(2)}, u32[]{:S(2)}) collective-permute-start(bf16[2,16,5120]{2,1,0:T(8,128)(2,1)} %get-tuple-element.26), channel_id=1, source_target_pairs={{0,1},{1,5},{2,3},{3,7},{4,8},{5,12},{6,10},{7,14},{8,9},{9,13},{1... | collective-permute-start | bytes 983048 | tf_op jit(solution)/shard_map/ppermute | solution.py:364
  21.5 20.0 %collective-permute-start.5 = (bf16[2,16,5120]{2,1,0:T(8,128)(2,1)}, bf16[2,16,5120]{2,1,0:T(8,128)(2,1)S(1)}, u32[]{:S(2)}, u32[]{:S(2)}) collective-permute-start(bf16[2,16,5120]{2,1,0:T(8,128)(2,1)} %get-tuple-element.28), channel_id=1, source_target_pairs={{0,9},{1,13},{2,11},{3,15},{4,16},{5,20},{6,18},{7,22},{8,17},{9,2... | collective-permute-start | bytes 983048 | tf_op jit(solution)/shard_map/ppermute | solution.py:364
  44.6 2.2 collective-permute-start.8
  46.9 23.2 %collective-permute-done.5.rest_3_ = bf16[2,16,5120]{2,1,0:T(8,128)(2,1)S(1)} collective-permute-done((bf16[2,16,5120]{2,1,0:T(8,128)(2,1)}, bf16[2,16,5120]{2,1,0:T(8,128)(2,1)S(1)}, u32[]{:S(2)}, u32[]{:S(2)}) %collective-permute-start.5) | collective-permute-done | bytes 327712 | tf_op jit(solution)/shard_map/ppermute | solution.py:364
  70.7 5.2 %collective-permute-done.6.rest_4_ = bf16[2,16,5120]{2,1,0:T(8,128)(2,1)} collective-permute-done((bf16[2,16,5120]{2,1,0:T(8,128)(2,1)}, bf16[2,16,5120]{2,1,0:T(8,128)(2,1)}, u32[]{:S(2)}, u32[]{:S(2)}) %collective-permute-start.6) | collective-permute-done | bytes 327712 | tf_op jit(solution)/shard_map/ppermute | solution.py:364
  75.9 3.2 collective-permute-done.9.rest_7_
  79.7 8.5 %norm_tiles.1.refs_0_.refs_1_.refs_2_.refs_3_.refs_4_.refs_5_ = bf16[8,256,640]{2,1,0:T(8,128)(2,1)} custom-call(s32[16]{0:T(128)} %broadcast_maximum_fusion.1.member_ref, s32[16]{0:T(128)} %iota.28.place_ref, s32[2]{0:T(128)} %pad_add_fusion.2.ids_ref, f32[4,2,5120]{2,1,0:T(2,128)} %copy-done.11, bf16[2,16,5120]{2,1,0:T(8,128)(2,1)} %copy-done.7, ...), custom_call_target="tpu_custom_call" | custom-call | flops 15728640 | bytes 5242880 | tf_op jit(solution)/shard_map/norm_tiles/pallas_call | solution.py:116
  89.8 14.6 %collective-permute-start.18 = (bf16[6,640,256]{2,1,0:T(8,128)(2,1)S(1)}, bf16[6,640,256]{2,1,0:T(8,128)(2,1)}, u32[]{:S(2)}, u32[]{:S(2)}) collective-permute-start(bf16[6,640,256]{2,1,0:T(8,128)(2,1)S(1)} %collective-permute-done.14.refs_30_), channel_id=1, source_target_pairs={{0,8},{1,9},{2,10},{3,11},{4,12},{5,13},{6,14},{7,15},{8,0},{9,1},... | collective-permute-start | bytes 5898248 | tf_op jit(solution)/shard_map/ppermute | solution.py:364
  104.4 3.3 collective-permute-start.15
  109.5 34.6 %collective-permute-done.11.refs_12_.refs_13_.refs_14_.refs_15_.refs_16_.refs_17_.refs_4_.refs_5_ = bf16[8,256,640]{2,1,0:T(8,128)(2,1)S(1)} collective-permute-done((bf16[8,256,640]{2,1,0:T(8,128)(2,1)}, bf16[8,256,640]{2,1,0:T(8,128)(2,1)S(1)}, u32[]{:S(2)}, u32[]{:S(2)}) %collective-permute-start.11) | collective-permute-done | bytes 2621472 | tf_op jit(solution)/shard_map/ppermute | solution.py:364
  144.4 42.5 %collective-permute-done.18.refs_32_ = bf16[6,640,256]{2,1,0:T(8,128)(2,1)} collective-permute-done((bf16[6,640,256]{2,1,0:T(8,128)(2,1)S(1)}, bf16[6,640,256]{2,1,0:T(8,128)(2,1)}, u32[]{:S(2)}, u32[]{:S(2)}) %collective-permute-start.18) | collective-permute-done | bytes 1966112 | tf_op jit(solution)/shard_map/ppermute | solution.py:364
  186.9 3.3 collective-permute-start.19
  193.4 1.9 collective-permute-start.16
  199.7 23.2 %collective-permute-done.13.refs_24_.refs_25_.refs_26_.refs_27_.refs_28_.refs_29_.refs_8_.refs_9_ = bf16[8,128,640]{2,1,0:T(8,128)(2,1)} collective-permute-done((bf16[8,128,640]{2,1,0:T(8,128)(2,1)}, bf16[8,128,640]{2,1,0:T(8,128)(2,1)}, u32[]{:S(2)}, u32[]{:S(2)}) %collective-permute-start.13) | collective-permute-done | bytes 1310752 | tf_op jit(solution)/shard_map/ppermute | solution.py:364
  222.9 8.9 %collective-permute-start.28 = (bf16[3,640,256]{2,1,0:T(8,128)(2,1)}, bf16[3,640,256]{2,1,0:T(8,128)(2,1)}, u32[]{:S(2)}, u32[]{:S(2)}) collective-permute-start(bf16[3,640,256]{2,1,0:T(8,128)(2,1)} %pad_maximum_fusion), channel_id=1, source_target_pairs={{0,0},{1,4},{2,2},{3,6},{4,1},{5,5},{6,3},{7,7},{8,8},{9,12},{10,1... | collective-permute-start | bytes 2949128 | tf_op jit(solution)/shard_map/ppermute | solution.py:364
  231.8 20.5 %project.4.refs_12_ = f32[6,1024,256]{2,1,0:T(8,128)} custom-call(s32[6]{0:T(128)} %stack.78.at_ref, bf16[8,256,640]{2,1,0:T(8,128)(2,1)} %norm_tiles.1.refs_0_.refs_1_.refs_2_.refs_3_.refs_4_.refs_5_, bf16[8,256,640]{2,1,0:T(8,128)(2,1)} %norm_tiles.1.refs_0_.refs_1_.refs_2_.refs_3_.refs_4_.refs_5_, ...), custom_call_target="tpu_custom_call" | custom-call | flops 12079595520 | bytes 32243712 | tf_op jit(solution)/shard_map/project/pallas_call | solution.py:186
  252.3 2.6 add.125.refs_10_
  255.1 2.6 collective-permute-start.29
  257.6 5.4 %collective-permute-start.32 = (bf16[3,640,256]{2,1,0:T(8,128)(2,1)}, bf16[3,640,256]{2,1,0:T(8,128)(2,1)}, u32[]{:S(2)}, u32[]{:S(2)}) collective-permute-start(bf16[3,640,256]{2,1,0:T(8,128)(2,1)} %collective-permute-done.28.refs_30_), channel_id=1, source_target_pairs={{0,8},{1,9},{2,10},{3,11},{4,12},{5,13},{6,14},{7,15},{8,0},{9,1},... | collective-permute-start | bytes 2949128 | tf_op jit(solution)/shard_map/ppermute | solution.py:364
  265.1 36.5 %collective-permute-done.29.refs_34_ = bf16[3,640,256]{2,1,0:T(8,128)(2,1)} collective-permute-done((bf16[3,640,256]{2,1,0:T(8,128)(2,1)}, bf16[3,640,256]{2,1,0:T(8,128)(2,1)}, u32[]{:S(2)}, u32[]{:S(2)}) %collective-permute-start.29) | collective-permute-done | bytes 983072 | tf_op jit(solution)/shard_map/ppermute | solution.py:364
  302.2 12.7 %project.5 = (f32[6,1024,256]{2,1,0:T(8,128)}, f32[8,1024]{1,0:T(8,128)}) custom-call(s32[2]{0:T(128)} %pad_add_fusion.1.at_ref, bf16[8,256,640]{2,1,0:T(8,128)(2,1)} %norm_tiles.1.refs_0_.refs_1_.refs_2_.refs_3_.refs_4_.refs_5_, bf16[8,256,640]{2,1,0:T(8,128)(2,1)} %norm_tiles.1.refs_0_.refs_1_.refs_2_.refs_3_.refs_4_.refs_5_, ...), custom_call_target="tpu_custom_call", output_to_operand_aliasing={{0}: (13, {})} | custom-call | flops 4026531840 | bytes 19136512 | tf_op jit(solution)/shard_map/project/pallas_call | solution.py:186
  314.9 3.6 collective-permute-start.23
  326.4 13.5 %soft_weights.2.refs_0_ = bf16[3,1024,1024]{2,1,0:T(8,128)(2,1)} custom-call(f32[6,1024,256]{2,1,0:T(8,128)} %get-tuple-element.37.refs_0_.refs_1_, f32[6,1024,256]{2,1,0:T(8,128)} %get-tuple-element.37.refs_0_.refs_1_, f32[8,1024]{1,0:T(8,128)} %get-tuple-element.38.refs_2_, f32[8,1024]{1,0:T(8,128)} %copy-done.12, f32[8,1024]{1,0:T(8,128)} %copy-done.13, ...), custom_call_target="tpu_custom_call" | custom-call | flops 830472192 | bytes 9437184 | tf_op jit(solution)/shard_map/soft_weights/pallas_call | solution.py:244
  342.0 13.6 %soft_weights.3.refs_1_ = bf16[3,1024,1024]{2,1,0:T(8,128)(2,1)} custom-call(f32[6,1024,256]{2,1,0:T(8,128)} %get-tuple-element.37.refs_0_.refs_1_, f32[6,1024,256]{2,1,0:T(8,128)} %get-tuple-element.37.refs_0_.refs_1_, f32[8,1024]{1,0:T(8,128)} %get-tuple-element.38.refs_2_, f32[8,1024]{1,0:T(8,128)} %copy-done.12, f32[8,1024]{1,0:T(8,128)} %copy-done.13, ...), custom_call_target="tpu_custom_call" | custom-call | flops 830472192 | bytes 9437184 | tf_op jit(solution)/shard_map/soft_weights/pallas_call | solution.py:244
  355.6 12.9 %project.6.refs_12_ = f32[3,1024,256]{2,1,0:T(8,128)} custom-call(s32[6]{0:T(128)} %stack.78.at_ref, bf16[8,256,640]{2,1,0:T(8,128)(2,1)} %norm_tiles.1.refs_0_.refs_1_.refs_2_.refs_3_.refs_4_.refs_5_, bf16[8,256,640]{2,1,0:T(8,128)(2,1)} %norm_tiles.1.refs_0_.refs_1_.refs_2_.refs_3_.refs_4_.refs_5_, ...), custom_call_target="tpu_custom_call" | custom-call | flops 6039797760 | bytes 20054016 | tf_op jit(solution)/shard_map/project/pallas_call | solution.py:186
  372.4 7.5 %project.7.refs_2_ = f32[3,1024,256]{2,1,0:T(8,128)} custom-call(s32[2]{0:T(128)} %pad_add_fusion.1.at_ref, bf16[8,256,640]{2,1,0:T(8,128)(2,1)} %norm_tiles.1.refs_0_.refs_1_.refs_2_.refs_3_.refs_4_.refs_5_, bf16[8,256,640]{2,1,0:T(8,128)(2,1)} %norm_tiles.1.refs_0_.refs_1_.refs_2_.refs_3_.refs_4_.refs_5_, ...), custom_call_target="tpu_custom_call", output_to_operand_aliasing={{}: (13, {})} | custom-call | flops 2013265920 | bytes 10878976 | tf_op jit(solution)/shard_map/project/pallas_call | solution.py:186
  380.4 10.5 %mix_values.1 = bf16[8,4,32,768]{3,2,1,0:T(8,128)(2,1)} custom-call(s32[4]{0:T(128)} %pad_add_fusion.order_ref, s32[16]{0:T(128)} %iota.27.place_ref, bf16[3,1024,1024]{2,1,0:T(8,128)(2,1)} %soft_weights.2.refs_0_, bf16[3,1024,1024]{2,1,0:T(8,128)(2,1)} %soft_weights.3.refs_1_, f32[3,1024,256]{2,1,0:T(8,128)} %project.7.refs_2_), custom_call_target="tpu_custom_call" | custom-call | flops 1610612736 | bytes 17301504 | tf_op jit(solution)/shard_map/mix_values/pallas_call | solution.py:298
  390.9 44.4 %all_to_all.5.in_ref = bf16[32,32,768]{2,1,0:T(8,128)(2,1)} all-to-all(bf16[32,32,768]{2,1,0:T(8,128)(2,1)} %bitcast.24), channel_id=1, replica_groups=mesh['bal'=8,'seq'=4] {'bal','seq'}, dimensions={0} | all-to-all | bytes 3145728 | tf_op jit(solution)/shard_map/all_to_all | solution.py:497
  435.4 2.7 place_tiles.1
  (125 shorter events, 37.6 us)
Async XLA Ops:
  3.0 86.8 %collective-permute-start.14 = (bf16[6,640,256]{2,1,0:T(8,128)(2,1)}, bf16[6,640,256]{2,1,0:T(8,128)(2,1)S(1)}, u32[]{:S(2)}, u32[]{:S(2)}) collective-permute-start(bf16[6,640,256]{2,1,0:T(8,128)(2,1)} %slice.38), channel_id=1, source_target_pairs={{0,0},{1,4},{2,2},{3,6},{4,1},{5,5},{6,3},{7,7},{8,8},{9,12},{10,1... | collective-permute-start | bytes 5898248 | tf_op jit(solution)/shard_map/ppermute | solution.py:364
  5.3 16.2 %collective-permute-start.1 = (f32[4,2,5120]{2,1,0:T(2,128)S(1)}, f32[4,2,5120]{2,1,0:T(2,128)S(1)}, u32[]{:S(2)}, u32[]{:S(2)}) collective-permute-start(f32[4,2,5120]{2,1,0:T(2,128)S(1)} %bitcast.30), channel_id=1, source_target_pairs={{0,0},{1,4},{2,2},{3,6},{4,1},{5,5},{6,3},{7,7},{8,8},{9,12},{10,1... | collective-permute-start | bytes 491528 | tf_op jit(solution)/shard_map/ppermute | solution.py:364
  10.2 31.8 %collective-permute-start.2 = (bf16[2,16,5120]{2,1,0:T(8,128)(2,1)}, bf16[2,16,5120]{2,1,0:T(8,128)(2,1)S(1)}, u32[]{:S(2)}, u32[]{:S(2)}) collective-permute-start(bf16[2,16,5120]{2,1,0:T(8,128)(2,1)} %get-tuple-element.25), channel_id=1, source_target_pairs={{0,0},{1,4},{2,2},{3,6},{4,1},{5,5},{6,3},{7,7},{8,8},{9,12},{10,1... | collective-permute-start | bytes 983048 | tf_op jit(solution)/shard_map/ppermute | solution.py:364
  12.5 31.2 %collective-permute-start.3 = (bf16[2,16,5120]{2,1,0:T(8,128)(2,1)}, bf16[2,16,5120]{2,1,0:T(8,128)(2,1)S(1)}, u32[]{:S(2)}, u32[]{:S(2)}) collective-permute-start(bf16[2,16,5120]{2,1,0:T(8,128)(2,1)} %get-tuple-element.26), channel_id=1, source_target_pairs={{0,1},{1,5},{2,3},{3,7},{4,8},{5,12},{6,10},{7,14},{8,9},{9,13},{1... | collective-permute-start | bytes 983048 | tf_op jit(solution)/shard_map/ppermute | solution.py:364
  19.9 24.7 %collective-permute-start.4 = (bf16[2,16,5120]{2,1,0:T(8,128)(2,1)}, bf16[2,16,5120]{2,1,0:T(8,128)(2,1)S(1)}, u32[]{:S(2)}, u32[]{:S(2)}) collective-permute-start(bf16[2,16,5120]{2,1,0:T(8,128)(2,1)} %get-tuple-element.27), channel_id=1, source_target_pairs={{0,8},{1,12},{2,10},{3,14},{4,9},{5,13},{6,11},{7,15},{8,16},{9,20... | collective-permute-start | bytes 983048 | tf_op jit(solution)/shard_map/ppermute | solution.py:364
  21.5 48.6 %collective-permute-start.5 = (bf16[2,16,5120]{2,1,0:T(8,128)(2,1)}, bf16[2,16,5120]{2,1,0:T(8,128)(2,1)S(1)}, u32[]{:S(2)}, u32[]{:S(2)}) collective-permute-start(bf16[2,16,5120]{2,1,0:T(8,128)(2,1)} %get-tuple-element.28), channel_id=1, source_target_pairs={{0,9},{1,13},{2,11},{3,15},{4,16},{5,20},{6,18},{7,22},{8,17},{9,2... | collective-permute-start | bytes 983048 | tf_op jit(solution)/shard_map/ppermute | solution.py:364
  42.0 34.0 %collective-permute-start.6 = (bf16[2,16,5120]{2,1,0:T(8,128)(2,1)}, bf16[2,16,5120]{2,1,0:T(8,128)(2,1)}, u32[]{:S(2)}, u32[]{:S(2)}) collective-permute-start(bf16[2,16,5120]{2,1,0:T(8,128)(2,1)} %get-tuple-element.29), channel_id=1, source_target_pairs={{0,16},{1,20},{2,18},{3,22},{4,17},{5,21},{6,19},{7,23},{8,24},{9,... | collective-permute-start | bytes 983048 | tf_op jit(solution)/shard_map/ppermute | solution.py:364
  43.7 32.2 %collective-permute-start.7 = (bf16[2,16,5120]{2,1,0:T(8,128)(2,1)}, bf16[2,16,5120]{2,1,0:T(8,128)(2,1)}, u32[]{:S(2)}, u32[]{:S(2)}) collective-permute-start(bf16[2,16,5120]{2,1,0:T(8,128)(2,1)} %get-tuple-element.30), channel_id=1, source_target_pairs={{0,17},{1,21},{2,19},{3,23},{4,24},{5,28},{6,26},{7,30},{8,25},{9,... | collective-permute-start | bytes 983048 | tf_op jit(solution)/shard_map/ppermute | solution.py:364
  44.6 31.3 %collective-permute-start.8 = (bf16[2,16,5120]{2,1,0:T(8,128)(2,1)}, bf16[2,16,5120]{2,1,0:T(8,128)(2,1)}, u32[]{:S(2)}, u32[]{:S(2)}) collective-permute-start(bf16[2,16,5120]{2,1,0:T(8,128)(2,1)} %get-tuple-element.31), channel_id=1, source_target_pairs={{0,24},{1,28},{2,26},{3,30},{4,25},{5,29},{6,27},{7,31},{8,0},{9,4... | collective-permute-start | bytes 983048 | tf_op jit(solution)/shard_map/ppermute | solution.py:364
  70.1 9.0 %collective-permute-start.9 = (bf16[2,16,5120]{2,1,0:T(8,128)(2,1)}, bf16[2,16,5120]{2,1,0:T(8,128)(2,1)}, u32[]{:S(2)}, u32[]{:S(2)}) collective-permute-start(bf16[2,16,5120]{2,1,0:T(8,128)(2,1)} %get-tuple-element.32), channel_id=1, source_target_pairs={{0,25},{1,29},{2,27},{3,31},{4,0},{5,4},{6,2},{7,6},{8,1},{9,5},{1... | collective-permute-start | bytes 983048 | tf_op jit(solution)/shard_map/ppermute | solution.py:364
  88.3 55.9 %collective-permute-start.11 = (bf16[8,256,640]{2,1,0:T(8,128)(2,1)}, bf16[8,256,640]{2,1,0:T(8,128)(2,1)S(1)}, u32[]{:S(2)}, u32[]{:S(2)}) collective-permute-start(bf16[8,256,640]{2,1,0:T(8,128)(2,1)} %norm_tiles.1.refs_0_.refs_1_.refs_2_.refs_3_.refs_4_.refs_5_), channel_id=1, source_target_pairs={{0,2},{1,3},{2,0},{3,1},{4,6},{5,7},{6,4},{7,5},{8,10},{9,11},{10,... | collective-permute-start | bytes 7864328 | tf_op jit(solution)/shard_map/ppermute | solution.py:364
  89.8 100.4 %collective-permute-start.10 = (bf16[8,256,640]{2,1,0:T(8,128)(2,1)}, bf16[8,256,640]{2,1,0:T(8,128)(2,1)S(1)}, u32[]{:S(2)}, u32[]{:S(2)}) collective-permute-start(bf16[8,256,640]{2,1,0:T(8,128)(2,1)} %norm_tiles.1.refs_0_.refs_1_.refs_2_.refs_3_.refs_4_.refs_5_), channel_id=1, source_target_pairs={{0,4},{1,5},{2,6},{3,7},{4,0},{5,1},{6,2},{7,3},{8,12},{9,13},{10,... | collective-permute-start | bytes 7864328 | tf_op jit(solution)/shard_map/ppermute | solution.py:364
  89.8 97.1 %collective-permute-start.18 = (bf16[6,640,256]{2,1,0:T(8,128)(2,1)S(1)}, bf16[6,640,256]{2,1,0:T(8,128)(2,1)}, u32[]{:S(2)}, u32[]{:S(2)}) collective-permute-start(bf16[6,640,256]{2,1,0:T(8,128)(2,1)S(1)} %collective-permute-done.14.refs_30_), channel_id=1, source_target_pairs={{0,8},{1,9},{2,10},{3,11},{4,12},{5,13},{6,14},{7,15},{8,0},{9,1},... | collective-permute-start | bytes 5898248 | tf_op jit(solution)/shard_map/ppermute | solution.py:364
  104.4 85.7 %collective-permute-start.15 = (bf16[6,640,256]{2,1,0:T(8,128)(2,1)S(1)}, bf16[6,640,256]{2,1,0:T(8,128)(2,1)}, u32[]{:S(2)}, u32[]{:S(2)}) collective-permute-start(bf16[6,640,256]{2,1,0:T(8,128)(2,1)S(1)} %collective-permute-done.14.refs_30_), channel_id=1, source_target_pairs={{0,16},{1,17},{2,18},{3,19},{4,20},{5,21},{6,22},{7,23},{8,24},{9,... | collective-permute-start | bytes 5898248 | tf_op jit(solution)/shard_map/ppermute | solution.py:364
  107.8 84.3 %collective-permute-start.17 = (bf16[6,640,256]{2,1,0:T(8,128)(2,1)S(1)}, bf16[6,640,256]{2,1,0:T(8,128)(2,1)S(1)}, u32[]{:S(2)}, u32[]{:S(2)}) collective-permute-start(bf16[6,640,256]{2,1,0:T(8,128)(2,1)S(1)} %collective-permute-done.14.refs_30_), channel_id=1, source_target_pairs={{0,1},{1,0},{2,3},{3,2},{4,5},{5,4},{6,7},{7,6},{8,9},{9,8},{10,11... | collective-permute-start | bytes 5898248 | tf_op jit(solution)/shard_map/ppermute | solution.py:364
  144.3 51.0 %collective-permute-start.12 = (bf16[8,128,640]{2,1,0:T(8,128)(2,1)S(1)}, bf16[8,128,640]{2,1,0:T(8,128)(2,1)}, u32[]{:S(2)}, u32[]{:S(2)}) collective-permute-start(bf16[8,128,640]{2,1,0:T(8,128)(2,1)S(1)} %slice.36), channel_id=1, source_target_pairs={{0,4},{1,5},{2,6},{3,7},{4,0},{5,1},{6,2},{7,3},{8,12},{9,13},{10,... | collective-permute-start | bytes 3932168 | tf_op jit(solution)/shard_map/ppermute | solution.py:364
  186.9 44.9 %collective-permute-start.19 = (bf16[6,640,256]{2,1,0:T(8,128)(2,1)}, bf16[6,640,256]{2,1,0:T(8,128)(2,1)}, u32[]{:S(2)}, u32[]{:S(2)}) collective-permute-start(bf16[6,640,256]{2,1,0:T(8,128)(2,1)} %collective-permute-done.18.refs_32_), channel_id=1, source_target_pairs={{0,1},{1,0},{2,3},{3,2},{4,5},{5,4},{6,7},{7,6},{8,9},{9,8},{10,11... | collective-permute-start | bytes 5898248 | tf_op jit(solution)/shard_map/ppermute | solution.py:364
  190.2 41.7 %collective-permute-start.20 = (bf16[6,640,256]{2,1,0:T(8,128)(2,1)}, bf16[6,640,256]{2,1,0:T(8,128)(2,1)}, u32[]{:S(2)}, u32[]{:S(2)}) collective-permute-start(bf16[6,640,256]{2,1,0:T(8,128)(2,1)} %collective-permute-done.15.refs_34_), channel_id=1, source_target_pairs={{0,1},{1,0},{2,3},{3,2},{4,5},{5,4},{6,7},{7,6},{8,9},{9,8},{10,11... | collective-permute-start | bytes 5898248 | tf_op jit(solution)/shard_map/ppermute | solution.py:364
  191.5 31.5 %collective-permute-start.13 = (bf16[8,128,640]{2,1,0:T(8,128)(2,1)}, bf16[8,128,640]{2,1,0:T(8,128)(2,1)}, u32[]{:S(2)}, u32[]{:S(2)}) collective-permute-start(bf16[8,128,640]{2,1,0:T(8,128)(2,1)} %slice.37), channel_id=1, source_target_pairs={{0,2},{1,3},{2,0},{3,1},{4,6},{5,7},{6,4},{7,5},{8,10},{9,11},{10,... | collective-permute-start | bytes 3932168 | tf_op jit(solution)/shard_map/ppermute | solution.py:364
  193.4 58.9 %collective-permute-start.16 = (bf16[6,640,256]{2,1,0:T(8,128)(2,1)S(1)}, bf16[6,640,256]{2,1,0:T(8,128)(2,1)}, u32[]{:S(2)}, u32[]{:S(2)}) collective-permute-start(bf16[6,640,256]{2,1,0:T(8,128)(2,1)S(1)} %collective-permute-done.14.refs_30_), channel_id=1, source_target_pairs={{8,16},{9,17},{10,18},{11,19},{12,20},{13,21},{14,22},{15,23},{16,... | collective-permute-start | bytes 5898248 | tf_op jit(solution)/shard_map/ppermute | solution.py:455
  195.3 57.0 %collective-permute-start.21 = (bf16[6,640,256]{2,1,0:T(8,128)(2,1)}, bf16[6,640,256]{2,1,0:T(8,128)(2,1)}, u32[]{:S(2)}, u32[]{:S(2)}) collective-permute-start(bf16[6,640,256]{2,1,0:T(8,128)(2,1)} %collective-permute-done.15.refs_34_), channel_id=1, source_target_pairs={{8,0},{9,1},{10,2},{11,3},{12,4},{13,5},{14,6},{15,7},{16,24},{17,... | collective-permute-start | bytes 5898248 | tf_op jit(solution)/shard_map/ppermute | solution.py:455
  222.9 32.1 %collective-permute-start.28 = (bf16[3,640,256]{2,1,0:T(8,128)(2,1)}, bf16[3,640,256]{2,1,0:T(8,128)(2,1)}, u32[]{:S(2)}, u32[]{:S(2)}) collective-permute-start(bf16[3,640,256]{2,1,0:T(8,128)(2,1)} %pad_maximum_fusion), channel_id=1, source_target_pairs={{0,0},{1,4},{2,2},{3,6},{4,1},{5,5},{6,3},{7,7},{8,8},{9,12},{10,1... | collective-permute-start | bytes 2949128 | tf_op jit(solution)/shard_map/ppermute | solution.py:364
  255.0 47.1 %collective-permute-start.22 = (bf16[6,640,256]{2,1,0:T(8,128)(2,1)S(1)}, bf16[6,640,256]{2,1,0:T(8,128)(2,1)}, u32[]{:S(2)}, u32[]{:S(2)}) collective-permute-start(bf16[6,640,256]{2,1,0:T(8,128)(2,1)S(1)} %add.125.refs_10_), channel_id=1, source_target_pairs={{0,1},{1,0},{2,3},{3,2},{4,5},{5,4},{6,7},{7,6},{8,9},{9,8},{10,11... | collective-permute-start | bytes 5898248 | tf_op jit(solution)/shard_map/ppermute | solution.py:364
  255.1 46.5 %collective-permute-start.29 = (bf16[3,640,256]{2,1,0:T(8,128)(2,1)}, bf16[3,640,256]{2,1,0:T(8,128)(2,1)}, u32[]{:S(2)}, u32[]{:S(2)}) collective-permute-start(bf16[3,640,256]{2,1,0:T(8,128)(2,1)} %collective-permute-done.28.refs_30_), channel_id=1, source_target_pairs={{0,16},{1,17},{2,18},{3,19},{4,20},{5,21},{6,22},{7,23},{8,24},{9,... | collective-permute-start | bytes 2949128 | tf_op jit(solution)/shard_map/ppermute | solution.py:364
  257.6 44.1 %collective-permute-start.32 = (bf16[3,640,256]{2,1,0:T(8,128)(2,1)}, bf16[3,640,256]{2,1,0:T(8,128)(2,1)}, u32[]{:S(2)}, u32[]{:S(2)}) collective-permute-start(bf16[3,640,256]{2,1,0:T(8,128)(2,1)} %collective-permute-done.28.refs_30_), channel_id=1, source_target_pairs={{0,8},{1,9},{2,10},{3,11},{4,12},{5,13},{6,14},{7,15},{8,0},{9,1},... | collective-permute-start | bytes 2949128 | tf_op jit(solution)/shard_map/ppermute | solution.py:364
  263.0 51.9 %collective-permute-start.26 = (f32[6,128]{1,0:T(8,128)S(1)}, f32[6,128]{1,0:T(8,128)S(1)}, u32[]{:S(2)}, u32[]{:S(2)}) collective-permute-start(f32[6,128]{1,0:T(8,128)S(1)} %copy-done.19), channel_id=1, source_target_pairs={{0,0},{1,4},{2,2},{3,6},{4,1},{5,5},{6,3},{7,7},{8,8},{9,12},{10,1... | collective-permute-start | bytes 9224 | tf_op jit(solution)/shard_map/ppermute | solution.py:364
  263.7 55.1 %collective-permute-start.27 = (f32[6,128]{1,0:T(8,128)S(1)}, f32[6,128]{1,0:T(8,128)S(1)}, u32[]{:S(2)}, u32[]{:S(2)}) collective-permute-start(f32[6,128]{1,0:T(8,128)S(1)} %copy-done.20), channel_id=1, source_target_pairs={{0,0},{1,4},{2,2},{3,6},{4,1},{5,5},{6,3},{7,7},{8,8},{9,12},{10,1... | collective-permute-start | bytes 9224 | tf_op jit(solution)/shard_map/ppermute | solution.py:364
  301.6 54.0 %collective-permute-start.31 = (bf16[3,640,256]{2,1,0:T(8,128)(2,1)}, bf16[3,640,256]{2,1,0:T(8,128)(2,1)}, u32[]{:S(2)}, u32[]{:S(2)}) collective-permute-start(bf16[3,640,256]{2,1,0:T(8,128)(2,1)} %collective-permute-done.28.refs_30_), channel_id=1, source_target_pairs={{0,1},{1,0},{2,3},{3,2},{4,5},{5,4},{6,7},{7,6},{8,9},{9,8},{10,11... | collective-permute-start | bytes 2949128 | tf_op jit(solution)/shard_map/ppermute | solution.py:364
  301.7 53.9 %collective-permute-start.33 = (bf16[3,640,256]{2,1,0:T(8,128)(2,1)}, bf16[3,640,256]{2,1,0:T(8,128)(2,1)}, u32[]{:S(2)}, u32[]{:S(2)}) collective-permute-start(bf16[3,640,256]{2,1,0:T(8,128)(2,1)} %collective-permute-done.32.refs_32_), channel_id=1, source_target_pairs={{0,1},{1,0},{2,3},{3,2},{4,5},{5,4},{6,7},{7,6},{8,9},{9,8},{10,11... | collective-permute-start | bytes 2949128 | tf_op jit(solution)/shard_map/ppermute | solution.py:364
  302.1 53.5 %collective-permute-start.34 = (bf16[3,640,256]{2,1,0:T(8,128)(2,1)}, bf16[3,640,256]{2,1,0:T(8,128)(2,1)}, u32[]{:S(2)}, u32[]{:S(2)}) collective-permute-start(bf16[3,640,256]{2,1,0:T(8,128)(2,1)} %collective-permute-done.29.refs_34_), channel_id=1, source_target_pairs={{0,1},{1,0},{2,3},{3,2},{4,5},{5,4},{6,7},{7,6},{8,9},{9,8},{10,11... | collective-permute-start | bytes 2949128 | tf_op jit(solution)/shard_map/ppermute | solution.py:364
  339.8 28.7 %collective-permute-start.30 = (bf16[3,640,256]{2,1,0:T(8,128)(2,1)}, bf16[3,640,256]{2,1,0:T(8,128)(2,1)S(1)}, u32[]{:S(2)}, u32[]{:S(2)}) collective-permute-start(bf16[3,640,256]{2,1,0:T(8,128)(2,1)} %collective-permute-done.28.refs_30_), channel_id=1, source_target_pairs={{8,16},{9,17},{10,18},{11,19},{12,20},{13,21},{14,22},{15,23},{16,... | collective-permute-start | bytes 2949128 | tf_op jit(solution)/shard_map/ppermute | solution.py:455
  340.6 28.0 %collective-permute-start.35 = (bf16[3,640,256]{2,1,0:T(8,128)(2,1)}, bf16[3,640,256]{2,1,0:T(8,128)(2,1)S(1)}, u32[]{:S(2)}, u32[]{:S(2)}) collective-permute-start(bf16[3,640,256]{2,1,0:T(8,128)(2,1)} %collective-permute-done.29.refs_34_), channel_id=1, source_target_pairs={{8,0},{9,1},{10,2},{11,3},{12,4},{13,5},{14,6},{15,7},{16,24},{17,... | collective-permute-start | bytes 2949128 | tf_op jit(solution)/shard_map/ppermute | solution.py:455
  (26 other events, 504.3 us)

commit v2 on v1

--- a/solution.py
+++ b/solution.py
@@ -10,7 +10,8 @@
 AXES = ("bal", "seq")
 
 eps_norm = 1e-06
-score_fill = -1e30
+log2_e = 1.4426950408889634
+mask_bias = -3e38
 
 
 def tile_layout(clip_shape):
@@ -199,20 +200,22 @@
     )(at, *args)
 
 
-def soft_weights(qk, partial_sums, gains, mask, features, first, count):
+def soft_weights(qk, partial_sums, gains, bias, features, first, count):
     heads, total, cols = qk.shape
     dim = cols // 2
-    rows = mask.shape[0]
     n = len(partial_sums)
+    rows = total // n
+    extra = bias.shape[1]
 
     def body(*refs):
         q_ref, k_ref = refs[0], refs[1]
         sum_refs = refs[2 : 2 + n]
-        qg_ref, kg_ref, mask_ref, out_ref, scales, keys = refs[2 + n :]
+        qg_ref, kg_ref, bias_ref, out_ref, scales, keys = refs[2 + n :]
         head, block = pl.program_id(0), pl.program_id(1)
 
         @pl.when((head == 0) & (block == 0))
         def _():
+            keys[:, dim:] = bias_ref[...]
             for p in range(n):
                 whole = None
                 for q in range(n):
@@ -223,19 +226,21 @@
 
         @pl.when(block == 0)
         def _():
-            keys[...] = (k_ref[0] * scales[:, 1:2] * kg_ref[pl.ds(first + head, 1), :]).astype(keys.dtype)
+            keys[:, :dim] = (k_ref[0] * scales[:, 1:2] * kg_ref[pl.ds(first + head, 1), :]).astype(keys.dtype)
 
         at = pl.multiple_of(block * rows, rows)
         query = q_ref[0] * scales[pl.ds(at, rows), 0:1] * qg_ref[pl.ds(first + head, 1), :]
+        lane = lax.broadcasted_iota(jnp.int32, (rows, extra), 1)
+        row = lax.broadcasted_iota(jnp.int32, (rows, extra), 0)
+        tile = (row // (rows // TILES_OWN) == lane).astype(keys.dtype)
         scores = lax.dot_general(
-            query.astype(keys.dtype),
+            jnp.concatenate([query.astype(keys.dtype), tile], axis=1),
             keys[...],
             (((1,), (1,)), ((), ())),
             preferred_element_type=jnp.float32,
-        ) * dim ** (-0.5)
-        scores = jnp.where(mask_ref[...] > 0.5, scores, score_fill)
+        )
         largest = jnp.max(scores, axis=-1, keepdims=True)
-        powers = jnp.exp(scores - largest)
+        powers = jnp.exp2((scores - largest) * (dim ** (-0.5) * log2_e))
         share = 1.0 / jnp.sum(powers, axis=-1, keepdims=True)
         out_ref[0] = (powers * share).astype(out_ref.dtype)
 
@@ -250,74 +255,85 @@
             pl.BlockSpec((1, total, dim), lambda h, b: (first + h, 0, 1)),
         ]
         + [whole_sum] * n
-        + [gain, gain, pl.BlockSpec(mask.shape, lambda h, b: (0, 0))],
+        + [gain, gain, pl.BlockSpec(bias.shape, lambda h, b: (0, 0))],
         out_specs=pl.BlockSpec((1, rows, total), lambda h, b: (h, b, 0)),
-        scratch_shapes=[pltpu.VMEM((total, 8), jnp.float32), pltpu.VMEM((total, dim), jnp.bfloat16)],
+        scratch_shapes=[pltpu.VMEM((total, 8), jnp.float32), pltpu.VMEM((total, dim + extra), jnp.bfloat16)],
         cost_estimate=pl.CostEstimate(
             flops=(2 * dim + 8) * count * total * total,
             bytes_accessed=count * total * (2 * total + 4 * cols),
             transcendentals=count * total * total,
         ),
         name="soft_weights",
-    )(qk, qk, *partial_sums, *gains, mask)
-
-
-def mix_values(weights, values, order, place, groups, capacity, piece):
+    )(qk, qk, *partial_sums, *gains, bias)
+
+
+def mix_values(weights, values, xs, blocks, at, order, place, groups, capacity, piece):
     parts, (count, total, _) = len(weights), weights[0].shape
     heads = parts * count
     packed, _, cols = values.shape
+    depth = blocks[0].shape[1]
     dim = packed * cols // heads
     share = heads // packed
     n = order.shape[0]
     rows = total // n
+    sizes = [x.shape[1] for x in xs]
+    m, k = len(xs), len(blocks)
     full = groups * capacity == TILES_OWN
 
-    def body(order_ref, place_ref, *refs):
-        w_refs, (v_ref, out_ref, *staged) = refs[:parts], refs[parts:]
+    def body(order_ref, place_ref, at_ref, *refs):
+        weight_refs, x_refs, refs = refs[:parts], refs[parts : parts + m * k], refs[parts + m * k :]
+        w_refs, (acc_ref, out_ref, held, *staged) = refs[:k], refs[k:]
+        head = pl.program_id(0)
+
+        @pl.when(head % share == 0)
+        def _():
+            left = [jnp.concatenate([x_refs[i * k + j][0] for j in range(k)], axis=1) for i in range(m)]
+            right = jnp.concatenate([ref[0] for ref in w_refs], axis=0)
+            done = acc_ref[0] + jnp.dot(jnp.concatenate(left, axis=0), right, preferred_element_type=jnp.float32)
+            for i in range(share):
+                held[i] = done[:, i * dim : (i + 1) * dim].astype(held.dtype)
+
         for i in range(parts):
 
-            @pl.when(pl.program_id(0) // count == i)
-            def _(w_ref=w_refs[i]):
-                one_head(order_ref, place_ref, w_ref, v_ref, out_ref, staged)
-
-    def one_head(order_ref, place_ref, w_ref, v_ref, out_ref, staged):
-        held = v_ref[0].astype(w_ref.dtype)
-        mixed = jnp.dot(w_ref[0], held, preferred_element_type=jnp.float32)
-        for p in range(n):
-            block = mixed[p * rows : (p + 1) * rows]
-            if full:
-                out_ref[:, order_ref[p]] = block.astype(out_ref.dtype).reshape(groups, capacity * piece, dim)
-                continue
-            staged[0][...] = block
-            for slot in range(groups * capacity):
-                tile = jnp.minimum(place_ref[slot], TILES_OWN - 1)
-                tile_rows = staged[0][pl.ds(pl.multiple_of(tile * piece, piece), piece), :]
-                at = slot % capacity * piece
-                out_ref[slot // capacity, order_ref[p], at : at + piece] = tile_rows.astype(out_ref.dtype)
+            @pl.when(head // count == i)
+            def _(weight_ref=weight_refs[i]):
+                mixed = jnp.dot(weight_ref[0], held[head % share], preferred_element_type=jnp.float32)
+                for p in range(n):
+                    block = mixed[p * rows : (p + 1) * rows]
+                    if full:
+                        out_ref[:, order_ref[p]] = block.astype(out_ref.dtype).reshape(groups, capacity * piece, dim)
+                        continue
+                    staged[0][...] = block
+                    for slot in range(groups * capacity):
+                        tile = jnp.minimum(place_ref[slot], TILES_OWN - 1)
+                        tile_rows = staged[0][pl.ds(pl.multiple_of(tile * piece, piece), piece), :]
+                        to = slot % capacity * piece
+                        out_ref[slot // capacity, order_ref[p], to : to + piece] = tile_rows.astype(out_ref.dtype)
+
+    def weight_block(i):
+        return pl.BlockSpec((1, total, total), lambda h, o, s, a: (jnp.clip(h - i * count, 0, count - 1), 0, 0))
 
     return pl.pallas_call(
         body,
         out_shape=jax.ShapeDtypeStruct((groups, n, capacity * piece, heads * dim), jnp.bfloat16),
         grid_spec=pltpu.PrefetchScalarGridSpec(
-            num_scalar_prefetch=2,
+            num_scalar_prefetch=3,
             grid=(heads,),
-            in_specs=[
-                pl.BlockSpec((1, total, total), lambda h, o, s, i=i: (jnp.clip(h - i * count, 0, count - 1), 0, 0))
-                for i in range(parts)
-            ]
-            + [
-                pl.BlockSpec((1, total, dim), lambda h, o, s: (h // share, 0, h % share)),
-            ],
-            out_specs=pl.BlockSpec((groups, n, capacity * piece, dim), lambda h, o, s: (0, 0, 0, h)),
-            scratch_shapes=[pltpu.VMEM((rows, dim), jnp.float32)] * (not full),
+            in_specs=[weight_block(i) for i in range(parts)]
+            + [pl.BlockSpec((1, size, depth), lambda h, o, s, a, j=j: (a[j], 0, 0)) for size in sizes for j in range(k)]
+            + [pl.BlockSpec((1, depth, cols), lambda h, o, s, a: (h // share, 0, 0))] * k
+            + [pl.BlockSpec((1, total, cols), lambda h, o, s, a: (h // share, 0, 0))],
+            out_specs=pl.BlockSpec((groups, n, capacity * piece, dim), lambda h, o, s, a: (0, 0, 0, h)),
+            scratch_shapes=[pltpu.VMEM((share, total, dim), jnp.bfloat16)]
+            + [pltpu.VMEM((rows, dim), jnp.float32)] * (not full),
         ),
         cost_estimate=pl.CostEstimate(
-            flops=2 * heads * total * total * dim,
+            flops=2 * heads * total * (total + k * depth) * dim,
             bytes_accessed=heads * total * (2 * total + 6 * dim),
             transcendentals=0,
         ),
         name="mix_values",
-    )(order, place, *weights, values)
+    )(order, place, at, *weights, *[x for x in xs for _ in range(k)], *blocks, values)
 
 
 def place_tiles(returned, tile_owner, groups, n, capacity):
@@ -468,23 +484,24 @@
     qk_own = start_planes(after(qk_own[0], outgoing[0]), *arrived)
     v_first = swap(after(v_columns, outgoing[0]))
     qk_ends = end_planes(qk_own)
-    v_own = start_planes(after(v_first, *pieces[-2:]))
-
     blocks, at = blocks_of(qk_own, early)
     qk, *_ = project(pieces, blocks, at, None, False)
+    v_own = start_planes(after(v_first, *pieces[-2:]), *qk_ends)
     qk_own.append(last_plane(qk_ends, qk))
-    qk, sums = project(pieces, *blocks_of(qk_own, late), qk, True)
+    blocks, at = blocks_of(qk_own, late)
+    qk, sums = project(pieces, blocks, at, qk, True)
     partial_sums = [sums, along_x(sums)]
     for py in range(1, lines):
         partial_sums.append(along_y(sums, py))
         partial_sums.append(send(sums, lambda z, x, y, c: (z, x ^ 1, (y - py) % lines, c)))
 
-    spread = jnp.repeat(jnp.repeat(tile_mask.astype(jnp.float32), piece, axis=0), piece, axis=1)
-    mask = jnp.tile(spread, (1, n))
+    bias = jnp.where(tile_mask.T, 0.0, mask_bias).astype(jnp.bfloat16)
+    bias = jnp.pad(bias, ((0, 0), (0, dim - TILES_OWN)))
+    bias = jnp.tile(jnp.repeat(bias, piece, axis=0), (n, 1))
     parts = 2 if heads % 2 == 0 else 1
     weights = []
     for i in range(parts):
-        part = soft_weights(qk, partial_sums, gains, mask, features, i * heads // parts, heads // parts)
+        part = soft_weights(qk, partial_sums, gains, bias, features, i * heads // parts, heads // parts)
         weights.append(part)
         if i == 0:
             v_ends = end_planes(v_own, weights[0])
@@ -492,8 +509,8 @@
     blocks[0] = after(blocks[0], weights[-1])
     values, *_ = project(pieces, blocks, at, None, False)
     v_own.append(last_plane(v_ends, values))
-    values, *_ = project(pieces, *blocks_of(v_own, late), values, False)
-    mixed = mix_values(weights, values, order, place, groups, capacity, piece)
+    blocks, at = blocks_of(v_own, late)
+    mixed = mix_values(weights, values, pieces, blocks, at, order, place, groups, capacity, piece)
     returned = lax.all_to_all(
         mixed.reshape(groups * n, capacity * piece, heads * dim), AXES, split_axis=0, concat_axis=0, tiled=True
     )

time: 440 us -> 436 us (level)
  waiting for transfers between devices: 173 us -> 184 us
  starting transfers between devices: 94.6 us -> 89.2 us
    ppermute x33, waiting for transfers between devices: 173 us -> 184 us  [send(): return lax.ppermute(value, AXES, pairs)]
    pallas_call x4 -> x3, Pallas kernels: 53.5 us -> 46 us  [project(): pl.pallas_call(body, out_shape=out_shape, grid_spec=pltpu.PrefetchScalarG...]
    ppermute x33, starting transfers between devices: 89.2 us -> 83.8 us  [send(): return lax.ppermute(value, AXES, pairs)]
    pallas_call x1, Pallas kernels: 10.5 us -> 15 us  [mix_values(): pl.pallas_call(body, out_shape=jax.ShapeDtypeStruct((groups, n, capacity...]
  transfers between devices with their start and end apart: 37 -> 37, of which waited for: 11 -> 12; matrix products, arithmetic and copies ran while one was open for 3% -> 3% of each run, Pallas kernels for 19% -> 19%
where the time goes in v2:
time: 436 us; the launch traced here: 435 us
  waiting for transfers between devices  184 us (42%)
  Pallas kernels  102 us (23%)
  starting transfers between devices  89.2 us (20%)
  blocking collectives  42.1 us (10%)
  local copies, waits for them, and re-layouts  10.2 us (2%)
  other arithmetic  7.25 us (2%)
    ppermute x33, waiting for transfers between devices, send(): return lax.ppermute(value, AXES, pairs)  184 us
    ppermute x33, starting transfers between devices, send(): return lax.ppermute(value, AXES, pairs)  83.8 us
    pallas_call x3, Pallas kernels, project(): pl.pallas_call(body, out_shape=out_shape, grid_spec=pltpu.PrefetchScalarG...  46 us
    all_to_all x1, blocking collectives, transposed(): lax.all_to_all(mixed.reshape(groups * n, capacity * piece, heads * dim),...  42.1 us
    pallas_call x2, Pallas kernels, soft_weights(): pl.pallas_call(body, out_shape=jax.ShapeDtypeStruct((count, total, total)...  26.2 us
    pallas_call x1, Pallas kernels, mix_values(): pl.pallas_call(body, out_shape=jax.ShapeDtypeStruct((groups, n, capacity...  15 us
  transfers between devices with their start and end apart: 37, of which 12 were waited for; matrix products, arithmetic and copies ran while one was open for 3% of the time, Pallas kernels for 19%

profile of v2, /device:TPU:0, one launch (start us, length us, event | category | flops | bytes accessed | tf_op | source)
XLA Modules:
  0.0 434.7 jit_solution(6284295031312742836)
XLA Ops:
  0.0 3.0 slice.38
  3.0 2.3 collective-permute-start.14
  6.7 3.5 pick_tiles.1
  12.5 7.4 %collective-permute-start.3 = (bf16[2,16,5120]{2,1,0:T(8,128)(2,1)}, bf16[2,16,5120]{2,1,0:T(8,128)(2,1)S(1)}, u32[]{:S(2)}, u32[]{:S(2)}) collective-permute-start(bf16[2,16,5120]{2,1,0:T(8,128)(2,1)} %get-tuple-element.27), channel_id=1, source_target_pairs={{0,1},{1,5},{2,3},{3,7},{4,8},{5,12},{6,10},{7,14},{8,9},{9,13},{1... | collective-permute-start | bytes 983048 | tf_op jit(solution)/shard_map/ppermute | solution.py:380
  21.5 20.0 %collective-permute-start.5 = (bf16[2,16,5120]{2,1,0:T(8,128)(2,1)}, bf16[2,16,5120]{2,1,0:T(8,128)(2,1)S(1)}, u32[]{:S(2)}, u32[]{:S(2)}) collective-permute-start(bf16[2,16,5120]{2,1,0:T(8,128)(2,1)} %get-tuple-element.29), channel_id=1, source_target_pairs={{0,9},{1,13},{2,11},{3,15},{4,16},{5,20},{6,18},{7,22},{8,17},{9,2... | collective-permute-start | bytes 983048 | tf_op jit(solution)/shard_map/ppermute | solution.py:380
  44.6 2.2 collective-permute-start.8
  46.9 23.2 %collective-permute-done.5.rest_3_ = bf16[2,16,5120]{2,1,0:T(8,128)(2,1)S(1)} collective-permute-done((bf16[2,16,5120]{2,1,0:T(8,128)(2,1)}, bf16[2,16,5120]{2,1,0:T(8,128)(2,1)S(1)}, u32[]{:S(2)}, u32[]{:S(2)}) %collective-permute-start.5) | collective-permute-done | bytes 327712 | tf_op jit(solution)/shard_map/ppermute | solution.py:380
  70.7 5.2 %collective-permute-done.6.rest_4_ = bf16[2,16,5120]{2,1,0:T(8,128)(2,1)} collective-permute-done((bf16[2,16,5120]{2,1,0:T(8,128)(2,1)}, bf16[2,16,5120]{2,1,0:T(8,128)(2,1)}, u32[]{:S(2)}, u32[]{:S(2)}) %collective-permute-start.6) | collective-permute-done | bytes 327712 | tf_op jit(solution)/shard_map/ppermute | solution.py:380
  75.9 3.2 collective-permute-done.9.rest_7_
  79.7 8.5 %norm_tiles.1.refs_0_.refs_1_.refs_2_.refs_3_.refs_4_.refs_5_ = bf16[8,256,640]{2,1,0:T(8,128)(2,1)} custom-call(s32[16]{0:T(128)} %broadcast_maximum_fusion.1.member_ref, s32[16]{0:T(128)} %iota.28.place_ref, s32[2]{0:T(128)} %pad_add_fusion.2.ids_ref, f32[4,2,5120]{2,1,0:T(2,128)} %copy-done.11, bf16[2,16,5120]{2,1,0:T(8,128)(2,1)} %copy-done.7, ...), custom_call_target="tpu_custom_call" | custom-call | flops 15728640 | bytes 5242880 | tf_op jit(solution)/shard_map/norm_tiles/pallas_call | solution.py:117
  89.8 14.6 %collective-permute-start.18 = (bf16[6,640,256]{2,1,0:T(8,128)(2,1)S(1)}, bf16[6,640,256]{2,1,0:T(8,128)(2,1)}, u32[]{:S(2)}, u32[]{:S(2)}) collective-permute-start(bf16[6,640,256]{2,1,0:T(8,128)(2,1)S(1)} %collective-permute-done.14.refs_30_), channel_id=1, source_target_pairs={{0,8},{1,9},{2,10},{3,11},{4,12},{5,13},{6,14},{7,15},{8,0},{9,1},... | collective-permute-start | bytes 5898248 | tf_op jit(solution)/shard_map/ppermute | solution.py:380
  104.4 3.3 collective-permute-start.15
  109.5 34.6 %collective-permute-done.11.refs_12_.refs_13_.refs_14_.refs_15_.refs_16_.refs_17_.refs_4_.refs_5_.refs_6_.refs_7_ = bf16[8,256,640]{2,1,0:T(8,128)(2,1)S(1)} collective-permute-done((bf16[8,256,640]{2,1,0:T(8,128)(2,1)}, bf16[8,256,640]{2,1,0:T(8,128)(2,1)S(1)}, u32[]{:S(2)}, u32[]{:S(2)}) %collective-permute-start.11) | collective-permute-done | bytes 2621472 | tf_op jit(solution)/shard_map/ppermute | solution.py:380
  144.4 42.5 %collective-permute-done.18.refs_32_ = bf16[6,640,256]{2,1,0:T(8,128)(2,1)} collective-permute-done((bf16[6,640,256]{2,1,0:T(8,128)(2,1)S(1)}, bf16[6,640,256]{2,1,0:T(8,128)(2,1)}, u32[]{:S(2)}, u32[]{:S(2)}) %collective-permute-start.18) | collective-permute-done | bytes 1966112 | tf_op jit(solution)/shard_map/ppermute | solution.py:380
  186.9 3.3 collective-permute-start.19
  199.7 23.3 %collective-permute-done.13.refs_24_.refs_25_.refs_26_.refs_27_.refs_28_.refs_29_.refs_8_.refs_9_.refs_10_.refs_11_ = bf16[8,128,640]{2,1,0:T(8,128)(2,1)} collective-permute-done((bf16[8,128,640]{2,1,0:T(8,128)(2,1)}, bf16[8,128,640]{2,1,0:T(8,128)(2,1)}, u32[]{:S(2)}, u32[]{:S(2)}) %collective-permute-start.13) | collective-permute-done | bytes 1310752 | tf_op jit(solution)/shard_map/ppermute | solution.py:380
  222.9 8.9 %collective-permute-start.28 = (bf16[3,640,256]{2,1,0:T(8,128)(2,1)}, bf16[3,640,256]{2,1,0:T(8,128)(2,1)}, u32[]{:S(2)}, u32[]{:S(2)}) collective-permute-start(bf16[3,640,256]{2,1,0:T(8,128)(2,1)} %pad_maximum_fusion), channel_id=1, source_target_pairs={{0,0},{1,4},{2,2},{3,6},{4,1},{5,5},{6,3},{7,7},{8,8},{9,12},{10,1... | collective-permute-start | bytes 2949128 | tf_op jit(solution)/shard_map/ppermute | solution.py:380
  231.8 20.5 %project.3.refs_12_ = f32[6,1024,256]{2,1,0:T(8,128)} custom-call(s32[6]{0:T(128)} %stack.78.at_ref, bf16[8,256,640]{2,1,0:T(8,128)(2,1)} %norm_tiles.1.refs_0_.refs_1_.refs_2_.refs_3_.refs_4_.refs_5_, bf16[8,256,640]{2,1,0:T(8,128)(2,1)} %norm_tiles.1.refs_0_.refs_1_.refs_2_.refs_3_.refs_4_.refs_5_, ...), custom_call_target="tpu_custom_call" | custom-call | flops 12079595520 | bytes 32243712 | tf_op jit(solution)/shard_map/project/pallas_call | solution.py:187
  252.3 2.6 add.127.refs_10_
  255.1 4.8 %collective-permute-start.32 = (bf16[3,640,256]{2,1,0:T(8,128)(2,1)}, bf16[3,640,256]{2,1,0:T(8,128)(2,1)}, u32[]{:S(2)}, u32[]{:S(2)}) collective-permute-start(bf16[3,640,256]{2,1,0:T(8,128)(2,1)} %collective-permute-done.28.refs_30_), channel_id=1, source_target_pairs={{0,8},{1,9},{2,10},{3,11},{4,12},{5,13},{6,14},{7,15},{8,0},{9,1},... | collective-permute-start | bytes 2949128 | tf_op jit(solution)/shard_map/ppermute | solution.py:380
  259.9 3.2 collective-permute-start.29
  265.1 38.2 %collective-permute-done.32.refs_32_ = bf16[3,640,256]{2,1,0:T(8,128)(2,1)} collective-permute-done((bf16[3,640,256]{2,1,0:T(8,128)(2,1)}, bf16[3,640,256]{2,1,0:T(8,128)(2,1)}, u32[]{:S(2)}, u32[]{:S(2)}) %collective-permute-start.32) | collective-permute-done | bytes 983072 | tf_op jit(solution)/shard_map/ppermute | solution.py:380
  303.3 3.2 collective-permute-done.29.refs_34_
  307.1 12.7 %project.4 = (f32[6,1024,256]{2,1,0:T(8,128)}, f32[8,1024]{1,0:T(8,128)}) custom-call(s32[2]{0:T(128)} %pad_add_fusion.1.at_ref, bf16[8,256,640]{2,1,0:T(8,128)(2,1)} %norm_tiles.1.refs_0_.refs_1_.refs_2_.refs_3_.refs_4_.refs_5_, bf16[8,256,640]{2,1,0:T(8,128)(2,1)} %norm_tiles.1.refs_0_.refs_1_.refs_2_.refs_3_.refs_4_.refs_5_, ...), custom_call_target="tpu_custom_call", output_to_operand_aliasing={{0}: (13, {})} | custom-call | flops 4026531840 | bytes 19136512 | tf_op jit(solution)/shard_map/project/pallas_call | solution.py:187
  320.7 3.3 collective-permute-done.23.refs_3_
  324.3 4.7 %collective-permute-done.25.refs_5_ = f32[8,1024]{1,0:T(8,128)S(1)} collective-permute-done((f32[8,1024]{1,0:T(8,128)}, f32[8,1024]{1,0:T(8,128)S(1)}, u32[]{:S(2)}, u32[]{:S(2)}) %collective-permute-start.25) | collective-permute-done | bytes 32800 | tf_op jit(solution)/shard_map/ppermute | solution.py:380
  329.8 13.1 %soft_weights.2.refs_0_ = bf16[3,1024,1024]{2,1,0:T(8,128)(2,1)} custom-call(f32[6,1024,256]{2,1,0:T(8,128)} %get-tuple-element.38.refs_0_.refs_1_, f32[6,1024,256]{2,1,0:T(8,128)} %get-tuple-element.38.refs_0_.refs_1_, f32[8,1024]{1,0:T(8,128)} %get-tuple-element.39.refs_2_, f32[8,1024]{1,0:T(8,128)} %copy-done.12, f32[8,1024]{1,0:T(8,128)} %copy-done.13, ...), custom_call_target="tpu_custom_call" | custom-call | flops 830472192 | bytes 9437184 | tf_op jit(solution)/shard_map/soft_weights/pallas_call | solution.py:249
  345.1 13.1 %soft_weights.3.refs_1_ = bf16[3,1024,1024]{2,1,0:T(8,128)(2,1)} custom-call(f32[6,1024,256]{2,1,0:T(8,128)} %get-tuple-element.38.refs_0_.refs_1_, f32[6,1024,256]{2,1,0:T(8,128)} %get-tuple-element.38.refs_0_.refs_1_, f32[8,1024]{1,0:T(8,128)} %get-tuple-element.39.refs_2_, f32[8,1024]{1,0:T(8,128)} %copy-done.12, f32[8,1024]{1,0:T(8,128)} %copy-done.13, ...), custom_call_target="tpu_custom_call" | custom-call | flops 830472192 | bytes 9437184 | tf_op jit(solution)/shard_map/soft_weights/pallas_call | solution.py:249
  358.2 12.9 %project.5.refs_14_ = f32[3,1024,256]{2,1,0:T(8,128)} custom-call(s32[6]{0:T(128)} %stack.78.at_ref, bf16[8,256,640]{2,1,0:T(8,128)(2,1)} %norm_tiles.1.refs_0_.refs_1_.refs_2_.refs_3_.refs_4_.refs_5_, bf16[8,256,640]{2,1,0:T(8,128)(2,1)} %norm_tiles.1.refs_0_.refs_1_.refs_2_.refs_3_.refs_4_.refs_5_, ...), custom_call_target="tpu_custom_call" | custom-call | flops 6039797760 | bytes 20054016 | tf_op jit(solution)/shard_map/project/pallas_call | solution.py:187
  375.0 15.0 %mix_values.1 = bf16[8,4,32,768]{3,2,1,0:T(8,128)(2,1)} custom-call(s32[4]{0:T(128)} %pad_add_fusion.order_ref, s32[16]{0:T(128)} %iota.27.place_ref, s32[2]{0:T(128)} %pad_add_fusion.1.at_ref, bf16[3,1024,1024]{2,1,0:T(8,128)(2,1)} %soft_weights.2.refs_0_, bf16[3,1024,1024]{2,1,0:T(8,128)(2,1)} %soft_weights.3.refs_1_, ...), custom_call_target="tpu_custom_call" | custom-call | flops 3623878656 | bytes 17301504 | tf_op jit(solution)/shard_map/mix_values/pallas_call | solution.py:316
  390.0 42.1 %all_to_all.5.in_ref = bf16[32,32,768]{2,1,0:T(8,128)(2,1)} all-to-all(bf16[32,32,768]{2,1,0:T(8,128)(2,1)} %bitcast.19), channel_id=1, replica_groups=mesh['bal'=8,'seq'=4] {'bal','seq'}, dimensions={0} | all-to-all | bytes 3145728 | tf_op jit(solution)/shard_map/all_to_all | solution.py:514
  432.0 2.7 place_tiles.1
  (121 shorter events, 33.1 us)
Async XLA Ops:
  3.0 86.8 %collective-permute-start.14 = (bf16[6,640,256]{2,1,0:T(8,128)(2,1)}, bf16[6,640,256]{2,1,0:T(8,128)(2,1)S(1)}, u32[]{:S(2)}, u32[]{:S(2)}) collective-permute-start(bf16[6,640,256]{2,1,0:T(8,128)(2,1)} %slice.38), channel_id=1, source_target_pairs={{0,0},{1,4},{2,2},{3,6},{4,1},{5,5},{6,3},{7,7},{8,8},{9,12},{10,1... | collective-permute-start | bytes 5898248 | tf_op jit(solution)/shard_map/ppermute | solution.py:380
  5.3 16.2 %collective-permute-start.1 = (f32[4,2,5120]{2,1,0:T(2,128)S(1)}, f32[4,2,5120]{2,1,0:T(2,128)S(1)}, u32[]{:S(2)}, u32[]{:S(2)}) collective-permute-start(f32[4,2,5120]{2,1,0:T(2,128)S(1)} %bitcast.26), channel_id=1, source_target_pairs={{0,0},{1,4},{2,2},{3,6},{4,1},{5,5},{6,3},{7,7},{8,8},{9,12},{10,1... | collective-permute-start | bytes 491528 | tf_op jit(solution)/shard_map/ppermute | solution.py:380
  10.2 31.8 %collective-permute-start.2 = (bf16[2,16,5120]{2,1,0:T(8,128)(2,1)}, bf16[2,16,5120]{2,1,0:T(8,128)(2,1)S(1)}, u32[]{:S(2)}, u32[]{:S(2)}) collective-permute-start(bf16[2,16,5120]{2,1,0:T(8,128)(2,1)} %get-tuple-element.26), channel_id=1, source_target_pairs={{0,0},{1,4},{2,2},{3,6},{4,1},{5,5},{6,3},{7,7},{8,8},{9,12},{10,1... | collective-permute-start | bytes 983048 | tf_op jit(solution)/shard_map/ppermute | solution.py:380
  12.5 31.2 %collective-permute-start.3 = (bf16[2,16,5120]{2,1,0:T(8,128)(2,1)}, bf16[2,16,5120]{2,1,0:T(8,128)(2,1)S(1)}, u32[]{:S(2)}, u32[]{:S(2)}) collective-permute-start(bf16[2,16,5120]{2,1,0:T(8,128)(2,1)} %get-tuple-element.27), channel_id=1, source_target_pairs={{0,1},{1,5},{2,3},{3,7},{4,8},{5,12},{6,10},{7,14},{8,9},{9,13},{1... | collective-permute-start | bytes 983048 | tf_op jit(solution)/shard_map/ppermute | solution.py:380
  19.9 24.7 %collective-permute-start.4 = (bf16[2,16,5120]{2,1,0:T(8,128)(2,1)}, bf16[2,16,5120]{2,1,0:T(8,128)(2,1)S(1)}, u32[]{:S(2)}, u32[]{:S(2)}) collective-permute-start(bf16[2,16,5120]{2,1,0:T(8,128)(2,1)} %get-tuple-element.28), channel_id=1, source_target_pairs={{0,8},{1,12},{2,10},{3,14},{4,9},{5,13},{6,11},{7,15},{8,16},{9,20... | collective-permute-start | bytes 983048 | tf_op jit(solution)/shard_map/ppermute | solution.py:380
  21.5 48.6 %collective-permute-start.5 = (bf16[2,16,5120]{2,1,0:T(8,128)(2,1)}, bf16[2,16,5120]{2,1,0:T(8,128)(2,1)S(1)}, u32[]{:S(2)}, u32[]{:S(2)}) collective-permute-start(bf16[2,16,5120]{2,1,0:T(8,128)(2,1)} %get-tuple-element.29), channel_id=1, source_target_pairs={{0,9},{1,13},{2,11},{3,15},{4,16},{5,20},{6,18},{7,22},{8,17},{9,2... | collective-permute-start | bytes 983048 | tf_op jit(solution)/shard_map/ppermute | solution.py:380
  42.0 34.0 %collective-permute-start.6 = (bf16[2,16,5120]{2,1,0:T(8,128)(2,1)}, bf16[2,16,5120]{2,1,0:T(8,128)(2,1)}, u32[]{:S(2)}, u32[]{:S(2)}) collective-permute-start(bf16[2,16,5120]{2,1,0:T(8,128)(2,1)} %get-tuple-element.30), channel_id=1, source_target_pairs={{0,16},{1,20},{2,18},{3,22},{4,17},{5,21},{6,19},{7,23},{8,24},{9,... | collective-permute-start | bytes 983048 | tf_op jit(solution)/shard_map/ppermute | solution.py:380
  43.7 32.2 %collective-permute-start.7 = (bf16[2,16,5120]{2,1,0:T(8,128)(2,1)}, bf16[2,16,5120]{2,1,0:T(8,128)(2,1)}, u32[]{:S(2)}, u32[]{:S(2)}) collective-permute-start(bf16[2,16,5120]{2,1,0:T(8,128)(2,1)} %get-tuple-element.31), channel_id=1, source_target_pairs={{0,17},{1,21},{2,19},{3,23},{4,24},{5,28},{6,26},{7,30},{8,25},{9,... | collective-permute-start | bytes 983048 | tf_op jit(solution)/shard_map/ppermute | solution.py:380
  44.6 31.3 %collective-permute-start.8 = (bf16[2,16,5120]{2,1,0:T(8,128)(2,1)}, bf16[2,16,5120]{2,1,0:T(8,128)(2,1)}, u32[]{:S(2)}, u32[]{:S(2)}) collective-permute-start(bf16[2,16,5120]{2,1,0:T(8,128)(2,1)} %get-tuple-element.32), channel_id=1, source_target_pairs={{0,24},{1,28},{2,26},{3,30},{4,25},{5,29},{6,27},{7,31},{8,0},{9,4... | collective-permute-start | bytes 983048 | tf_op jit(solution)/shard_map/ppermute | solution.py:380
  70.1 9.0 %collective-permute-start.9 = (bf16[2,16,5120]{2,1,0:T(8,128)(2,1)}, bf16[2,16,5120]{2,1,0:T(8,128)(2,1)}, u32[]{:S(2)}, u32[]{:S(2)}) collective-permute-start(bf16[2,16,5120]{2,1,0:T(8,128)(2,1)} %get-tuple-element.33), channel_id=1, source_target_pairs={{0,25},{1,29},{2,27},{3,31},{4,0},{5,4},{6,2},{7,6},{8,1},{9,5},{1... | collective-permute-start | bytes 983048 | tf_op jit(solution)/shard_map/ppermute | solution.py:380
  88.3 55.9 %collective-permute-start.11 = (bf16[8,256,640]{2,1,0:T(8,128)(2,1)}, bf16[8,256,640]{2,1,0:T(8,128)(2,1)S(1)}, u32[]{:S(2)}, u32[]{:S(2)}) collective-permute-start(bf16[8,256,640]{2,1,0:T(8,128)(2,1)} %norm_tiles.1.refs_0_.refs_1_.refs_2_.refs_3_.refs_4_.refs_5_), channel_id=1, source_target_pairs={{0,2},{1,3},{2,0},{3,1},{4,6},{5,7},{6,4},{7,5},{8,10},{9,11},{10,... | collective-permute-start | bytes 7864328 | tf_op jit(solution)/shard_map/ppermute | solution.py:380
  89.8 100.4 %collective-permute-start.10 = (bf16[8,256,640]{2,1,0:T(8,128)(2,1)}, bf16[8,256,640]{2,1,0:T(8,128)(2,1)S(1)}, u32[]{:S(2)}, u32[]{:S(2)}) collective-permute-start(bf16[8,256,640]{2,1,0:T(8,128)(2,1)} %norm_tiles.1.refs_0_.refs_1_.refs_2_.refs_3_.refs_4_.refs_5_), channel_id=1, source_target_pairs={{0,4},{1,5},{2,6},{3,7},{4,0},{5,1},{6,2},{7,3},{8,12},{9,13},{10,... | collective-permute-start | bytes 7864328 | tf_op jit(solution)/shard_map/ppermute | solution.py:380
  89.8 97.1 %collective-permute-start.18 = (bf16[6,640,256]{2,1,0:T(8,128)(2,1)S(1)}, bf16[6,640,256]{2,1,0:T(8,128)(2,1)}, u32[]{:S(2)}, u32[]{:S(2)}) collective-permute-start(bf16[6,640,256]{2,1,0:T(8,128)(2,1)S(1)} %collective-permute-done.14.refs_30_), channel_id=1, source_target_pairs={{0,8},{1,9},{2,10},{3,11},{4,12},{5,13},{6,14},{7,15},{8,0},{9,1},... | collective-permute-start | bytes 5898248 | tf_op jit(solution)/shard_map/ppermute | solution.py:380
  104.4 85.7 %collective-permute-start.15 = (bf16[6,640,256]{2,1,0:T(8,128)(2,1)S(1)}, bf16[6,640,256]{2,1,0:T(8,128)(2,1)}, u32[]{:S(2)}, u32[]{:S(2)}) collective-permute-start(bf16[6,640,256]{2,1,0:T(8,128)(2,1)S(1)} %collective-permute-done.14.refs_30_), channel_id=1, source_target_pairs={{0,16},{1,17},{2,18},{3,19},{4,20},{5,21},{6,22},{7,23},{8,24},{9,... | collective-permute-start | bytes 5898248 | tf_op jit(solution)/shard_map/ppermute | solution.py:380
  107.8 84.3 %collective-permute-start.17 = (bf16[6,640,256]{2,1,0:T(8,128)(2,1)S(1)}, bf16[6,640,256]{2,1,0:T(8,128)(2,1)S(1)}, u32[]{:S(2)}, u32[]{:S(2)}) collective-permute-start(bf16[6,640,256]{2,1,0:T(8,128)(2,1)S(1)} %collective-permute-done.14.refs_30_), channel_id=1, source_target_pairs={{0,1},{1,0},{2,3},{3,2},{4,5},{5,4},{6,7},{7,6},{8,9},{9,8},{10,11... | collective-permute-start | bytes 5898248 | tf_op jit(solution)/shard_map/ppermute | solution.py:380
  144.3 51.0 %collective-permute-start.12 = (bf16[8,128,640]{2,1,0:T(8,128)(2,1)S(1)}, bf16[8,128,640]{2,1,0:T(8,128)(2,1)}, u32[]{:S(2)}, u32[]{:S(2)}) collective-permute-start(bf16[8,128,640]{2,1,0:T(8,128)(2,1)S(1)} %slice.36), channel_id=1, source_target_pairs={{0,4},{1,5},{2,6},{3,7},{4,0},{5,1},{6,2},{7,3},{8,12},{9,13},{10,... | collective-permute-start | bytes 3932168 | tf_op jit(solution)/shard_map/ppermute | solution.py:380
  186.9 44.9 %collective-permute-start.19 = (bf16[6,640,256]{2,1,0:T(8,128)(2,1)}, bf16[6,640,256]{2,1,0:T(8,128)(2,1)}, u32[]{:S(2)}, u32[]{:S(2)}) collective-permute-start(bf16[6,640,256]{2,1,0:T(8,128)(2,1)} %collective-permute-done.18.refs_32_), channel_id=1, source_target_pairs={{0,1},{1,0},{2,3},{3,2},{4,5},{5,4},{6,7},{7,6},{8,9},{9,8},{10,11... | collective-permute-start | bytes 5898248 | tf_op jit(solution)/shard_map/ppermute | solution.py:380
  190.2 41.7 %collective-permute-start.20 = (bf16[6,640,256]{2,1,0:T(8,128)(2,1)}, bf16[6,640,256]{2,1,0:T(8,128)(2,1)}, u32[]{:S(2)}, u32[]{:S(2)}) collective-permute-start(bf16[6,640,256]{2,1,0:T(8,128)(2,1)} %collective-permute-done.15.refs_34_), channel_id=1, source_target_pairs={{0,1},{1,0},{2,3},{3,2},{4,5},{5,4},{6,7},{7,6},{8,9},{9,8},{10,11... | collective-permute-start | bytes 5898248 | tf_op jit(solution)/shard_map/ppermute | solution.py:380
  191.5 31.5 %collective-permute-start.13 = (bf16[8,128,640]{2,1,0:T(8,128)(2,1)}, bf16[8,128,640]{2,1,0:T(8,128)(2,1)}, u32[]{:S(2)}, u32[]{:S(2)}) collective-permute-start(bf16[8,128,640]{2,1,0:T(8,128)(2,1)} %slice.37), channel_id=1, source_target_pairs={{0,2},{1,3},{2,0},{3,1},{4,6},{5,7},{6,4},{7,5},{8,10},{9,11},{10,... | collective-permute-start | bytes 3932168 | tf_op jit(solution)/shard_map/ppermute | solution.py:380
  193.4 58.9 %collective-permute-start.16 = (bf16[6,640,256]{2,1,0:T(8,128)(2,1)S(1)}, bf16[6,640,256]{2,1,0:T(8,128)(2,1)}, u32[]{:S(2)}, u32[]{:S(2)}) collective-permute-start(bf16[6,640,256]{2,1,0:T(8,128)(2,1)S(1)} %collective-permute-done.14.refs_30_), channel_id=1, source_target_pairs={{8,16},{9,17},{10,18},{11,19},{12,20},{13,21},{14,22},{15,23},{16,... | collective-permute-start | bytes 5898248 | tf_op jit(solution)/shard_map/ppermute | solution.py:471
  195.3 57.0 %collective-permute-start.21 = (bf16[6,640,256]{2,1,0:T(8,128)(2,1)}, bf16[6,640,256]{2,1,0:T(8,128)(2,1)}, u32[]{:S(2)}, u32[]{:S(2)}) collective-permute-start(bf16[6,640,256]{2,1,0:T(8,128)(2,1)} %collective-permute-done.15.refs_34_), channel_id=1, source_target_pairs={{8,0},{9,1},{10,2},{11,3},{12,4},{13,5},{14,6},{15,7},{16,24},{17,... | collective-permute-start | bytes 5898248 | tf_op jit(solution)/shard_map/ppermute | solution.py:471
  222.9 32.1 %collective-permute-start.28 = (bf16[3,640,256]{2,1,0:T(8,128)(2,1)}, bf16[3,640,256]{2,1,0:T(8,128)(2,1)}, u32[]{:S(2)}, u32[]{:S(2)}) collective-permute-start(bf16[3,640,256]{2,1,0:T(8,128)(2,1)} %pad_maximum_fusion), channel_id=1, source_target_pairs={{0,0},{1,4},{2,2},{3,6},{4,1},{5,5},{6,3},{7,7},{8,8},{9,12},{10,1... | collective-permute-start | bytes 2949128 | tf_op jit(solution)/shard_map/ppermute | solution.py:380
  255.0 51.6 %collective-permute-start.22 = (bf16[6,640,256]{2,1,0:T(8,128)(2,1)S(1)}, bf16[6,640,256]{2,1,0:T(8,128)(2,1)}, u32[]{:S(2)}, u32[]{:S(2)}) collective-permute-start(bf16[6,640,256]{2,1,0:T(8,128)(2,1)S(1)} %add.127.refs_10_), channel_id=1, source_target_pairs={{0,1},{1,0},{2,3},{3,2},{4,5},{5,4},{6,7},{7,6},{8,9},{9,8},{10,11... | collective-permute-start | bytes 5898248 | tf_op jit(solution)/shard_map/ppermute | solution.py:380
  255.1 48.3 %collective-permute-start.32 = (bf16[3,640,256]{2,1,0:T(8,128)(2,1)}, bf16[3,640,256]{2,1,0:T(8,128)(2,1)}, u32[]{:S(2)}, u32[]{:S(2)}) collective-permute-start(bf16[3,640,256]{2,1,0:T(8,128)(2,1)} %collective-permute-done.28.refs_30_), channel_id=1, source_target_pairs={{0,8},{1,9},{2,10},{3,11},{4,12},{5,13},{6,14},{7,15},{8,0},{9,1},... | collective-permute-start | bytes 2949128 | tf_op jit(solution)/shard_map/ppermute | solution.py:380
  259.9 46.7 %collective-permute-start.29 = (bf16[3,640,256]{2,1,0:T(8,128)(2,1)}, bf16[3,640,256]{2,1,0:T(8,128)(2,1)}, u32[]{:S(2)}, u32[]{:S(2)}) collective-permute-start(bf16[3,640,256]{2,1,0:T(8,128)(2,1)} %collective-permute-done.28.refs_30_), channel_id=1, source_target_pairs={{0,16},{1,17},{2,18},{3,19},{4,20},{5,21},{6,22},{7,23},{8,24},{9,... | collective-permute-start | bytes 2949128 | tf_op jit(solution)/shard_map/ppermute | solution.py:380
  263.0 56.7 %collective-permute-start.26 = (f32[6,128]{1,0:T(8,128)S(1)}, f32[6,128]{1,0:T(8,128)S(1)}, u32[]{:S(2)}, u32[]{:S(2)}) collective-permute-start(f32[6,128]{1,0:T(8,128)S(1)} %copy-done.19), channel_id=1, source_target_pairs={{0,0},{1,4},{2,2},{3,6},{4,1},{5,5},{6,3},{7,7},{8,8},{9,12},{10,1... | collective-permute-start | bytes 9224 | tf_op jit(solution)/shard_map/ppermute | solution.py:380
  263.7 56.4 %collective-permute-start.27 = (f32[6,128]{1,0:T(8,128)S(1)}, f32[6,128]{1,0:T(8,128)S(1)}, u32[]{:S(2)}, u32[]{:S(2)}) collective-permute-start(f32[6,128]{1,0:T(8,128)S(1)} %copy-done.20), channel_id=1, source_target_pairs={{0,0},{1,4},{2,2},{3,6},{4,1},{5,5},{6,3},{7,7},{8,8},{9,12},{10,1... | collective-permute-start | bytes 9224 | tf_op jit(solution)/shard_map/ppermute | solution.py:380
  303.3 54.9 %collective-permute-start.31 = (bf16[3,640,256]{2,1,0:T(8,128)(2,1)}, bf16[3,640,256]{2,1,0:T(8,128)(2,1)}, u32[]{:S(2)}, u32[]{:S(2)}) collective-permute-start(bf16[3,640,256]{2,1,0:T(8,128)(2,1)} %collective-permute-done.28.refs_30_), channel_id=1, source_target_pairs={{0,1},{1,0},{2,3},{3,2},{4,5},{5,4},{6,7},{7,6},{8,9},{9,8},{10,11... | collective-permute-start | bytes 2949128 | tf_op jit(solution)/shard_map/ppermute | solution.py:380
  306.6 51.7 %collective-permute-start.33 = (bf16[3,640,256]{2,1,0:T(8,128)(2,1)}, bf16[3,640,256]{2,1,0:T(8,128)(2,1)}, u32[]{:S(2)}, u32[]{:S(2)}) collective-permute-start(bf16[3,640,256]{2,1,0:T(8,128)(2,1)} %collective-permute-done.32.refs_32_), channel_id=1, source_target_pairs={{0,1},{1,0},{2,3},{3,2},{4,5},{5,4},{6,7},{7,6},{8,9},{9,8},{10,11... | collective-permute-start | bytes 2949128 | tf_op jit(solution)/shard_map/ppermute | solution.py:380
  306.6 51.7 %collective-permute-start.34 = (bf16[3,640,256]{2,1,0:T(8,128)(2,1)}, bf16[3,640,256]{2,1,0:T(8,128)(2,1)}, u32[]{:S(2)}, u32[]{:S(2)}) collective-permute-start(bf16[3,640,256]{2,1,0:T(8,128)(2,1)} %collective-permute-done.29.refs_34_), channel_id=1, source_target_pairs={{0,1},{1,0},{2,3},{3,2},{4,5},{5,4},{6,7},{7,6},{8,9},{9,8},{10,11... | collective-permute-start | bytes 2949128 | tf_op jit(solution)/shard_map/ppermute | solution.py:380
  342.9 28.2 %collective-permute-start.30 = (bf16[3,640,256]{2,1,0:T(8,128)(2,1)}, bf16[3,640,256]{2,1,0:T(8,128)(2,1)S(1)}, u32[]{:S(2)}, u32[]{:S(2)}) collective-permute-start(bf16[3,640,256]{2,1,0:T(8,128)(2,1)} %collective-permute-done.28.refs_30_), channel_id=1, source_target_pairs={{8,16},{9,17},{10,18},{11,19},{12,20},{13,21},{14,22},{15,23},{16,... | collective-permute-start | bytes 2949128 | tf_op jit(solution)/shard_map/ppermute | solution.py:471
  343.6 27.5 %collective-permute-start.35 = (bf16[3,640,256]{2,1,0:T(8,128)(2,1)}, bf16[3,640,256]{2,1,0:T(8,128)(2,1)S(1)}, u32[]{:S(2)}, u32[]{:S(2)}) collective-permute-start(bf16[3,640,256]{2,1,0:T(8,128)(2,1)} %collective-permute-done.29.refs_34_), channel_id=1, source_target_pairs={{8,0},{9,1},{10,2},{11,3},{12,4},{13,5},{14,6},{15,7},{16,24},{17,... | collective-permute-start | bytes 2949128 | tf_op jit(solution)/shard_map/ppermute | solution.py:471
  (26 other events, 517.5 us)

commit v3 on v2

--- a/solution.py
+++ b/solution.py
@@ -211,9 +211,9 @@
         q_ref, k_ref = refs[0], refs[1]
         sum_refs = refs[2 : 2 + n]
         qg_ref, kg_ref, bias_ref, out_ref, scales, keys = refs[2 + n :]
-        head, block = pl.program_id(0), pl.program_id(1)
-
-        @pl.when((head == 0) & (block == 0))
+        head = pl.program_id(0)
+
+        @pl.when(head == 0)
         def _():
             keys[:, dim:] = bias_ref[...]
             for p in range(n):
@@ -224,39 +224,37 @@
                     whole = part if whole is None else whole + part
                 scales[p * rows : (p + 1) * rows] = jnp.transpose(lax.rsqrt(whole / features + eps_norm))
 
-        @pl.when(block == 0)
-        def _():
-            keys[:, :dim] = (k_ref[0] * scales[:, 1:2] * kg_ref[pl.ds(first + head, 1), :]).astype(keys.dtype)
-
-        at = pl.multiple_of(block * rows, rows)
-        query = q_ref[0] * scales[pl.ds(at, rows), 0:1] * qg_ref[pl.ds(first + head, 1), :]
+        keys[:, :dim] = (k_ref[0] * scales[:, 1:2] * kg_ref[pl.ds(first + head, 1), :]).astype(keys.dtype)
         lane = lax.broadcasted_iota(jnp.int32, (rows, extra), 1)
         row = lax.broadcasted_iota(jnp.int32, (rows, extra), 0)
         tile = (row // (rows // TILES_OWN) == lane).astype(keys.dtype)
-        scores = lax.dot_general(
-            jnp.concatenate([query.astype(keys.dtype), tile], axis=1),
-            keys[...],
-            (((1,), (1,)), ((), ())),
-            preferred_element_type=jnp.float32,
-        )
-        largest = jnp.max(scores, axis=-1, keepdims=True)
-        powers = jnp.exp2((scores - largest) * (dim ** (-0.5) * log2_e))
-        share = 1.0 / jnp.sum(powers, axis=-1, keepdims=True)
-        out_ref[0] = (powers * share).astype(out_ref.dtype)
-
-    whole_sum = pl.BlockSpec((8, total), lambda h, b: (0, 0))
-    gain = pl.BlockSpec((heads, dim), lambda h, b: (0, 0))
+        for p in range(n):
+            here = slice(p * rows, (p + 1) * rows)
+            query = q_ref[0, here] * scales[here, 0:1] * qg_ref[pl.ds(first + head, 1), :]
+            scores = lax.dot_general(
+                jnp.concatenate([query.astype(keys.dtype), tile], axis=1),
+                keys[...],
+                (((1,), (1,)), ((), ())),
+                preferred_element_type=jnp.float32,
+            )
+            largest = jnp.max(scores, axis=-1, keepdims=True)
+            powers = jnp.exp2((scores - largest) * (dim ** (-0.5) * log2_e))
+            share = 1.0 / jnp.sum(powers, axis=-1, keepdims=True)
+            out_ref[0, here] = (powers * share).astype(out_ref.dtype)
+
+    whole_sum = pl.BlockSpec((8, total), lambda h: (0, 0))
+    gain = pl.BlockSpec((heads, dim), lambda h: (0, 0))
     return pl.pallas_call(
         body,
         out_shape=jax.ShapeDtypeStruct((count, total, total), jnp.bfloat16),
-        grid=(count, total // rows),
+        grid=(count,),
         in_specs=[
-            pl.BlockSpec((1, rows, dim), lambda h, b: (first + h, b, 0)),
-            pl.BlockSpec((1, total, dim), lambda h, b: (first + h, 0, 1)),
+            pl.BlockSpec((1, total, dim), lambda h: (first + h, 0, 0)),
+            pl.BlockSpec((1, total, dim), lambda h: (first + h, 0, 1)),
         ]
         + [whole_sum] * n
-        + [gain, gain, pl.BlockSpec(bias.shape, lambda h, b: (0, 0))],
-        out_specs=pl.BlockSpec((1, rows, total), lambda h, b: (h, b, 0)),
+        + [gain, gain, pl.BlockSpec(bias.shape, lambda h: (0, 0))],
+        out_specs=pl.BlockSpec((1, total, total), lambda h: (h, 0, 0)),
         scratch_shapes=[pltpu.VMEM((total, 8), jnp.float32), pltpu.VMEM((total, dim + extra), jnp.bfloat16)],
         cost_estimate=pl.CostEstimate(
             flops=(2 * dim + 8) * count * total * total,
@@ -388,13 +386,16 @@
     def other_core(value):
         return send(value, lambda z, x, y, c: (z, x, y, 1 - c))
 
+    def after(value, *others):
+        return lax.optimization_barrier((value, *others))[0]
+
     bal, seq = lax.axis_index("bal"), lax.axis_index("seq")
     z, x, y, c = bal // 2, bal % 2, seq // 2, seq % 2
     ids = jnp.stack([bal, z * 2 + c]).astype(jnp.int32)
 
     outgoing = pick_tiles(tokens, tile_owner, ids, groups, capacity)
 
-    by_head = jnp.transpose(w_qkv, (1, 0, 2))
+    by_head = after(jnp.transpose(w_qkv, (1, 0, 2)), outgoing[0])
     pair = 2 if heads % 2 == 0 else 1
     v_columns = by_head[:, :, 2 * dim :]
     v_columns = jnp.concatenate([v_columns[i::pair] for i in range(pair)], axis=2)
@@ -410,8 +411,8 @@
     arrived = []
     for k in range(groups):
         arrived.append(send(outgoing[k], to_owner(k)))
-    table = swap(modulation[0])
-    clips = swap(clip_dims[0])
+    table = swap(after(modulation[0], outgoing[0]))
+    clips = swap(after(clip_dims[0], outgoing[0]))
     gains = (swap(q_gain), swap(k_gain))
     member, tile_mask = tile_layout(clips)
     if groups * capacity == TILES_OWN:
@@ -441,17 +442,18 @@
         order += [(y + py) % lines * 2 + x, (y + py) % lines * 2 + (x ^ 1)]
     order = jnp.stack(order).astype(jnp.int32)
 
-    def after(value, *others):
-        return lax.optimization_barrier((value, *others))[0]
-
-    def start_planes(own, *earlier):
+    def near_planes(own):
         if planes == 4:
-            one = send(own, lambda z, x, y, c: (z ^ 1, x, y, c))
-            return [own, one, send(after(own, *earlier), lambda z, x, y, c: (z ^ 2, x, y, c))]
+            return [own, send(own, lambda z, x, y, c: (z ^ 1, x, y, c))]
         got = [own]
         for _ in range(planes - 2):
             got.append(ring(got[-1]))
         return got
+
+    def far_plane(got, *earlier):
+        if planes != 4:
+            return got
+        return [*got, send(after(got[0], *earlier), lambda z, x, y, c: (z ^ 2, x, y, c))]
 
     def end_planes(got, *earlier):
         if planes == 4:
@@ -480,15 +482,21 @@
             at += [plane_at(step) * 2 + c, plane_at(step) * 2 + 1 - c]
         return blocks, jnp.stack(at).astype(jnp.int32)
 
-    early, late = range(planes - 1), [planes - 1]
-    qk_own = start_planes(after(qk_own[0], outgoing[0]), *arrived)
-    v_first = swap(after(v_columns, outgoing[0]))
+    qk_own = near_planes(qk_own[0])
+    qk_own = far_plane(qk_own, *arrived)
+    v_first = swap(v_columns)
+    v_own = near_planes(after(v_first, *arrived))
     qk_ends = end_planes(qk_own)
-    blocks, at = blocks_of(qk_own, early)
+
+    blocks, at = blocks_of(qk_own, range(planes - 1))
     qk, *_ = project(pieces, blocks, at, None, False)
-    v_own = start_planes(after(v_first, *pieces[-2:]), *qk_ends)
-    qk_own.append(last_plane(qk_ends, qk))
-    blocks, at = blocks_of(qk_own, late)
+    split = max(planes - 2, 1)
+    blocks, at = blocks_of(v_own, range(split))
+    blocks[0] = after(blocks[0], qk)
+    values, *_ = project(pieces, blocks, at, None, False)
+    v_own = far_plane(v_own, *qk_ends)
+    qk_own.append(last_plane(qk_ends, values))
+    blocks, at = blocks_of(qk_own, [planes - 1])
     qk, sums = project(pieces, blocks, at, qk, True)
     partial_sums = [sums, along_x(sums)]
     for py in range(1, lines):
@@ -505,11 +513,8 @@
         weights.append(part)
         if i == 0:
             v_ends = end_planes(v_own, weights[0])
-    blocks, at = blocks_of(v_own, early)
-    blocks[0] = after(blocks[0], weights[-1])
-    values, *_ = project(pieces, blocks, at, None, False)
-    v_own.append(last_plane(v_ends, values))
-    blocks, at = blocks_of(v_own, late)
+    v_own.append(last_plane(v_ends, weights[-1]))
+    blocks, at = blocks_of(v_own, range(split, planes))
     mixed = mix_values(weights, values, pieces, blocks, at, order, place, groups, capacity, piece)
     returned = lax.all_to_all(
         mixed.reshape(groups * n, capacity * piece, heads * dim), AXES, split_axis=0, concat_axis=0, tiled=True

time: 436 us -> 428 us (0.982)
  starting transfers between devices: 89.2 us -> 146 us
  waiting for transfers between devices: 184 us -> 130 us
  Pallas kernels: 102 us -> 92.1 us
    ppermute x33, waiting for transfers between devices: 184 us -> 113 us  [send(): return lax.ppermute(value, AXES, pairs)]
    ppermute x33, starting transfers between devices: 83.8 us -> 141 us  [send(): return lax.ppermute(value, AXES, pairs)]
    ppermute x4, waiting for transfers between devices: 0.01 us -> 16.5 us  [send_some(): return lax.ppermute(value, AXES, pairs)]
    pallas_call x2, Pallas kernels: 26.2 us -> 16.1 us  [soft_weights(): pl.pallas_call(body, out_shape=jax.ShapeDtypeStruct((count, total, total)...]
  transfers between devices with their start and end apart: 37 -> 37, of which waited for: 12 -> 15; matrix products, arithmetic and copies ran while one was open for 3% -> 2% of each run, Pallas kernels for 19% -> 16%
where the time goes in v3:
time: 428 us
  starting transfers between devices  146 us (34%)
  waiting for transfers between devices  130 us (30%)
  Pallas kernels  92.1 us (22%)
  blocking collectives  41.5 us (10%)
  local copies, waits for them, and re-layouts  9.4 us (2%)
  other arithmetic  8.18 us (2%)
    ppermute x33, starting transfers between devices, send(): return lax.ppermute(value, AXES, pairs)  141 us
    ppermute x33, waiting for transfers between devices, send(): return lax.ppermute(value, AXES, pairs)  113 us
    pallas_call x3, Pallas kernels, project(): pl.pallas_call(body, out_shape=out_shape, grid_spec=pltpu.PrefetchScalarG...  42.8 us
    all_to_all x1, blocking collectives, transposed(): lax.all_to_all(mixed.reshape(groups * n, capacity * piece, heads * dim),...  41.5 us
    pallas_call x1, Pallas kernels, mix_values(): pl.pallas_call(body, out_shape=jax.ShapeDtypeStruct((groups, n, capacity...  18.5 us
    ppermute x4, waiting for transfers between devices, send_some(): return lax.ppermute(value, AXES, pairs)  16.5 us
    pallas_call x2, Pallas kernels, soft_weights(): pl.pallas_call(body, out_shape=jax.ShapeDtypeStruct((count, total, total)...  16.1 us
  transfers between devices with their start and end apart: 37, of which 15 were waited for; matrix products, arithmetic and copies ran while one was open for 2% of the time, Pallas kernels for 16%

profile of v3, /device:TPU:0, one launch (start us, length us, event | category | flops | bytes accessed | tf_op | source)
XLA Modules:
  0.0 427.5 jit_solution(17914071012873135951)
XLA Ops:
  0.6 3.5 pick_tiles.1
  4.1 3.0 slice.32
  7.1 2.2 collective-permute-start.14
  11.6 6.1 %collective-permute-start.3 = (bf16[2,16,5120]{2,1,0:T(8,128)(2,1)}, bf16[2,16,5120]{2,1,0:T(8,128)(2,1)S(1)}, u32[]{:S(2)}, u32[]{:S(2)}) collective-permute-start(bf16[2,16,5120]{2,1,0:T(8,128)(2,1)} %get-tuple-element.30), channel_id=1, source_target_pairs={{0,1},{1,5},{2,3},{3,7},{4,8},{5,12},{6,10},{7,14},{8,9},{9,13},{1... | collective-permute-start | bytes 983048 | tf_op jit(solution)/shard_map/ppermute | solution.py:378
  20.1 27.2 %collective-permute-start.5 = (bf16[2,16,5120]{2,1,0:T(8,128)(2,1)}, bf16[2,16,5120]{2,1,0:T(8,128)(2,1)S(1)}, u32[]{:S(2)}, u32[]{:S(2)}) collective-permute-start(bf16[2,16,5120]{2,1,0:T(8,128)(2,1)} %get-tuple-element.32), channel_id=1, source_target_pairs={{0,9},{1,13},{2,11},{3,15},{4,16},{5,20},{6,18},{7,22},{8,17},{9,2... | collective-permute-start | bytes 983048 | tf_op jit(solution)/shard_map/ppermute | solution.py:378
  49.1 2.8 collective-permute-start.8
  51.8 22.6 %collective-permute-done.5.rest_3_ = bf16[2,16,5120]{2,1,0:T(8,128)(2,1)S(1)} collective-permute-done((bf16[2,16,5120]{2,1,0:T(8,128)(2,1)}, bf16[2,16,5120]{2,1,0:T(8,128)(2,1)S(1)}, u32[]{:S(2)}, u32[]{:S(2)}) %collective-permute-start.5) | collective-permute-done | bytes 327712 | tf_op jit(solution)/shard_map/ppermute | solution.py:378
  75.0 6.3 %collective-permute-done.6.rest_4_ = bf16[2,16,5120]{2,1,0:T(8,128)(2,1)} collective-permute-done((bf16[2,16,5120]{2,1,0:T(8,128)(2,1)}, bf16[2,16,5120]{2,1,0:T(8,128)(2,1)}, u32[]{:S(2)}, u32[]{:S(2)}) %collective-permute-start.6) | collective-permute-done | bytes 327712 | tf_op jit(solution)/shard_map/ppermute | solution.py:378
  81.3 2.6 collective-permute-done.9.rest_7_
  84.5 8.5 %norm_tiles.1.refs_0_.refs_1_.refs_2_.refs_3_.refs_4_.refs_5_ = bf16[8,256,640]{2,1,0:T(8,128)(2,1)} custom-call(s32[16]{0:T(128)} %broadcast_maximum_fusion.1.member_ref, s32[16]{0:T(128)} %iota.28.place_ref, s32[2]{0:T(128)} %pad_add_fusion.3.ids_ref, f32[4,2,5120]{2,1,0:T(2,128)} %copy-done.15, bf16[2,16,5120]{2,1,0:T(8,128)(2,1)} %copy-done.11, ...), custom_call_target="tpu_custom_call" | custom-call | flops 15728640 | bytes 5242880 | tf_op jit(solution)/shard_map/norm_tiles/pallas_call | solution.py:117
  94.5 18.0 %collective-permute-start.15 = (bf16[6,640,256]{2,1,0:T(8,128)(2,1)S(1)}, bf16[6,640,256]{2,1,0:T(8,128)(2,1)}, u32[]{:S(2)}, u32[]{:S(2)}) collective-permute-start(bf16[6,640,256]{2,1,0:T(8,128)(2,1)S(1)} %collective-permute-done.14.refs_30_), channel_id=1, source_target_pairs={{0,16},{1,17},{2,18},{3,19},{4,20},{5,21},{6,22},{7,23},{8,24},{9,... | collective-permute-start | bytes 5898248 | tf_op jit(solution)/shard_map/ppermute | solution.py:378
  114.7 50.5 %collective-permute-start.18 = (bf16[6,640,256]{2,1,0:T(8,128)(2,1)S(1)}, bf16[6,640,256]{2,1,0:T(8,128)(2,1)S(1)}, u32[]{:S(2)}, u32[]{:S(2)}) collective-permute-start(bf16[6,640,256]{2,1,0:T(8,128)(2,1)S(1)} %collective-permute-done.14.refs_30_), channel_id=1, source_target_pairs={{0,1},{1,0},{2,3},{3,2},{4,5},{5,4},{6,7},{7,6},{8,9},{9,8},{10,11... | collective-permute-start | bytes 5898248 | tf_op jit(solution)/shard_map/ppermute | solution.py:378
  165.2 15.6 %collective-permute-start.23 = (bf16[3,640,256]{2,1,0:T(8,128)(2,1)S(1)}, bf16[3,640,256]{2,1,0:T(8,128)(2,1)S(1)}, u32[]{:S(2)}, u32[]{:S(2)}) collective-permute-start(bf16[3,640,256]{2,1,0:T(8,128)(2,1)S(1)} %collective-permute-done.17.refs_20_), channel_id=1, source_target_pairs={{0,8},{1,9},{2,10},{3,11},{4,12},{5,13},{6,14},{7,15},{8,0},{9,1},... | collective-permute-start | bytes 2949128 | tf_op jit(solution)/shard_map/ppermute | solution.py:378
  180.8 16.8 %collective-permute-done.15.refs_34_ = bf16[6,640,256]{2,1,0:T(8,128)(2,1)} collective-permute-done((bf16[6,640,256]{2,1,0:T(8,128)(2,1)S(1)}, bf16[6,640,256]{2,1,0:T(8,128)(2,1)}, u32[]{:S(2)}, u32[]{:S(2)}) %collective-permute-start.15) | collective-permute-done | bytes 1966112 | tf_op jit(solution)/shard_map/ppermute | solution.py:378
  201.8 18.2 %collective-permute-done.23.refs_22_ = bf16[3,640,256]{2,1,0:T(8,128)(2,1)S(1)} collective-permute-done((bf16[3,640,256]{2,1,0:T(8,128)(2,1)S(1)}, bf16[3,640,256]{2,1,0:T(8,128)(2,1)S(1)}, u32[]{:S(2)}, u32[]{:S(2)}) %collective-permute-start.23) | collective-permute-done | bytes 983072 | tf_op jit(solution)/shard_map/ppermute | solution.py:378
  220.5 2.0 collective-permute-start.16
  222.5 8.3 %collective-permute-done.12.refs_18_.refs_19_.refs_20_.refs_21_.refs_22_.refs_23_.refs_12_.refs_13_.refs_14_.refs_15_.refs_6_.refs_7_.refs_16_.refs_17_ = bf16[8,128,640]{2,1,0:T(8,128)(2,1)} collective-permute-done((bf16[8,128,640]{2,1,0:T(8,128)(2,1)S(1)}, bf16[8,128,640]{2,1,0:T(8,128)(2,1)}, u32[]{:S(2)}, u32[]{:S(2)}) %collective-permute-start.12) | collective-permute-done | bytes 1310752 | tf_op jit(solution)/shard_map/ppermute | solution.py:378
  233.3 18.1 %collective-permute-done.13.refs_24_.refs_25_.refs_26_.refs_27_.refs_28_.refs_29_.refs_16_.refs_17_.refs_18_.refs_19_.refs_8_.refs_9_.refs_20_.refs_21_ = bf16[8,128,640]{2,1,0:T(8,128)(2,1)S(1)} collective-permute-done((bf16[8,128,640]{2,1,0:T(8,128)(2,1)}, bf16[8,128,640]{2,1,0:T(8,128)(2,1)S(1)}, u32[]{:S(2)}, u32[]{:S(2)}) %collective-permute-start.13) | collective-permute-done | bytes 1310752 | tf_op jit(solution)/shard_map/ppermute | solution.py:378
  252.5 20.4 %project.3.refs_12_ = f32[6,1024,256]{2,1,0:T(8,128)} custom-call(s32[6]{0:T(128)} %stack.84.at_ref, bf16[8,256,640]{2,1,0:T(8,128)(2,1)} %norm_tiles.1.refs_0_.refs_1_.refs_2_.refs_3_.refs_4_.refs_5_, bf16[8,256,640]{2,1,0:T(8,128)(2,1)} %norm_tiles.1.refs_0_.refs_1_.refs_2_.refs_3_.refs_4_.refs_5_, ...), custom_call_target="tpu_custom_call" | custom-call | flops 12079595520 | bytes 32243712 | tf_op jit(solution)/shard_map/project/pallas_call | solution.py:187
  273.0 9.6 %project.4.refs_26_ = f32[3,1024,256]{2,1,0:T(8,128)} custom-call(s32[4]{0:T(128)} %pad_add_fusion.4.at_ref, bf16[8,256,640]{2,1,0:T(8,128)(2,1)} %norm_tiles.1.refs_0_.refs_1_.refs_2_.refs_3_.refs_4_.refs_5_, bf16[8,256,640]{2,1,0:T(8,128)(2,1)} %norm_tiles.1.refs_0_.refs_1_.refs_2_.refs_3_.refs_4_.refs_5_, ...), custom_call_target="tpu_custom_call" | custom-call | flops 4026531840 | bytes 15466496 | tf_op jit(solution)/shard_map/project/pallas_call | solution.py:187
  282.6 2.7 add.127.refs_10_
  289.5 12.7 %project.5 = (f32[6,1024,256]{2,1,0:T(8,128)}, f32[8,1024]{1,0:T(8,128)}) custom-call(s32[2]{0:T(128)} %pad_add_fusion.2.at_ref, bf16[8,256,640]{2,1,0:T(8,128)(2,1)} %norm_tiles.1.refs_0_.refs_1_.refs_2_.refs_3_.refs_4_.refs_5_, bf16[8,256,640]{2,1,0:T(8,128)(2,1)} %norm_tiles.1.refs_0_.refs_1_.refs_2_.refs_3_.refs_4_.refs_5_, ...), custom_call_target="tpu_custom_call", output_to_operand_aliasing={{0}: (13, {})} | custom-call | flops 4026531840 | bytes 19136512 | tf_op jit(solution)/shard_map/project/pallas_call | solution.py:187
  302.2 4.4 %collective-permute-start.27 = (f32[8,1024]{1,0:T(8,128)}, f32[8,1024]{1,0:T(8,128)S(1)}, u32[]{:S(2)}, u32[]{:S(2)}) collective-permute-start(f32[8,1024]{1,0:T(8,128)} %get-tuple-element.44.refs_2_), channel_id=1, source_target_pairs={{0,4},{1,5},{2,6},{3,7},{4,0},{5,1},{6,2},{7,3},{8,12},{9,13},{10,... | collective-permute-start | bytes 98312 | tf_op jit(solution)/shard_map/ppermute | solution.py:378
  309.0 1.8 collective-permute-done.28.refs_4_
  313.0 8.1 %soft_weights.2.refs_0_ = bf16[3,1024,1024]{2,1,0:T(8,128)(2,1)} custom-call(f32[6,1024,256]{2,1,0:T(8,128)} %get-tuple-element.43.refs_0_.refs_1_, f32[6,1024,256]{2,1,0:T(8,128)} %get-tuple-element.43.refs_0_.refs_1_, f32[8,1024]{1,0:T(8,128)} %get-tuple-element.44.refs_2_, f32[8,1024]{1,0:T(8,128)} %copy-done.16, f32[8,1024]{1,0:T(8,128)} %copy-done.17, ...), custom_call_target="tpu_custom_call" | custom-call | flops 830472192 | bytes 9437184 | tf_op jit(solution)/shard_map/soft_weights/pallas_call | solution.py:247
  321.1 12.0 %collective-permute-done.32.refs_22_ = bf16[3,640,256]{2,1,0:T(8,128)(2,1)} collective-permute-done((bf16[3,640,256]{2,1,0:T(8,128)(2,1)S(1)}, bf16[3,640,256]{2,1,0:T(8,128)(2,1)}, u32[]{:S(2)}, u32[]{:S(2)}) %collective-permute-start.32) | collective-permute-done | bytes 983072 | tf_op jit(solution)/shard_map/ppermute | solution.py:378
  335.3 8.0 %soft_weights.3.refs_1_ = bf16[3,1024,1024]{2,1,0:T(8,128)(2,1)} custom-call(f32[6,1024,256]{2,1,0:T(8,128)} %get-tuple-element.43.refs_0_.refs_1_, f32[6,1024,256]{2,1,0:T(8,128)} %get-tuple-element.43.refs_0_.refs_1_, f32[8,1024]{1,0:T(8,128)} %get-tuple-element.44.refs_2_, f32[8,1024]{1,0:T(8,128)} %copy-done.16, f32[8,1024]{1,0:T(8,128)} %copy-done.17, ...), custom_call_target="tpu_custom_call" | custom-call | flops 830472192 | bytes 9437184 | tf_op jit(solution)/shard_map/soft_weights/pallas_call | solution.py:247
  343.3 16.5 %collective-permute-done.35 = bf16[3,640,256]{2,1,0:T(8,128)(2,1)} collective-permute-done((bf16[3,640,256]{2,1,0:T(8,128)(2,1)}, bf16[3,640,256]{2,1,0:T(8,128)(2,1)}, u32[]{:S(2)}, u32[]{:S(2)}) %collective-permute-start.35) | collective-permute-done | bytes 983072 | tf_op jit(solution)/shard_map/ppermute | solution.py:473
  362.1 1.8 collective-permute-done.36.refs_25_
  364.8 18.5 %mix_values.1 = bf16[8,4,32,768]{3,2,1,0:T(8,128)(2,1)} custom-call(s32[4]{0:T(128)} %get-tuple-element.61.order_ref, s32[16]{0:T(128)} %iota.27.place_ref, s32[4]{0:T(128)} %get-tuple-element.62.at_ref, bf16[3,1024,1024]{2,1,0:T(8,128)(2,1)} %soft_weights.2.refs_0_, bf16[3,1024,1024]{2,1,0:T(8,128)(2,1)} %soft_weights.3.refs_1_, ...), custom_call_target="tpu_custom_call" | custom-call | flops 5637144576 | bytes 17301504 | tf_op jit(solution)/shard_map/mix_values/pallas_call | solution.py:314
  383.3 41.5 %all_to_all.5.in_ref = bf16[32,32,768]{2,1,0:T(8,128)(2,1)} all-to-all(bf16[32,32,768]{2,1,0:T(8,128)(2,1)} %bitcast.19), channel_id=1, replica_groups=mesh['bal'=8,'seq'=4] {'bal','seq'}, dimensions={0} | all-to-all | bytes 3145728 | tf_op jit(solution)/shard_map/all_to_all | solution.py:519
  424.8 2.7 place_tiles.1
  (130 shorter events, 34.2 us)
Async XLA Ops:
  7.1 87.4 %collective-permute-start.14 = (bf16[6,640,256]{2,1,0:T(8,128)(2,1)}, bf16[6,640,256]{2,1,0:T(8,128)(2,1)S(1)}, u32[]{:S(2)}, u32[]{:S(2)}) collective-permute-start(bf16[6,640,256]{2,1,0:T(8,128)(2,1)} %slice.32), channel_id=1, source_target_pairs={{0,0},{1,4},{2,2},{3,6},{4,1},{5,5},{6,3},{7,7},{8,8},{9,12},{10,1... | collective-permute-start | bytes 5898248 | tf_op jit(solution)/shard_map/ppermute | solution.py:378
  9.3 10.8 %collective-permute-start.1 = (f32[4,2,5120]{2,1,0:T(2,128)S(1)}, f32[4,2,5120]{2,1,0:T(2,128)S(1)}, u32[]{:S(2)}, u32[]{:S(2)}) collective-permute-start(f32[4,2,5120]{2,1,0:T(2,128)S(1)} %bitcast.26), channel_id=1, source_target_pairs={{0,0},{1,4},{2,2},{3,6},{4,1},{5,5},{6,3},{7,7},{8,8},{9,12},{10,1... | collective-permute-start | bytes 491528 | tf_op jit(solution)/shard_map/ppermute | solution.py:378
  10.0 37.7 %collective-permute-start.2 = (bf16[2,16,5120]{2,1,0:T(8,128)(2,1)}, bf16[2,16,5120]{2,1,0:T(8,128)(2,1)S(1)}, u32[]{:S(2)}, u32[]{:S(2)}) collective-permute-start(bf16[2,16,5120]{2,1,0:T(8,128)(2,1)} %get-tuple-element.27), channel_id=1, source_target_pairs={{0,0},{1,4},{2,2},{3,6},{4,1},{5,5},{6,3},{7,7},{8,8},{9,12},{10,1... | collective-permute-start | bytes 983048 | tf_op jit(solution)/shard_map/ppermute | solution.py:378
  11.6 37.4 %collective-permute-start.3 = (bf16[2,16,5120]{2,1,0:T(8,128)(2,1)}, bf16[2,16,5120]{2,1,0:T(8,128)(2,1)S(1)}, u32[]{:S(2)}, u32[]{:S(2)}) collective-permute-start(bf16[2,16,5120]{2,1,0:T(8,128)(2,1)} %get-tuple-element.30), channel_id=1, source_target_pairs={{0,1},{1,5},{2,3},{3,7},{4,8},{5,12},{6,10},{7,14},{8,9},{9,13},{1... | collective-permute-start | bytes 983048 | tf_op jit(solution)/shard_map/ppermute | solution.py:378
  18.5 30.5 %collective-permute-start.4 = (bf16[2,16,5120]{2,1,0:T(8,128)(2,1)}, bf16[2,16,5120]{2,1,0:T(8,128)(2,1)S(1)}, u32[]{:S(2)}, u32[]{:S(2)}) collective-permute-start(bf16[2,16,5120]{2,1,0:T(8,128)(2,1)} %get-tuple-element.31), channel_id=1, source_target_pairs={{0,8},{1,12},{2,10},{3,14},{4,9},{5,13},{6,11},{7,15},{8,16},{9,20... | collective-permute-start | bytes 983048 | tf_op jit(solution)/shard_map/ppermute | solution.py:378
  20.1 54.3 %collective-permute-start.5 = (bf16[2,16,5120]{2,1,0:T(8,128)(2,1)}, bf16[2,16,5120]{2,1,0:T(8,128)(2,1)S(1)}, u32[]{:S(2)}, u32[]{:S(2)}) collective-permute-start(bf16[2,16,5120]{2,1,0:T(8,128)(2,1)} %get-tuple-element.32), channel_id=1, source_target_pairs={{0,9},{1,13},{2,11},{3,15},{4,16},{5,20},{6,18},{7,22},{8,17},{9,2... | collective-permute-start | bytes 983048 | tf_op jit(solution)/shard_map/ppermute | solution.py:378
  47.7 33.6 %collective-permute-start.6 = (bf16[2,16,5120]{2,1,0:T(8,128)(2,1)}, bf16[2,16,5120]{2,1,0:T(8,128)(2,1)}, u32[]{:S(2)}, u32[]{:S(2)}) collective-permute-start(bf16[2,16,5120]{2,1,0:T(8,128)(2,1)} %get-tuple-element.33), channel_id=1, source_target_pairs={{0,16},{1,20},{2,18},{3,22},{4,17},{5,21},{6,19},{7,23},{8,24},{9,... | collective-permute-start | bytes 983048 | tf_op jit(solution)/shard_map/ppermute | solution.py:378
  49.0 32.3 %collective-permute-start.7 = (bf16[2,16,5120]{2,1,0:T(8,128)(2,1)}, bf16[2,16,5120]{2,1,0:T(8,128)(2,1)}, u32[]{:S(2)}, u32[]{:S(2)}) collective-permute-start(bf16[2,16,5120]{2,1,0:T(8,128)(2,1)} %get-tuple-element.34), channel_id=1, source_target_pairs={{0,17},{1,21},{2,19},{3,23},{4,24},{5,28},{6,26},{7,30},{8,25},{9,... | collective-permute-start | bytes 983048 | tf_op jit(solution)/shard_map/ppermute | solution.py:378
  49.1 32.2 %collective-permute-start.8 = (bf16[2,16,5120]{2,1,0:T(8,128)(2,1)}, bf16[2,16,5120]{2,1,0:T(8,128)(2,1)}, u32[]{:S(2)}, u32[]{:S(2)}) collective-permute-start(bf16[2,16,5120]{2,1,0:T(8,128)(2,1)} %get-tuple-element.35), channel_id=1, source_target_pairs={{0,24},{1,28},{2,26},{3,30},{4,25},{5,29},{6,27},{7,31},{8,0},{9,4... | collective-permute-start | bytes 983048 | tf_op jit(solution)/shard_map/ppermute | solution.py:378
  74.4 9.5 %collective-permute-start.9 = (bf16[2,16,5120]{2,1,0:T(8,128)(2,1)}, bf16[2,16,5120]{2,1,0:T(8,128)(2,1)}, u32[]{:S(2)}, u32[]{:S(2)}) collective-permute-start(bf16[2,16,5120]{2,1,0:T(8,128)(2,1)} %get-tuple-element.36), channel_id=1, source_target_pairs={{0,25},{1,29},{2,27},{3,31},{4,0},{5,4},{6,2},{7,6},{8,1},{9,5},{1... | collective-permute-start | bytes 983048 | tf_op jit(solution)/shard_map/ppermute | solution.py:378
  93.0 72.2 %collective-permute-start.11 = (bf16[8,256,640]{2,1,0:T(8,128)(2,1)}, bf16[8,256,640]{2,1,0:T(8,128)(2,1)S(1)}, u32[]{:S(2)}, u32[]{:S(2)}) collective-permute-start(bf16[8,256,640]{2,1,0:T(8,128)(2,1)} %norm_tiles.1.refs_0_.refs_1_.refs_2_.refs_3_.refs_4_.refs_5_), channel_id=1, source_target_pairs={{0,2},{1,3},{2,0},{3,1},{4,6},{5,7},{6,4},{7,5},{8,10},{9,11},{10,... | collective-permute-start | bytes 7864328 | tf_op jit(solution)/shard_map/ppermute | solution.py:378
  94.5 105.4 %collective-permute-start.10 = (bf16[8,256,640]{2,1,0:T(8,128)(2,1)}, bf16[8,256,640]{2,1,0:T(8,128)(2,1)S(1)}, u32[]{:S(2)}, u32[]{:S(2)}) collective-permute-start(bf16[8,256,640]{2,1,0:T(8,128)(2,1)} %norm_tiles.1.refs_0_.refs_1_.refs_2_.refs_3_.refs_4_.refs_5_), channel_id=1, source_target_pairs={{0,4},{1,5},{2,6},{3,7},{4,0},{5,1},{6,2},{7,3},{8,12},{9,13},{10,... | collective-permute-start | bytes 7864328 | tf_op jit(solution)/shard_map/ppermute | solution.py:378
  94.5 103.1 %collective-permute-start.15 = (bf16[6,640,256]{2,1,0:T(8,128)(2,1)S(1)}, bf16[6,640,256]{2,1,0:T(8,128)(2,1)}, u32[]{:S(2)}, u32[]{:S(2)}) collective-permute-start(bf16[6,640,256]{2,1,0:T(8,128)(2,1)S(1)} %collective-permute-done.14.refs_30_), channel_id=1, source_target_pairs={{0,16},{1,17},{2,18},{3,19},{4,20},{5,21},{6,22},{7,23},{8,24},{9,... | collective-permute-start | bytes 5898248 | tf_op jit(solution)/shard_map/ppermute | solution.py:378
  112.5 86.5 %collective-permute-start.19 = (bf16[6,640,256]{2,1,0:T(8,128)(2,1)S(1)}, bf16[6,640,256]{2,1,0:T(8,128)(2,1)}, u32[]{:S(2)}, u32[]{:S(2)}) collective-permute-start(bf16[6,640,256]{2,1,0:T(8,128)(2,1)S(1)} %collective-permute-done.14.refs_30_), channel_id=1, source_target_pairs={{0,8},{1,9},{2,10},{3,11},{4,12},{5,13},{6,14},{7,15},{8,0},{9,1},... | collective-permute-start | bytes 5898248 | tf_op jit(solution)/shard_map/ppermute | solution.py:378
  114.7 105.8 %collective-permute-start.18 = (bf16[6,640,256]{2,1,0:T(8,128)(2,1)S(1)}, bf16[6,640,256]{2,1,0:T(8,128)(2,1)S(1)}, u32[]{:S(2)}, u32[]{:S(2)}) collective-permute-start(bf16[6,640,256]{2,1,0:T(8,128)(2,1)S(1)} %collective-permute-done.14.refs_30_), channel_id=1, source_target_pairs={{0,1},{1,0},{2,3},{3,2},{4,5},{5,4},{6,7},{7,6},{8,9},{9,8},{10,11... | collective-permute-start | bytes 5898248 | tf_op jit(solution)/shard_map/ppermute | solution.py:378
  165.2 54.8 %collective-permute-start.23 = (bf16[3,640,256]{2,1,0:T(8,128)(2,1)S(1)}, bf16[3,640,256]{2,1,0:T(8,128)(2,1)S(1)}, u32[]{:S(2)}, u32[]{:S(2)}) collective-permute-start(bf16[3,640,256]{2,1,0:T(8,128)(2,1)S(1)} %collective-permute-done.17.refs_20_), channel_id=1, source_target_pairs={{0,8},{1,9},{2,10},{3,11},{4,12},{5,13},{6,14},{7,15},{8,0},{9,1},... | collective-permute-start | bytes 2949128 | tf_op jit(solution)/shard_map/ppermute | solution.py:378
  197.6 53.9 %collective-permute-start.21 = (bf16[6,640,256]{2,1,0:T(8,128)(2,1)}, bf16[6,640,256]{2,1,0:T(8,128)(2,1)}, u32[]{:S(2)}, u32[]{:S(2)}) collective-permute-start(bf16[6,640,256]{2,1,0:T(8,128)(2,1)} %collective-permute-done.15.refs_34_), channel_id=1, source_target_pairs={{0,1},{1,0},{2,3},{3,2},{4,5},{5,4},{6,7},{7,6},{8,9},{9,8},{10,11... | collective-permute-start | bytes 5898248 | tf_op jit(solution)/shard_map/ppermute | solution.py:378
  199.0 53.0 %collective-permute-start.20 = (bf16[6,640,256]{2,1,0:T(8,128)(2,1)}, bf16[6,640,256]{2,1,0:T(8,128)(2,1)}, u32[]{:S(2)}, u32[]{:S(2)}) collective-permute-start(bf16[6,640,256]{2,1,0:T(8,128)(2,1)} %collective-permute-done.19.refs_32_), channel_id=1, source_target_pairs={{0,1},{1,0},{2,3},{3,2},{4,5},{5,4},{6,7},{7,6},{8,9},{9,8},{10,11... | collective-permute-start | bytes 5898248 | tf_op jit(solution)/shard_map/ppermute | solution.py:378
  199.9 30.9 %collective-permute-start.12 = (bf16[8,128,640]{2,1,0:T(8,128)(2,1)S(1)}, bf16[8,128,640]{2,1,0:T(8,128)(2,1)}, u32[]{:S(2)}, u32[]{:S(2)}) collective-permute-start(bf16[8,128,640]{2,1,0:T(8,128)(2,1)S(1)} %slice.36), channel_id=1, source_target_pairs={{0,4},{1,5},{2,6},{3,7},{4,0},{5,1},{6,2},{7,3},{8,12},{9,13},{10,... | collective-permute-start | bytes 3932168 | tf_op jit(solution)/shard_map/ppermute | solution.py:378
  220.0 31.5 %collective-permute-start.13 = (bf16[8,128,640]{2,1,0:T(8,128)(2,1)}, bf16[8,128,640]{2,1,0:T(8,128)(2,1)S(1)}, u32[]{:S(2)}, u32[]{:S(2)}) collective-permute-start(bf16[8,128,640]{2,1,0:T(8,128)(2,1)} %slice.37), channel_id=1, source_target_pairs={{0,2},{1,3},{2,0},{3,1},{4,6},{5,7},{6,4},{7,5},{8,10},{9,11},{10,... | collective-permute-start | bytes 3932168 | tf_op jit(solution)/shard_map/ppermute | solution.py:378
  220.5 62.1 %collective-permute-start.16 = (bf16[6,640,256]{2,1,0:T(8,128)(2,1)S(1)}, bf16[6,640,256]{2,1,0:T(8,128)(2,1)}, u32[]{:S(2)}, u32[]{:S(2)}) collective-permute-start(bf16[6,640,256]{2,1,0:T(8,128)(2,1)S(1)} %collective-permute-done.14.refs_30_), channel_id=1, source_target_pairs={{8,16},{9,17},{10,18},{11,19},{12,20},{13,21},{14,22},{15,23},{16,... | collective-permute-start | bytes 5898248 | tf_op jit(solution)/shard_map/ppermute | solution.py:473
  230.7 51.9 %collective-permute-start.25 = (bf16[6,640,256]{2,1,0:T(8,128)(2,1)}, bf16[6,640,256]{2,1,0:T(8,128)(2,1)}, u32[]{:S(2)}, u32[]{:S(2)}) collective-permute-start(bf16[6,640,256]{2,1,0:T(8,128)(2,1)} %collective-permute-done.15.refs_34_), channel_id=1, source_target_pairs={{8,0},{9,1},{10,2},{11,3},{12,4},{13,5},{14,6},{15,7},{16,24},{17,... | collective-permute-start | bytes 5898248 | tf_op jit(solution)/shard_map/ppermute | solution.py:473
  251.4 21.5 %collective-permute-start.22 = (bf16[3,640,256]{2,1,0:T(8,128)(2,1)}, bf16[3,640,256]{2,1,0:T(8,128)(2,1)}, u32[]{:S(2)}, u32[]{:S(2)}) collective-permute-start(bf16[3,640,256]{2,1,0:T(8,128)(2,1)} %copy-done.7), channel_id=1, source_target_pairs={{0,1},{1,0},{2,3},{3,2},{4,5},{5,4},{6,7},{7,6},{8,9},{9,8},{10,11... | collective-permute-start | bytes 2949128 | tf_op jit(solution)/shard_map/ppermute | solution.py:378
  251.5 21.5 %collective-permute-start.24 = (bf16[3,640,256]{2,1,0:T(8,128)(2,1)}, bf16[3,640,256]{2,1,0:T(8,128)(2,1)}, u32[]{:S(2)}, u32[]{:S(2)}) collective-permute-start(bf16[3,640,256]{2,1,0:T(8,128)(2,1)} %copy-done.9), channel_id=1, source_target_pairs={{0,1},{1,0},{2,3},{3,2},{4,5},{5,4},{6,7},{7,6},{8,9},{9,8},{10,11... | collective-permute-start | bytes 2949128 | tf_op jit(solution)/shard_map/ppermute | solution.py:378
  285.4 21.7 %collective-permute-start.30 = (f32[6,128]{1,0:T(8,128)S(1)}, f32[6,128]{1,0:T(8,128)S(1)}, u32[]{:S(2)}, u32[]{:S(2)}) collective-permute-start(f32[6,128]{1,0:T(8,128)S(1)} %copy-done.23), channel_id=1, source_target_pairs={{0,0},{1,4},{2,2},{3,6},{4,1},{5,5},{6,3},{7,7},{8,8},{9,12},{10,1... | collective-permute-start | bytes 9224 | tf_op jit(solution)/shard_map/ppermute | solution.py:378
  286.1 22.2 %collective-permute-start.31 = (f32[6,128]{1,0:T(8,128)S(1)}, f32[6,128]{1,0:T(8,128)S(1)}, u32[]{:S(2)}, u32[]{:S(2)}) collective-permute-start(f32[6,128]{1,0:T(8,128)S(1)} %copy-done.24), channel_id=1, source_target_pairs={{0,0},{1,4},{2,2},{3,6},{4,1},{5,5},{6,3},{7,7},{8,8},{9,12},{10,1... | collective-permute-start | bytes 9224 | tf_op jit(solution)/shard_map/ppermute | solution.py:378
  287.6 45.5 %collective-permute-start.32 = (bf16[3,640,256]{2,1,0:T(8,128)(2,1)S(1)}, bf16[3,640,256]{2,1,0:T(8,128)(2,1)}, u32[]{:S(2)}, u32[]{:S(2)}) collective-permute-start(bf16[3,640,256]{2,1,0:T(8,128)(2,1)S(1)} %copy-done.8), channel_id=1, source_target_pairs={{0,16},{1,17},{2,18},{3,19},{4,20},{5,21},{6,22},{7,23},{8,24},{9,... | collective-permute-start | bytes 2949128 | tf_op jit(solution)/shard_map/ppermute | solution.py:378
  302.2 6.7 %collective-permute-start.27 = (f32[8,1024]{1,0:T(8,128)}, f32[8,1024]{1,0:T(8,128)S(1)}, u32[]{:S(2)}, u32[]{:S(2)}) collective-permute-start(f32[8,1024]{1,0:T(8,128)} %get-tuple-element.44.refs_2_), channel_id=1, source_target_pairs={{0,4},{1,5},{2,6},{3,7},{4,0},{5,1},{6,2},{7,3},{8,12},{9,13},{10,... | collective-permute-start | bytes 98312 | tf_op jit(solution)/shard_map/ppermute | solution.py:378
  307.2 5.0 %collective-permute-start.29 = (f32[8,1024]{1,0:T(8,128)}, f32[8,1024]{1,0:T(8,128)S(1)}, u32[]{:S(2)}, u32[]{:S(2)}) collective-permute-start(f32[8,1024]{1,0:T(8,128)} %get-tuple-element.44.refs_2_), channel_id=1, source_target_pairs={{0,6},{1,7},{2,4},{3,5},{4,2},{5,3},{6,0},{7,1},{8,14},{9,15},{10,... | collective-permute-start | bytes 98312 | tf_op jit(solution)/shard_map/ppermute | solution.py:378
  333.1 10.2 %collective-permute-start.34 = (bf16[3,640,256]{2,1,0:T(8,128)(2,1)S(1)}, bf16[3,640,256]{2,1,0:T(8,128)(2,1)S(1)}, u32[]{:S(2)}, u32[]{:S(2)}) collective-permute-start(bf16[3,640,256]{2,1,0:T(8,128)(2,1)S(1)} %copy-done.8), channel_id=1, source_target_pairs={{8,16},{9,17},{10,18},{11,19},{12,20},{13,21},{14,22},{15,23},{16,... | collective-permute-start | bytes 2949128 | tf_op jit(solution)/shard_map/ppermute | solution.py:473
  333.8 26.0 %collective-permute-start.35 = (bf16[3,640,256]{2,1,0:T(8,128)(2,1)}, bf16[3,640,256]{2,1,0:T(8,128)(2,1)}, u32[]{:S(2)}, u32[]{:S(2)}) collective-permute-start(bf16[3,640,256]{2,1,0:T(8,128)(2,1)} %collective-permute-done.32.refs_22_), channel_id=1, source_target_pairs={{8,0},{9,1},{10,2},{11,3},{12,4},{13,5},{14,6},{15,7},{16,24},{17,... | collective-permute-start | bytes 2949128 | tf_op jit(solution)/shard_map/ppermute | solution.py:473
  335.1 27.0 %collective-permute-start.33 = (bf16[3,640,256]{2,1,0:T(8,128)(2,1)}, bf16[3,640,256]{2,1,0:T(8,128)(2,1)}, u32[]{:S(2)}, u32[]{:S(2)}) collective-permute-start(bf16[3,640,256]{2,1,0:T(8,128)(2,1)} %collective-permute-done.32.refs_22_), channel_id=1, source_target_pairs={{0,1},{1,0},{2,3},{3,2},{4,5},{5,4},{6,7},{7,6},{8,9},{9,8},{10,11... | collective-permute-start | bytes 2949128 | tf_op jit(solution)/shard_map/ppermute | solution.py:378
  (30 other events, 562.8 us)

commit v4 on v3

--- a/solution.py
+++ b/solution.py
@@ -450,20 +450,6 @@
             got.append(ring(got[-1]))
         return got
 
-    def far_plane(got, *earlier):
-        if planes != 4:
-            return got
-        return [*got, send(after(got[0], *earlier), lambda z, x, y, c: (z ^ 2, x, y, c))]
-
-    def end_planes(got, *earlier):
-        if planes == 4:
-            own, _, two = got
-            return [send_some(after(own, two, *earlier), {1: 2, 2: 1}), send_some(after(two, *earlier), {1: 0, 2: 3})]
-        return [ring(after(got[-1], *earlier))]
-
-    def last_plane(ends, *earlier):
-        return sum(ends[1:], after(ends[0], *earlier))
-
     def send_some(value, hops):
         pairs = []
         for b in range(groups):
@@ -472,8 +458,17 @@
                     pairs.append((b * n + s, (hops[b // 2] * 2 + b % 2) * n + s))
         return lax.ppermute(value, AXES, pairs)
 
+    def cross(value):
+        return send_some(value, {1: 2, 2: 1})
+
+    def outward(value):
+        return send_some(value, {1: 0, 2: 3})
+
     def plane_at(step):
-        return z ^ step if planes == 4 else (z - step) % planes
+        if planes != 4:
+            return (z - step) % planes
+        low = z < 2
+        return [z, z ^ 1, jnp.where(low, 2, 1), jnp.where(low, 3, 0)][step]
 
     def blocks_of(own, steps):
         blocks, at = [], []
@@ -483,22 +478,28 @@
         return blocks, jnp.stack(at).astype(jnp.int32)
 
     qk_own = near_planes(qk_own[0])
-    qk_own = far_plane(qk_own, *arrived)
     v_first = swap(v_columns)
     v_own = near_planes(after(v_first, *arrived))
-    qk_ends = end_planes(qk_own)
+    if planes == 4:
+        crossed = cross(after(qk_own[0], *arrived))
+        crossed_next = cross(after(qk_own[1], crossed))
+        qk_own.append(crossed + outward(crossed))
+        passed = outward(crossed_next)
+        v_crossed = cross(after(v_own[0], crossed_next))
+        v_crossed_next = cross(after(v_own[1], v_crossed))
+        v_passed = [outward(after(v_crossed, passed)), outward(after(v_crossed_next, passed))]
 
     blocks, at = blocks_of(qk_own, range(planes - 1))
     qk, *_ = project(pieces, blocks, at, None, False)
+    qk_own.append(after(crossed_next, qk) + passed if planes == 4 else ring(after(qk_own[-1], qk)))
+    blocks, at = blocks_of(qk_own, [planes - 1])
+    qk, sums = project(pieces, blocks, at, qk, True)
     split = max(planes - 2, 1)
     blocks, at = blocks_of(v_own, range(split))
-    blocks[0] = after(blocks[0], qk)
+    blocks[0] = after(blocks[0], sums)
     values, *_ = project(pieces, blocks, at, None, False)
-    v_own = far_plane(v_own, *qk_ends)
-    qk_own.append(last_plane(qk_ends, values))
-    blocks, at = blocks_of(qk_own, [planes - 1])
-    qk, sums = project(pieces, blocks, at, qk, True)
-    partial_sums = [sums, along_x(sums)]
+    partial_sums = [sums]
+    partial_sums.append(along_x(sums))
     for py in range(1, lines):
         partial_sums.append(along_y(sums, py))
         partial_sums.append(send(sums, lambda z, x, y, c: (z, x ^ 1, (y - py) % lines, c)))
@@ -506,14 +507,12 @@
     bias = jnp.where(tile_mask.T, 0.0, mask_bias).astype(jnp.bfloat16)
     bias = jnp.pad(bias, ((0, 0), (0, dim - TILES_OWN)))
     bias = jnp.tile(jnp.repeat(bias, piece, axis=0), (n, 1))
-    parts = 2 if heads % 2 == 0 else 1
-    weights = []
-    for i in range(parts):
-        part = soft_weights(qk, partial_sums, gains, bias, features, i * heads // parts, heads // parts)
-        weights.append(part)
-        if i == 0:
-            v_ends = end_planes(v_own, weights[0])
-    v_own.append(last_plane(v_ends, weights[-1]))
+    weights = [soft_weights(qk, partial_sums, gains, after(bias, values), features, 0, heads)]
+    if planes == 4:
+        v_own.append(after(v_crossed, weights[0]) + v_passed[0])
+        v_own.append(after(v_crossed_next, weights[0]) + v_passed[1])
+    else:
+        v_own.append(ring(after(v_own[-1], sums)))
     blocks, at = blocks_of(v_own, range(split, planes))
     mixed = mix_values(weights, values, pieces, blocks, at, order, place, groups, capacity, piece)
     returned = lax.all_to_all(

time: 428 us -> 406 us (0.949)
  starting transfers between devices: 146 us -> 101 us
  blocking collectives: 41.5 us -> 50.9 us
  waiting for transfers between devices: 130 us -> 139 us
  other arithmetic: 8.18 us -> 13.8 us
    ppermute x33 -> x31, starting transfers between devices: 141 us -> 88.7 us  [send(): return lax.ppermute(value, AXES, pairs)]
    ppermute x4 -> x8, waiting for transfers between devices: 16.5 us -> 55.8 us  [send_some(): return lax.ppermute(value, AXES, pairs)]
    ppermute x33 -> x31, waiting for transfers between devices: 113 us -> 83.3 us  [send(): return lax.ppermute(value, AXES, pairs)]
    all_to_all x1, blocking collectives: 41.5 us -> 50.9 us  [transposed(): lax.all_to_all(mixed.reshape(groups * n, capacity * piece, heads * dim),...]
    ppermute x4 -> x8, starting transfers between devices: 5.28 us -> 12.3 us  [send_some(): return lax.ppermute(value, AXES, pairs)]
    add x2 -> x4, other arithmetic: 4.11 us -> 9.54 us  [the longest x1 3.41 us: transposed(): qk_own.append(crossed + outward(crossed))]
    pallas_call x2 -> x1, Pallas kernels: 16.1 us -> 13.3 us  [soft_weights(): pl.pallas_call(body, out_shape=jax.ShapeDtypeStruct((count, total, total)...]
  transfers between devices with their start and end apart: 37 -> 39, of which waited for: 15 -> 11; matrix products, arithmetic and copies ran while one was open for 2% -> 5% of each run, Pallas kernels for 16% -> 16%
where the time goes in v4:
time: 406 us; the launch traced here: 405 us
  waiting for transfers between devices  139 us (34%)
  starting transfers between devices  101 us (25%)
  Pallas kernels  88.7 us (22%)
  blocking collectives  50.9 us (13%)
  other arithmetic  13.8 us (3%)
  local copies, waits for them, and re-layouts  10.5 us (3%)
    ppermute x31, starting transfers between devices, send(): return lax.ppermute(value, AXES, pairs)  88.7 us
    ppermute x31, waiting for transfers between devices, send(): return lax.ppermute(value, AXES, pairs)  83.3 us
    ppermute x8, waiting for transfers between devices, send_some(): return lax.ppermute(value, AXES, pairs)  55.8 us
    all_to_all x1, blocking collectives, transposed(): lax.all_to_all(mixed.reshape(groups * n, capacity * piece, heads * dim),...  50.9 us
    pallas_call x3, Pallas kernels, project(): pl.pallas_call(body, out_shape=out_shape, grid_spec=pltpu.PrefetchScalarG...  42.8 us
    pallas_call x1, Pallas kernels, mix_values(): pl.pallas_call(body, out_shape=jax.ShapeDtypeStruct((groups, n, capacity...  17.9 us
    pallas_call x1, Pallas kernels, soft_weights(): pl.pallas_call(body, out_shape=jax.ShapeDtypeStruct((count, total, total)...  13.3 us
    ppermute x8, starting transfers between devices, send_some(): return lax.ppermute(value, AXES, pairs)  12.3 us
  transfers between devices with their start and end apart: 39, of which 11 were waited for; matrix products, arithmetic and copies ran while one was open for 5% of the time, Pallas kernels for 16%

profile of v4, /device:TPU:0, one launch (start us, length us, event | category | flops | bytes accessed | tf_op | source)
XLA Modules:
  0.0 404.5 jit_solution(9691580685214629005)
XLA Ops:
  0.6 3.5 pick_tiles.1
  7.6 5.5 %collective-permute-start.3 = (bf16[2,16,5120]{2,1,0:T(8,128)(2,1)S(1)}, bf16[2,16,5120]{2,1,0:T(8,128)(2,1)S(1)}, u32[]{:S(2)}, u32[]{:S(2)}) collective-permute-start(bf16[2,16,5120]{2,1,0:T(8,128)(2,1)S(1)} %copy-done.33), channel_id=1, source_target_pairs={{0,1},{1,5},{2,3},{3,7},{4,8},{5,12},{6,10},{7,14},{8,9},{9,13},{1... | collective-permute-start | bytes 983048 | tf_op jit(solution)/shard_map/ppermute | solution.py:378
  14.7 2.4 collective-permute-start.5
  18.4 8.0 %collective-permute-done.3.rest_1_ = bf16[2,16,5120]{2,1,0:T(8,128)(2,1)S(1)} collective-permute-done((bf16[2,16,5120]{2,1,0:T(8,128)(2,1)S(1)}, bf16[2,16,5120]{2,1,0:T(8,128)(2,1)S(1)}, u32[]{:S(2)}, u32[]{:S(2)}) %collective-permute-start.3) | collective-permute-done | bytes 327712 | tf_op jit(solution)/shard_map/ppermute | solution.py:378
  26.4 23.3 %collective-permute-start.7 = (bf16[2,16,5120]{2,1,0:T(8,128)(2,1)S(1)}, bf16[2,16,5120]{2,1,0:T(8,128)(2,1)S(1)}, u32[]{:S(2)}, u32[]{:S(2)}) collective-permute-start(bf16[2,16,5120]{2,1,0:T(8,128)(2,1)S(1)} %copy-done.29), channel_id=1, source_target_pairs={{0,17},{1,21},{2,19},{3,23},{4,24},{5,28},{6,26},{7,30},{8,25},{9,... | collective-permute-start | bytes 983048 | tf_op jit(solution)/shard_map/ppermute | solution.py:378
  49.7 3.2 collective-permute-start.8
  53.0 11.7 %collective-permute-done.7.rest_5_ = bf16[2,16,5120]{2,1,0:T(8,128)(2,1)S(1)} collective-permute-done((bf16[2,16,5120]{2,1,0:T(8,128)(2,1)S(1)}, bf16[2,16,5120]{2,1,0:T(8,128)(2,1)S(1)}, u32[]{:S(2)}, u32[]{:S(2)}) %collective-permute-start.7) | collective-permute-done | bytes 327712 | tf_op jit(solution)/shard_map/ppermute | solution.py:378
  64.9 7.0 %collective-permute-done.9.rest_7_ = bf16[2,16,5120]{2,1,0:T(8,128)(2,1)S(1)} collective-permute-done((bf16[2,16,5120]{2,1,0:T(8,128)(2,1)S(1)}, bf16[2,16,5120]{2,1,0:T(8,128)(2,1)S(1)}, u32[]{:S(2)}, u32[]{:S(2)}) %collective-permute-start.9) | collective-permute-done | bytes 327712 | tf_op jit(solution)/shard_map/ppermute | solution.py:378
  71.9 2.0 collective-permute-start.16
  76.7 11.8 %collective-permute-start.15 = (bf16[6,640,256]{2,1,0:T(8,128)(2,1)S(1)}, bf16[6,640,256]{2,1,0:T(8,128)(2,1)}, u32[]{:S(2)}, u32[]{:S(2)}) collective-permute-start(bf16[6,640,256]{2,1,0:T(8,128)(2,1)S(1)} %collective-permute-done.14.refs_30_), channel_id=1, source_target_pairs={{0,8},{1,9},{2,10},{3,11},{4,12},{5,13},{6,14},{7,15},{8,0},{9,1},... | collective-permute-start | bytes 5898248 | tf_op jit(solution)/shard_map/ppermute | solution.py:378
  89.7 8.5 %norm_tiles.1.refs_0_.refs_1_.refs_2_.refs_3_.refs_4_.refs_5_ = bf16[8,256,640]{2,1,0:T(8,128)(2,1)} custom-call(s32[16]{0:T(128)} %broadcast_maximum_fusion.1.member_ref, s32[16]{0:T(128)} %iota.28.place_ref, s32[2]{0:T(128)} %pad_add_fusion.3.ids_ref, f32[4,2,5120]{2,1,0:T(2,128)} %copy-done.20, bf16[2,16,5120]{2,1,0:T(8,128)(2,1)} %copy-done.12, ...), custom_call_target="tpu_custom_call" | custom-call | flops 15728640 | bytes 5242880 | tf_op jit(solution)/shard_map/norm_tiles/pallas_call | solution.py:117
  99.7 8.9 %collective-permute-start.10 = (bf16[8,256,640]{2,1,0:T(8,128)(2,1)}, bf16[8,256,640]{2,1,0:T(8,128)(2,1)S(1)}, u32[]{:S(2)}, u32[]{:S(2)}) collective-permute-start(bf16[8,256,640]{2,1,0:T(8,128)(2,1)} %norm_tiles.1.refs_0_.refs_1_.refs_2_.refs_3_.refs_4_.refs_5_), channel_id=1, source_target_pairs={{0,4},{1,5},{2,6},{3,7},{4,0},{5,1},{6,2},{7,3},{8,12},{9,13},{10,... | collective-permute-start | bytes 7864328 | tf_op jit(solution)/shard_map/ppermute | solution.py:378
  110.0 15.3 %collective-permute-done.15.refs_32_ = bf16[6,640,256]{2,1,0:T(8,128)(2,1)} collective-permute-done((bf16[6,640,256]{2,1,0:T(8,128)(2,1)S(1)}, bf16[6,640,256]{2,1,0:T(8,128)(2,1)}, u32[]{:S(2)}, u32[]{:S(2)}) %collective-permute-start.15) | collective-permute-done | bytes 1966112 | tf_op jit(solution)/shard_map/ppermute | solution.py:378
  125.3 2.0 collective-permute-start.17
  128.7 44.4 %collective-permute-done.20 = bf16[6,640,256]{2,1,0:T(8,128)(2,1)S(1)} collective-permute-done((bf16[6,640,256]{2,1,0:T(8,128)(2,1)}, bf16[6,640,256]{2,1,0:T(8,128)(2,1)S(1)}, u32[]{:S(2)}, u32[]{:S(2)}) %collective-permute-start.20) | collective-permute-done | bytes 1966112 | tf_op jit(solution)/shard_map/ppermute | solution.py:459
  173.9 3.4 add.133.refs_34_
  177.3 5.9 %collective-permute-start.19 = (bf16[6,640,256]{2,1,0:T(8,128)(2,1)}, bf16[6,640,256]{2,1,0:T(8,128)(2,1)}, u32[]{:S(2)}, u32[]{:S(2)}) collective-permute-start(bf16[6,640,256]{2,1,0:T(8,128)(2,1)} %collective-permute-done.15.refs_32_), channel_id=1, source_target_pairs={{0,1},{1,0},{2,3},{3,2},{4,5},{5,4},{6,7},{7,6},{8,9},{9,8},{10,11... | collective-permute-start | bytes 5898248 | tf_op jit(solution)/shard_map/ppermute | solution.py:378
  185.8 7.3 %collective-permute-start.12 = (bf16[8,128,640]{2,1,0:T(8,128)(2,1)}, bf16[8,128,640]{2,1,0:T(8,128)(2,1)S(1)}, u32[]{:S(2)}, u32[]{:S(2)}) collective-permute-start(bf16[8,128,640]{2,1,0:T(8,128)(2,1)} %slice.36), channel_id=1, source_target_pairs={{0,4},{1,5},{2,6},{3,7},{4,0},{5,1},{6,2},{7,3},{8,12},{9,13},{10,... | collective-permute-start | bytes 3932168 | tf_op jit(solution)/shard_map/ppermute | solution.py:378
  197.9 24.5 %collective-permute-done.12.refs_18_.refs_19_.refs_20_.refs_21_.refs_22_.refs_23_.refs_6_.refs_7_.refs_12_.refs_13_.refs_14_.refs_15_.refs_16_ = bf16[8,128,640]{2,1,0:T(8,128)(2,1)S(1)} collective-permute-done((bf16[8,128,640]{2,1,0:T(8,128)(2,1)}, bf16[8,128,640]{2,1,0:T(8,128)(2,1)S(1)}, u32[]{:S(2)}, u32[]{:S(2)}) %collective-permute-start.12) | collective-permute-done | bytes 1310752 | tf_op jit(solution)/shard_map/ppermute | solution.py:378
  225.4 20.5 %project.3.refs_12_ = f32[6,1024,256]{2,1,0:T(8,128)} custom-call(s32[6]{0:T(128)} %stack.83.at_ref, bf16[8,256,640]{2,1,0:T(8,128)(2,1)} %norm_tiles.1.refs_0_.refs_1_.refs_2_.refs_3_.refs_4_.refs_5_, bf16[8,256,640]{2,1,0:T(8,128)(2,1)} %norm_tiles.1.refs_0_.refs_1_.refs_2_.refs_3_.refs_4_.refs_5_, ...), custom_call_target="tpu_custom_call" | custom-call | flops 12079595520 | bytes 32243712 | tf_op jit(solution)/shard_map/project/pallas_call | solution.py:187
  246.0 2.7 add.134.refs_10_
  248.7 13.4 %collective-permute-done.31.refs_22_ = bf16[3,640,256]{2,1,0:T(8,128)(2,1)} collective-permute-done((bf16[3,640,256]{2,1,0:T(8,128)(2,1)}, bf16[3,640,256]{2,1,0:T(8,128)(2,1)}, u32[]{:S(2)}, u32[]{:S(2)}) %collective-permute-start.31) | collective-permute-done | bytes 983072 | tf_op jit(solution)/shard_map/ppermute | solution.py:378
  265.7 3.1 collective-permute-start.30
  272.7 12.7 %project.4 = (f32[6,1024,256]{2,1,0:T(8,128)}, f32[8,1024]{1,0:T(8,128)}) custom-call(s32[2]{0:T(128)} %pad_add_fusion.2.at_ref, bf16[8,256,640]{2,1,0:T(8,128)(2,1)} %norm_tiles.1.refs_0_.refs_1_.refs_2_.refs_3_.refs_4_.refs_5_, bf16[8,256,640]{2,1,0:T(8,128)(2,1)} %norm_tiles.1.refs_0_.refs_1_.refs_2_.refs_3_.refs_4_.refs_5_, ...), custom_call_target="tpu_custom_call", output_to_operand_aliasing={{0}: (13, {})} | custom-call | flops 4026531840 | bytes 19136512 | tf_op jit(solution)/shard_map/project/pallas_call | solution.py:187
  285.5 3.4 collective-permute-start.24
  290.5 9.6 %project.5.refs_25_ = f32[3,1024,256]{2,1,0:T(8,128)} custom-call(s32[4]{0:T(128)} %pad_add_fusion.4.at_ref, bf16[8,256,640]{2,1,0:T(8,128)(2,1)} %norm_tiles.1.refs_0_.refs_1_.refs_2_.refs_3_.refs_4_.refs_5_, bf16[8,256,640]{2,1,0:T(8,128)(2,1)} %norm_tiles.1.refs_0_.refs_1_.refs_2_.refs_3_.refs_4_.refs_5_, ...), custom_call_target="tpu_custom_call" | custom-call | flops 4026531840 | bytes 15466496 | tf_op jit(solution)/shard_map/project/pallas_call | solution.py:187
  301.6 13.3 %soft_weights.1.refs_0_ = bf16[6,1024,1024]{2,1,0:T(8,128)(2,1)} custom-call(f32[6,1024,256]{2,1,0:T(8,128)} %get-tuple-element.44.refs_0_.refs_1_, f32[6,1024,256]{2,1,0:T(8,128)} %get-tuple-element.44.refs_0_.refs_1_, f32[8,1024]{1,0:T(8,128)} %get-tuple-element.45.refs_2_, f32[8,1024]{1,0:T(8,128)} %copy-done.21, f32[8,1024]{1,0:T(8,128)} %copy-done.22, ...), custom_call_target="tpu_custom_call" | custom-call | flops 1660944384 | bytes 18874368 | tf_op jit(solution)/shard_map/soft_weights/pallas_call | solution.py:247
  316.7 11.3 %collective-permute-done.34 = bf16[3,640,256]{2,1,0:T(8,128)(2,1)} collective-permute-done((bf16[3,640,256]{2,1,0:T(8,128)(2,1)}, bf16[3,640,256]{2,1,0:T(8,128)(2,1)}, u32[]{:S(2)}, u32[]{:S(2)}) %collective-permute-start.34) | collective-permute-done | bytes 983072 | tf_op jit(solution)/shard_map/ppermute | solution.py:459
  330.6 1.9 collective-permute-done.35.refs_22_
  333.0 17.9 %mix_values.1 = bf16[8,4,32,768]{3,2,1,0:T(8,128)(2,1)} custom-call(s32[4]{0:T(128)} %get-tuple-element.67.order_ref, s32[16]{0:T(128)} %iota.27.place_ref, s32[4]{0:T(128)} %get-tuple-element.68.at_ref, bf16[6,1024,1024]{2,1,0:T(8,128)(2,1)} %soft_weights.1.refs_0_, bf16[8,256,640]{2,1,0:T(8,128)(2,1)} %norm_tiles.1.refs_0_.refs_1_.refs_2_.refs_3_.refs_4_.refs_5_, ...), custom_call_target="tpu_custom_call" | custom-call | flops 5637144576 | bytes 17301504 | tf_op jit(solution)/shard_map/mix_values/pallas_call | solution.py:314
  351.0 50.9 %all_to_all.5.in_ref = bf16[32,32,768]{2,1,0:T(8,128)(2,1)} all-to-all(bf16[32,32,768]{2,1,0:T(8,128)(2,1)} %bitcast.19), channel_id=1, replica_groups=mesh['bal'=8,'seq'=4] {'bal','seq'}, dimensions={0} | all-to-all | bytes 3145728 | tf_op jit(solution)/shard_map/all_to_all | solution.py:518
  401.8 2.7 place_tiles.1
  (159 shorter events, 41.8 us)
Async XLA Ops:
  6.1 65.8 %collective-permute-start.14 = (bf16[6,640,256]{2,1,0:T(8,128)(2,1)S(1)}, bf16[6,640,256]{2,1,0:T(8,128)(2,1)S(1)}, u32[]{:S(2)}, u32[]{:S(2)}) collective-permute-start(bf16[6,640,256]{2,1,0:T(8,128)(2,1)S(1)} %slice.32), channel_id=1, source_target_pairs={{0,0},{1,4},{2,2},{3,6},{4,1},{5,5},{6,3},{7,7},{8,8},{9,12},{10,1... | collective-permute-start | bytes 5898248 | tf_op jit(solution)/shard_map/ppermute | solution.py:378
  7.6 18.8 %collective-permute-start.3 = (bf16[2,16,5120]{2,1,0:T(8,128)(2,1)S(1)}, bf16[2,16,5120]{2,1,0:T(8,128)(2,1)S(1)}, u32[]{:S(2)}, u32[]{:S(2)}) collective-permute-start(bf16[2,16,5120]{2,1,0:T(8,128)(2,1)S(1)} %copy-done.33), channel_id=1, source_target_pairs={{0,1},{1,5},{2,3},{3,7},{4,8},{5,12},{6,10},{7,14},{8,9},{9,13},{1... | collective-permute-start | bytes 983048 | tf_op jit(solution)/shard_map/ppermute | solution.py:378
  13.1 36.6 %collective-permute-start.4 = (bf16[2,16,5120]{2,1,0:T(8,128)(2,1)S(1)}, bf16[2,16,5120]{2,1,0:T(8,128)(2,1)S(1)}, u32[]{:S(2)}, u32[]{:S(2)}) collective-permute-start(bf16[2,16,5120]{2,1,0:T(8,128)(2,1)S(1)} %copy-done.32), channel_id=1, source_target_pairs={{0,8},{1,12},{2,10},{3,14},{4,9},{5,13},{6,11},{7,15},{8,16},{9,20... | collective-permute-start | bytes 983048 | tf_op jit(solution)/shard_map/ppermute | solution.py:378
  14.7 38.3 %collective-permute-start.5 = (bf16[2,16,5120]{2,1,0:T(8,128)(2,1)S(1)}, bf16[2,16,5120]{2,1,0:T(8,128)(2,1)S(1)}, u32[]{:S(2)}, u32[]{:S(2)}) collective-permute-start(bf16[2,16,5120]{2,1,0:T(8,128)(2,1)S(1)} %copy-done.31), channel_id=1, source_target_pairs={{0,9},{1,13},{2,11},{3,15},{4,16},{5,20},{6,18},{7,22},{8,17},{9,2... | collective-permute-start | bytes 983048 | tf_op jit(solution)/shard_map/ppermute | solution.py:378
  17.1 35.9 %collective-permute-start.6 = (bf16[2,16,5120]{2,1,0:T(8,128)(2,1)S(1)}, bf16[2,16,5120]{2,1,0:T(8,128)(2,1)S(1)}, u32[]{:S(2)}, u32[]{:S(2)}) collective-permute-start(bf16[2,16,5120]{2,1,0:T(8,128)(2,1)S(1)} %copy-done.30), channel_id=1, source_target_pairs={{0,16},{1,20},{2,18},{3,22},{4,17},{5,21},{6,19},{7,23},{8,24},{9,... | collective-permute-start | bytes 983048 | tf_op jit(solution)/shard_map/ppermute | solution.py:378
  26.4 38.3 %collective-permute-start.7 = (bf16[2,16,5120]{2,1,0:T(8,128)(2,1)S(1)}, bf16[2,16,5120]{2,1,0:T(8,128)(2,1)S(1)}, u32[]{:S(2)}, u32[]{:S(2)}) collective-permute-start(bf16[2,16,5120]{2,1,0:T(8,128)(2,1)S(1)} %copy-done.29), channel_id=1, source_target_pairs={{0,17},{1,21},{2,19},{3,23},{4,24},{5,28},{6,26},{7,30},{8,25},{9,... | collective-permute-start | bytes 983048 | tf_op jit(solution)/shard_map/ppermute | solution.py:378
  49.7 15.2 %collective-permute-start.8 = (bf16[2,16,5120]{2,1,0:T(8,128)(2,1)S(1)}, bf16[2,16,5120]{2,1,0:T(8,128)(2,1)S(1)}, u32[]{:S(2)}, u32[]{:S(2)}) collective-permute-start(bf16[2,16,5120]{2,1,0:T(8,128)(2,1)S(1)} %copy-done.28), channel_id=1, source_target_pairs={{0,24},{1,28},{2,26},{3,30},{4,25},{5,29},{6,27},{7,31},{8,0},{9,4... | collective-permute-start | bytes 983048 | tf_op jit(solution)/shard_map/ppermute | solution.py:378
  52.9 18.9 %collective-permute-start.9 = (bf16[2,16,5120]{2,1,0:T(8,128)(2,1)S(1)}, bf16[2,16,5120]{2,1,0:T(8,128)(2,1)S(1)}, u32[]{:S(2)}, u32[]{:S(2)}) collective-permute-start(bf16[2,16,5120]{2,1,0:T(8,128)(2,1)S(1)} %copy-done.27), channel_id=1, source_target_pairs={{0,25},{1,29},{2,27},{3,31},{4,0},{5,4},{6,2},{7,6},{8,1},{9,5},{1... | collective-permute-start | bytes 983048 | tf_op jit(solution)/shard_map/ppermute | solution.py:378
  71.9 36.7 %collective-permute-start.16 = (bf16[6,640,256]{2,1,0:T(8,128)(2,1)S(1)}, bf16[6,640,256]{2,1,0:T(8,128)(2,1)}, u32[]{:S(2)}, u32[]{:S(2)}) collective-permute-start(bf16[6,640,256]{2,1,0:T(8,128)(2,1)S(1)} %collective-permute-done.14.refs_30_), channel_id=1, source_target_pairs={{8,16},{9,17},{10,18},{11,19},{12,20},{13,21},{14,22},{15,23},{16,... | collective-permute-start | bytes 5898248 | tf_op jit(solution)/shard_map/ppermute | solution.py:459
  73.9 15.1 %collective-permute-start.1 = (f32[4,2,5120]{2,1,0:T(2,128)}, f32[4,2,5120]{2,1,0:T(2,128)S(1)}, u32[]{:S(2)}, u32[]{:S(2)}) collective-permute-start(f32[4,2,5120]{2,1,0:T(2,128)} %bitcast.11), channel_id=1, source_target_pairs={{0,0},{1,4},{2,2},{3,6},{4,1},{5,5},{6,3},{7,7},{8,8},{9,12},{10,1... | collective-permute-start | bytes 491528 | tf_op jit(solution)/shard_map/ppermute | solution.py:378
  76.7 48.6 %collective-permute-start.15 = (bf16[6,640,256]{2,1,0:T(8,128)(2,1)S(1)}, bf16[6,640,256]{2,1,0:T(8,128)(2,1)}, u32[]{:S(2)}, u32[]{:S(2)}) collective-permute-start(bf16[6,640,256]{2,1,0:T(8,128)(2,1)S(1)} %collective-permute-done.14.refs_30_), channel_id=1, source_target_pairs={{0,8},{1,9},{2,10},{3,11},{4,12},{5,13},{6,14},{7,15},{8,0},{9,1},... | collective-permute-start | bytes 5898248 | tf_op jit(solution)/shard_map/ppermute | solution.py:378
  98.2 79.1 %collective-permute-start.11 = (bf16[8,256,640]{2,1,0:T(8,128)(2,1)}, bf16[8,256,640]{2,1,0:T(8,128)(2,1)S(1)}, u32[]{:S(2)}, u32[]{:S(2)}) collective-permute-start(bf16[8,256,640]{2,1,0:T(8,128)(2,1)} %norm_tiles.1.refs_0_.refs_1_.refs_2_.refs_3_.refs_4_.refs_5_), channel_id=1, source_target_pairs={{0,2},{1,3},{2,0},{3,1},{4,6},{5,7},{6,4},{7,5},{8,10},{9,11},{10,... | collective-permute-start | bytes 7864328 | tf_op jit(solution)/shard_map/ppermute | solution.py:378
  99.7 83.5 %collective-permute-start.10 = (bf16[8,256,640]{2,1,0:T(8,128)(2,1)}, bf16[8,256,640]{2,1,0:T(8,128)(2,1)S(1)}, u32[]{:S(2)}, u32[]{:S(2)}) collective-permute-start(bf16[8,256,640]{2,1,0:T(8,128)(2,1)} %norm_tiles.1.refs_0_.refs_1_.refs_2_.refs_3_.refs_4_.refs_5_), channel_id=1, source_target_pairs={{0,4},{1,5},{2,6},{3,7},{4,0},{5,1},{6,2},{7,3},{8,12},{9,13},{10,... | collective-permute-start | bytes 7864328 | tf_op jit(solution)/shard_map/ppermute | solution.py:378
  108.6 64.5 %collective-permute-start.20 = (bf16[6,640,256]{2,1,0:T(8,128)(2,1)}, bf16[6,640,256]{2,1,0:T(8,128)(2,1)S(1)}, u32[]{:S(2)}, u32[]{:S(2)}) collective-permute-start(bf16[6,640,256]{2,1,0:T(8,128)(2,1)} %collective-permute-done.16), channel_id=1, source_target_pairs={{8,0},{9,1},{10,2},{11,3},{12,4},{13,5},{14,6},{15,7},{16,24},{17,... | collective-permute-start | bytes 5898248 | tf_op jit(solution)/shard_map/ppermute | solution.py:459
  109.9 83.3 %collective-permute-start.18 = (bf16[6,640,256]{2,1,0:T(8,128)(2,1)S(1)}, bf16[6,640,256]{2,1,0:T(8,128)(2,1)S(1)}, u32[]{:S(2)}, u32[]{:S(2)}) collective-permute-start(bf16[6,640,256]{2,1,0:T(8,128)(2,1)S(1)} %collective-permute-done.14.refs_30_), channel_id=1, source_target_pairs={{0,1},{1,0},{2,3},{3,2},{4,5},{5,4},{6,7},{7,6},{8,9},{9,8},{10,11... | collective-permute-start | bytes 5898248 | tf_op jit(solution)/shard_map/ppermute | solution.py:378
  125.3 70.7 %collective-permute-start.17 = (bf16[6,640,256]{2,1,0:T(8,128)(2,1)}, bf16[6,640,256]{2,1,0:T(8,128)(2,1)}, u32[]{:S(2)}, u32[]{:S(2)}) collective-permute-start(bf16[6,640,256]{2,1,0:T(8,128)(2,1)} %collective-permute-done.15.refs_32_), channel_id=1, source_target_pairs={{8,16},{9,17},{10,18},{11,19},{12,20},{13,21},{14,22},{15,23},{16,... | collective-permute-start | bytes 5898248 | tf_op jit(solution)/shard_map/ppermute | solution.py:459
  173.1 12.7 %collective-permute-start.29 = (bf16[3,640,256]{2,1,0:T(8,128)(2,1)S(1)}, bf16[3,640,256]{2,1,0:T(8,128)(2,1)S(1)}, u32[]{:S(2)}, u32[]{:S(2)}) collective-permute-start(bf16[3,640,256]{2,1,0:T(8,128)(2,1)S(1)} %pad_maximum_fusion), channel_id=1, source_target_pairs={{0,0},{1,4},{2,2},{3,6},{4,1},{5,5},{6,3},{7,7},{8,8},{9,12},{10,1... | collective-permute-start | bytes 2949128 | tf_op jit(solution)/shard_map/ppermute | solution.py:378
  177.3 48.1 %collective-permute-start.19 = (bf16[6,640,256]{2,1,0:T(8,128)(2,1)}, bf16[6,640,256]{2,1,0:T(8,128)(2,1)}, u32[]{:S(2)}, u32[]{:S(2)}) collective-permute-start(bf16[6,640,256]{2,1,0:T(8,128)(2,1)} %collective-permute-done.15.refs_32_), channel_id=1, source_target_pairs={{0,1},{1,0},{2,3},{3,2},{4,5},{5,4},{6,7},{7,6},{8,9},{9,8},{10,11... | collective-permute-start | bytes 5898248 | tf_op jit(solution)/shard_map/ppermute | solution.py:378
  183.2 42.2 %collective-permute-start.21 = (bf16[6,640,256]{2,1,0:T(8,128)(2,1)}, bf16[6,640,256]{2,1,0:T(8,128)(2,1)}, u32[]{:S(2)}, u32[]{:S(2)}) collective-permute-start(bf16[6,640,256]{2,1,0:T(8,128)(2,1)} %add.133.refs_34_), channel_id=1, source_target_pairs={{0,1},{1,0},{2,3},{3,2},{4,5},{5,4},{6,7},{7,6},{8,9},{9,8},{10,11... | collective-permute-start | bytes 5898248 | tf_op jit(solution)/shard_map/ppermute | solution.py:378
  185.8 36.6 %collective-permute-start.12 = (bf16[8,128,640]{2,1,0:T(8,128)(2,1)}, bf16[8,128,640]{2,1,0:T(8,128)(2,1)S(1)}, u32[]{:S(2)}, u32[]{:S(2)}) collective-permute-start(bf16[8,128,640]{2,1,0:T(8,128)(2,1)} %slice.36), channel_id=1, source_target_pairs={{0,4},{1,5},{2,6},{3,7},{4,0},{5,1},{6,2},{7,3},{8,12},{9,13},{10,... | collective-permute-start | bytes 3932168 | tf_op jit(solution)/shard_map/ppermute | solution.py:378
  194.5 29.3 %collective-permute-start.13 = (bf16[8,128,640]{2,1,0:T(8,128)(2,1)}, bf16[8,128,640]{2,1,0:T(8,128)(2,1)S(1)}, u32[]{:S(2)}, u32[]{:S(2)}) collective-permute-start(bf16[8,128,640]{2,1,0:T(8,128)(2,1)} %slice.37), channel_id=1, source_target_pairs={{0,2},{1,3},{2,0},{3,1},{4,6},{5,7},{6,4},{7,5},{8,10},{9,11},{10,... | collective-permute-start | bytes 3932168 | tf_op jit(solution)/shard_map/ppermute | solution.py:378
  196.0 49.9 %collective-permute-start.22 = (bf16[6,640,256]{2,1,0:T(8,128)(2,1)}, bf16[6,640,256]{2,1,0:T(8,128)(2,1)}, u32[]{:S(2)}, u32[]{:S(2)}) collective-permute-start(bf16[6,640,256]{2,1,0:T(8,128)(2,1)} %collective-permute-done.17), channel_id=1, source_target_pairs={{8,0},{9,1},{10,2},{11,3},{12,4},{13,5},{14,6},{15,7},{16,24},{17,... | collective-permute-start | bytes 5898248 | tf_op jit(solution)/shard_map/ppermute | solution.py:459
  222.5 39.7 %collective-permute-start.31 = (bf16[3,640,256]{2,1,0:T(8,128)(2,1)}, bf16[3,640,256]{2,1,0:T(8,128)(2,1)}, u32[]{:S(2)}, u32[]{:S(2)}) collective-permute-start(bf16[3,640,256]{2,1,0:T(8,128)(2,1)} %copy-done.9), channel_id=1, source_target_pairs={{0,8},{1,9},{2,10},{3,11},{4,12},{5,13},{6,14},{7,15},{8,0},{9,1},... | collective-permute-start | bytes 2949128 | tf_op jit(solution)/shard_map/ppermute | solution.py:378
  223.8 38.3 %collective-permute-start.33 = (bf16[3,640,256]{2,1,0:T(8,128)(2,1)}, bf16[3,640,256]{2,1,0:T(8,128)(2,1)}, u32[]{:S(2)}, u32[]{:S(2)}) collective-permute-start(bf16[3,640,256]{2,1,0:T(8,128)(2,1)} %copy-done.9), channel_id=1, source_target_pairs={{8,16},{9,17},{10,18},{11,19},{12,20},{13,21},{14,22},{15,23},{16,... | collective-permute-start | bytes 2949128 | tf_op jit(solution)/shard_map/ppermute | solution.py:459
  248.7 23.2 %collective-permute-start.23 = (bf16[6,640,256]{2,1,0:T(8,128)(2,1)S(1)}, bf16[6,640,256]{2,1,0:T(8,128)(2,1)}, u32[]{:S(2)}, u32[]{:S(2)}) collective-permute-start(bf16[6,640,256]{2,1,0:T(8,128)(2,1)S(1)} %add.134.refs_10_), channel_id=1, source_target_pairs={{0,1},{1,0},{2,3},{3,2},{4,5},{5,4},{6,7},{7,6},{8,9},{9,8},{10,11... | collective-permute-start | bytes 5898248 | tf_op jit(solution)/shard_map/ppermute | solution.py:378
  265.7 23.2 %collective-permute-start.30 = (bf16[3,640,256]{2,1,0:T(8,128)(2,1)S(1)}, bf16[3,640,256]{2,1,0:T(8,128)(2,1)}, u32[]{:S(2)}, u32[]{:S(2)}) collective-permute-start(bf16[3,640,256]{2,1,0:T(8,128)(2,1)S(1)} %copy-done.10), channel_id=1, source_target_pairs={{0,1},{1,0},{2,3},{3,2},{4,5},{5,4},{6,7},{7,6},{8,9},{9,8},{10,11... | collective-permute-start | bytes 2949128 | tf_op jit(solution)/shard_map/ppermute | solution.py:378
  268.8 20.7 %collective-permute-start.32 = (bf16[3,640,256]{2,1,0:T(8,128)(2,1)}, bf16[3,640,256]{2,1,0:T(8,128)(2,1)}, u32[]{:S(2)}, u32[]{:S(2)}) collective-permute-start(bf16[3,640,256]{2,1,0:T(8,128)(2,1)} %collective-permute-done.31.refs_22_), channel_id=1, source_target_pairs={{0,1},{1,0},{2,3},{3,2},{4,5},{5,4},{6,7},{7,6},{8,9},{9,8},{10,11... | collective-permute-start | bytes 2949128 | tf_op jit(solution)/shard_map/ppermute | solution.py:378
  269.1 45.7 %collective-permute-start.37 = (bf16[3,640,256]{2,1,0:T(8,128)(2,1)}, bf16[3,640,256]{2,1,0:T(8,128)(2,1)}, u32[]{:S(2)}, u32[]{:S(2)}) collective-permute-start(bf16[3,640,256]{2,1,0:T(8,128)(2,1)} %collective-permute-done.36), channel_id=1, source_target_pairs={{8,0},{9,1},{10,2},{11,3},{12,4},{13,5},{14,6},{15,7},{16,24},{17,... | collective-permute-start | bytes 2949128 | tf_op jit(solution)/shard_map/ppermute | solution.py:459
  270.5 57.5 %collective-permute-start.34 = (bf16[3,640,256]{2,1,0:T(8,128)(2,1)}, bf16[3,640,256]{2,1,0:T(8,128)(2,1)}, u32[]{:S(2)}, u32[]{:S(2)}) collective-permute-start(bf16[3,640,256]{2,1,0:T(8,128)(2,1)} %collective-permute-done.33), channel_id=1, source_target_pairs={{8,0},{9,1},{10,2},{11,3},{12,4},{13,5},{14,6},{15,7},{16,24},{17,... | collective-permute-start | bytes 2949128 | tf_op jit(solution)/shard_map/ppermute | solution.py:459
  271.9 13.6 %collective-permute-start.28 = (f32[6,128]{1,0:T(8,128)S(1)}, f32[6,128]{1,0:T(8,128)S(1)}, u32[]{:S(2)}, u32[]{:S(2)}) collective-permute-start(f32[6,128]{1,0:T(8,128)S(1)} %copy-done.36), channel_id=1, source_target_pairs={{0,0},{1,4},{2,2},{3,6},{4,1},{5,5},{6,3},{7,7},{8,8},{9,12},{10,1... | collective-permute-start | bytes 9224 | tf_op jit(solution)/shard_map/ppermute | solution.py:378
  285.5 15.4 %collective-permute-start.24 = (f32[8,1024]{1,0:T(8,128)}, f32[8,1024]{1,0:T(8,128)S(1)}, u32[]{:S(2)}, u32[]{:S(2)}) collective-permute-start(f32[8,1024]{1,0:T(8,128)} %get-tuple-element.45.refs_2_), channel_id=1, source_target_pairs={{0,4},{1,5},{2,6},{3,7},{4,0},{5,1},{6,2},{7,3},{8,12},{9,13},{10,... | collective-permute-start | bytes 98312 | tf_op jit(solution)/shard_map/ppermute | solution.py:378
  316.6 14.0 %collective-permute-start.38 = (bf16[3,640,256]{2,1,0:T(8,128)(2,1)S(1)}, bf16[3,640,256]{2,1,0:T(8,128)(2,1)S(1)}, u32[]{:S(2)}, u32[]{:S(2)}) collective-permute-start(bf16[3,640,256]{2,1,0:T(8,128)(2,1)S(1)} %add.138.refs_23_), channel_id=1, source_target_pairs={{0,1},{1,0},{2,3},{3,2},{4,5},{5,4},{6,7},{7,6},{8,9},{9,8},{10,11... | collective-permute-start | bytes 2949128 | tf_op jit(solution)/shard_map/ppermute | solution.py:378
  (44 other events, 735.8 us)

commit v5 on v4

--- a/solution.py
+++ b/solution.py
@@ -486,18 +486,18 @@
         qk_own.append(crossed + outward(crossed))
         passed = outward(crossed_next)
         v_crossed = cross(after(v_own[0], crossed_next))
-        v_crossed_next = cross(after(v_own[1], v_crossed))
+        v_crossed_next = cross(after(v_own[1], crossed_next))
         v_passed = [outward(after(v_crossed, passed)), outward(after(v_crossed_next, passed))]
 
     blocks, at = blocks_of(qk_own, range(planes - 1))
     qk, *_ = project(pieces, blocks, at, None, False)
-    qk_own.append(after(crossed_next, qk) + passed if planes == 4 else ring(after(qk_own[-1], qk)))
+    split = max(planes - 2, 1)
+    blocks, at = blocks_of(v_own, range(split))
+    blocks[0] = after(blocks[0], qk)
+    values, *_ = project(pieces, blocks, at, None, False)
+    qk_own.append(after(crossed_next, values) + passed if planes == 4 else ring(after(qk_own[-1], values)))
     blocks, at = blocks_of(qk_own, [planes - 1])
     qk, sums = project(pieces, blocks, at, qk, True)
-    split = max(planes - 2, 1)
-    blocks, at = blocks_of(v_own, range(split))
-    blocks[0] = after(blocks[0], sums)
-    values, *_ = project(pieces, blocks, at, None, False)
     partial_sums = [sums]
     partial_sums.append(along_x(sums))
     for py in range(1, lines):

time: 406 us -> 415 us (1.022)
  starting transfers between devices: 101 us -> 106 us
  blocking collectives: 50.9 us -> 55.5 us
    ppermute x31, waiting for transfers between devices: 83.3 us -> 76.6 us  [send(): return lax.ppermute(value, AXES, pairs)]
    ppermute x8, waiting for transfers between devices: 55.8 us -> 60.9 us  [send_some(): return lax.ppermute(value, AXES, pairs)]
    ppermute x31, starting transfers between devices: 88.7 us -> 93.7 us  [send(): return lax.ppermute(value, AXES, pairs)]
    all_to_all x1, blocking collectives: 50.9 us -> 55.5 us  [transposed(): lax.all_to_all(mixed.reshape(groups * n, capacity * piece, heads * dim),...]
  transfers between devices with their start and end apart: 39 -> 39, of which waited for: 11 -> 14; matrix products, arithmetic and copies ran while one was open for 5% -> 4% of each run, Pallas kernels for 16% -> 16%
where the time goes in v5:
time: 415 us; the launch traced here: 414 us
  waiting for transfers between devices  137 us (33%)
  starting transfers between devices  106 us (26%)
  Pallas kernels  88.8 us (21%)
  blocking collectives  55.5 us (13%)
  other arithmetic  13.4 us (3%)
  local copies, waits for them, and re-layouts  11.8 us (3%)
    ppermute x31, starting transfers between devices, send(): return lax.ppermute(value, AXES, pairs)  93.7 us
    ppermute x31, waiting for transfers between devices, send(): return lax.ppermute(value, AXES, pairs)  76.6 us
    ppermute x8, waiting for transfers between devices, send_some(): return lax.ppermute(value, AXES, pairs)  60.9 us
    all_to_all x1, blocking collectives, transposed(): lax.all_to_all(mixed.reshape(groups * n, capacity * piece, heads * dim),...  55.5 us
    pallas_call x3, Pallas kernels, project(): pl.pallas_call(body, out_shape=out_shape, grid_spec=pltpu.PrefetchScalarG...  42.8 us
    pallas_call x1, Pallas kernels, mix_values(): pl.pallas_call(body, out_shape=jax.ShapeDtypeStruct((groups, n, capacity...  17.9 us
    pallas_call x1, Pallas kernels, soft_weights(): pl.pallas_call(body, out_shape=jax.ShapeDtypeStruct((count, total, total)...  13.4 us
    ppermute x8, starting transfers between devices, send_some(): return lax.ppermute(value, AXES, pairs)  12.6 us
  transfers between devices with their start and end apart: 39, of which 14 were waited for; matrix products, arithmetic and copies ran while one was open for 4% of the time, Pallas kernels for 16%

profile of v5, /device:TPU:0, one launch (start us, length us, event | category | flops | bytes accessed | tf_op | source)
XLA Modules:
  0.0 413.7 jit_solution(12120565783749868473)
XLA Ops:
  0.6 3.5 pick_tiles.1
  7.5 5.5 %collective-permute-start.3 = (bf16[2,16,5120]{2,1,0:T(8,128)(2,1)S(1)}, bf16[2,16,5120]{2,1,0:T(8,128)(2,1)S(1)}, u32[]{:S(2)}, u32[]{:S(2)}) collective-permute-start(bf16[2,16,5120]{2,1,0:T(8,128)(2,1)S(1)} %copy-done.33), channel_id=1, source_target_pairs={{0,1},{1,5},{2,3},{3,7},{4,8},{5,12},{6,10},{7,14},{8,9},{9,13},{1... | collective-permute-start | bytes 983048 | tf_op jit(solution)/shard_map/ppermute | solution.py:378
  14.6 2.4 collective-permute-start.5
  18.3 8.0 %collective-permute-done.3.rest_1_ = bf16[2,16,5120]{2,1,0:T(8,128)(2,1)S(1)} collective-permute-done((bf16[2,16,5120]{2,1,0:T(8,128)(2,1)S(1)}, bf16[2,16,5120]{2,1,0:T(8,128)(2,1)S(1)}, u32[]{:S(2)}, u32[]{:S(2)}) %collective-permute-start.3) | collective-permute-done | bytes 327712 | tf_op jit(solution)/shard_map/ppermute | solution.py:378
  26.3 23.3 %collective-permute-start.7 = (bf16[2,16,5120]{2,1,0:T(8,128)(2,1)S(1)}, bf16[2,16,5120]{2,1,0:T(8,128)(2,1)S(1)}, u32[]{:S(2)}, u32[]{:S(2)}) collective-permute-start(bf16[2,16,5120]{2,1,0:T(8,128)(2,1)S(1)} %copy-done.29), channel_id=1, source_target_pairs={{0,17},{1,21},{2,19},{3,23},{4,24},{5,28},{6,26},{7,30},{8,25},{9,... | collective-permute-start | bytes 983048 | tf_op jit(solution)/shard_map/ppermute | solution.py:378
  49.7 3.2 collective-permute-start.8
  53.0 11.7 %collective-permute-done.7.rest_5_ = bf16[2,16,5120]{2,1,0:T(8,128)(2,1)S(1)} collective-permute-done((bf16[2,16,5120]{2,1,0:T(8,128)(2,1)S(1)}, bf16[2,16,5120]{2,1,0:T(8,128)(2,1)S(1)}, u32[]{:S(2)}, u32[]{:S(2)}) %collective-permute-start.7) | collective-permute-done | bytes 327712 | tf_op jit(solution)/shard_map/ppermute | solution.py:378
  64.8 7.0 %collective-permute-done.9.rest_7_ = bf16[2,16,5120]{2,1,0:T(8,128)(2,1)S(1)} collective-permute-done((bf16[2,16,5120]{2,1,0:T(8,128)(2,1)S(1)}, bf16[2,16,5120]{2,1,0:T(8,128)(2,1)S(1)}, u32[]{:S(2)}, u32[]{:S(2)}) %collective-permute-start.9) | collective-permute-done | bytes 327712 | tf_op jit(solution)/shard_map/ppermute | solution.py:378
  71.9 2.0 collective-permute-start.16
  73.9 11.8 %collective-permute-start.15 = (bf16[6,640,256]{2,1,0:T(8,128)(2,1)S(1)}, bf16[6,640,256]{2,1,0:T(8,128)(2,1)}, u32[]{:S(2)}, u32[]{:S(2)}) collective-permute-start(bf16[6,640,256]{2,1,0:T(8,128)(2,1)S(1)} %collective-permute-done.14.refs_30_), channel_id=1, source_target_pairs={{0,8},{1,9},{2,10},{3,11},{4,12},{5,13},{6,14},{7,15},{8,0},{9,1},... | collective-permute-start | bytes 5898248 | tf_op jit(solution)/shard_map/ppermute | solution.py:378
  89.7 8.5 %norm_tiles.1.refs_0_.refs_1_.refs_2_.refs_3_.refs_4_.refs_5_ = bf16[8,256,640]{2,1,0:T(8,128)(2,1)} custom-call(s32[16]{0:T(128)} %broadcast_maximum_fusion.1.member_ref, s32[16]{0:T(128)} %iota.28.place_ref, s32[2]{0:T(128)} %pad_add_fusion.3.ids_ref, f32[4,2,5120]{2,1,0:T(2,128)} %copy-done.20, bf16[2,16,5120]{2,1,0:T(8,128)(2,1)} %copy-done.12, ...), custom_call_target="tpu_custom_call" | custom-call | flops 15728640 | bytes 5242880 | tf_op jit(solution)/shard_map/norm_tiles/pallas_call | solution.py:117
  98.2 9.5 %collective-permute-start.10 = (bf16[8,256,640]{2,1,0:T(8,128)(2,1)}, bf16[8,256,640]{2,1,0:T(8,128)(2,1)S(1)}, u32[]{:S(2)}, u32[]{:S(2)}) collective-permute-start(bf16[8,256,640]{2,1,0:T(8,128)(2,1)} %norm_tiles.1.refs_0_.refs_1_.refs_2_.refs_3_.refs_4_.refs_5_), channel_id=1, source_target_pairs={{0,4},{1,5},{2,6},{3,7},{4,0},{5,1},{6,2},{7,3},{8,12},{9,13},{10,... | collective-permute-start | bytes 7864328 | tf_op jit(solution)/shard_map/ppermute | solution.py:378
  112.8 14.7 %collective-permute-done.15.refs_32_ = bf16[6,640,256]{2,1,0:T(8,128)(2,1)} collective-permute-done((bf16[6,640,256]{2,1,0:T(8,128)(2,1)S(1)}, bf16[6,640,256]{2,1,0:T(8,128)(2,1)}, u32[]{:S(2)}, u32[]{:S(2)}) %collective-permute-start.15) | collective-permute-done | bytes 1966112 | tf_op jit(solution)/shard_map/ppermute | solution.py:378
  127.5 2.0 collective-permute-start.19
  131.5 39.8 %collective-permute-done.21 = bf16[6,640,256]{2,1,0:T(8,128)(2,1)S(1)} collective-permute-done((bf16[6,640,256]{2,1,0:T(8,128)(2,1)}, bf16[6,640,256]{2,1,0:T(8,128)(2,1)S(1)}, u32[]{:S(2)}, u32[]{:S(2)}) %collective-permute-start.21) | collective-permute-done | bytes 1966112 | tf_op jit(solution)/shard_map/ppermute | solution.py:459
  171.2 3.4 add.133.refs_34_
  174.7 8.8 %collective-permute-start.20 = (bf16[6,640,256]{2,1,0:T(8,128)(2,1)}, bf16[6,640,256]{2,1,0:T(8,128)(2,1)}, u32[]{:S(2)}, u32[]{:S(2)}) collective-permute-start(bf16[6,640,256]{2,1,0:T(8,128)(2,1)} %collective-permute-done.15.refs_32_), channel_id=1, source_target_pairs={{0,1},{1,0},{2,3},{3,2},{4,5},{5,4},{6,7},{7,6},{8,9},{9,8},{10,11... | collective-permute-start | bytes 5898248 | tf_op jit(solution)/shard_map/ppermute | solution.py:378
  186.1 3.5 collective-permute-done.24.refs_22_
  189.7 7.0 %collective-permute-start.12 = (bf16[8,128,640]{2,1,0:T(8,128)(2,1)}, bf16[8,128,640]{2,1,0:T(8,128)(2,1)S(1)}, u32[]{:S(2)}, u32[]{:S(2)}) collective-permute-start(bf16[8,128,640]{2,1,0:T(8,128)(2,1)} %slice.36), channel_id=1, source_target_pairs={{0,4},{1,5},{2,6},{3,7},{4,0},{5,1},{6,2},{7,3},{8,12},{9,13},{10,... | collective-permute-start | bytes 3932168 | tf_op jit(solution)/shard_map/ppermute | solution.py:378
  202.0 24.3 %collective-permute-done.12.refs_18_.refs_19_.refs_20_.refs_21_.refs_22_.refs_23_.refs_12_.refs_13_.refs_14_.refs_15_.refs_6_.refs_7_.refs_16_ = bf16[8,128,640]{2,1,0:T(8,128)(2,1)S(1)} collective-permute-done((bf16[8,128,640]{2,1,0:T(8,128)(2,1)}, bf16[8,128,640]{2,1,0:T(8,128)(2,1)S(1)}, u32[]{:S(2)}, u32[]{:S(2)}) %collective-permute-start.12) | collective-permute-done | bytes 1310752 | tf_op jit(solution)/shard_map/ppermute | solution.py:378
  229.0 20.4 %project.3.refs_12_ = f32[6,1024,256]{2,1,0:T(8,128)} custom-call(s32[6]{0:T(128)} %stack.84.at_ref, bf16[8,256,640]{2,1,0:T(8,128)(2,1)} %norm_tiles.1.refs_0_.refs_1_.refs_2_.refs_3_.refs_4_.refs_5_, bf16[8,256,640]{2,1,0:T(8,128)(2,1)} %norm_tiles.1.refs_0_.refs_1_.refs_2_.refs_3_.refs_4_.refs_5_, ...), custom_call_target="tpu_custom_call" | custom-call | flops 12079595520 | bytes 32243712 | tf_op jit(solution)/shard_map/project/pallas_call | solution.py:187
  249.4 9.7 %project.4.refs_25_ = f32[3,1024,256]{2,1,0:T(8,128)} custom-call(s32[4]{0:T(128)} %pad_add_fusion.4.at_ref, bf16[8,256,640]{2,1,0:T(8,128)(2,1)} %norm_tiles.1.refs_0_.refs_1_.refs_2_.refs_3_.refs_4_.refs_5_, bf16[8,256,640]{2,1,0:T(8,128)(2,1)} %norm_tiles.1.refs_0_.refs_1_.refs_2_.refs_3_.refs_4_.refs_5_, ...), custom_call_target="tpu_custom_call" | custom-call | flops 4026531840 | bytes 15466496 | tf_op jit(solution)/shard_map/project/pallas_call | solution.py:187
  259.1 2.7 add.134.refs_10_
  270.3 12.7 %project.5 = (f32[6,1024,256]{2,1,0:T(8,128)}, f32[8,1024]{1,0:T(8,128)}) custom-call(s32[2]{0:T(128)} %pad_add_fusion.2.at_ref, bf16[8,256,640]{2,1,0:T(8,128)(2,1)} %norm_tiles.1.refs_0_.refs_1_.refs_2_.refs_3_.refs_4_.refs_5_, bf16[8,256,640]{2,1,0:T(8,128)(2,1)} %norm_tiles.1.refs_0_.refs_1_.refs_2_.refs_3_.refs_4_.refs_5_, ...), custom_call_target="tpu_custom_call", output_to_operand_aliasing={{0}: (13, {})} | custom-call | flops 4026531840 | bytes 19136512 | tf_op jit(solution)/shard_map/project/pallas_call | solution.py:187
  283.0 6.1 %collective-permute-start.28 = (f32[8,1024]{1,0:T(8,128)}, f32[8,1024]{1,0:T(8,128)S(1)}, u32[]{:S(2)}, u32[]{:S(2)}) collective-permute-start(f32[8,1024]{1,0:T(8,128)} %get-tuple-element.47.refs_2_), channel_id=1, source_target_pairs={{0,4},{1,5},{2,6},{3,7},{4,0},{5,1},{6,2},{7,3},{8,12},{9,13},{10,... | collective-permute-start | bytes 98312 | tf_op jit(solution)/shard_map/ppermute | solution.py:378
  291.6 2.0 collective-permute-done.29.refs_4_
  293.5 2.1 collective-permute-done.30.refs_5_
  296.3 13.4 %soft_weights.1.refs_0_ = bf16[6,1024,1024]{2,1,0:T(8,128)(2,1)} custom-call(f32[6,1024,256]{2,1,0:T(8,128)} %get-tuple-element.46.refs_0_.refs_1_, f32[6,1024,256]{2,1,0:T(8,128)} %get-tuple-element.46.refs_0_.refs_1_, f32[8,1024]{1,0:T(8,128)} %get-tuple-element.47.refs_2_, f32[8,1024]{1,0:T(8,128)} %copy-done.21, f32[8,1024]{1,0:T(8,128)} %copy-done.22, ...), custom_call_target="tpu_custom_call" | custom-call | flops 1660944384 | bytes 18874368 | tf_op jit(solution)/shard_map/soft_weights/pallas_call | solution.py:247
  313.5 19.1 %collective-permute-done.37 = bf16[3,640,256]{2,1,0:T(8,128)(2,1)S(1)} collective-permute-done((bf16[3,640,256]{2,1,0:T(8,128)(2,1)}, bf16[3,640,256]{2,1,0:T(8,128)(2,1)S(1)}, u32[]{:S(2)}, u32[]{:S(2)}) %collective-permute-start.37) | collective-permute-done | bytes 983072 | tf_op jit(solution)/shard_map/ppermute | solution.py:459
  337.6 17.9 %mix_values.1 = bf16[8,4,32,768]{3,2,1,0:T(8,128)(2,1)} custom-call(s32[4]{0:T(128)} %get-tuple-element.67.order_ref, s32[16]{0:T(128)} %iota.27.place_ref, s32[4]{0:T(128)} %get-tuple-element.68.at_ref, bf16[6,1024,1024]{2,1,0:T(8,128)(2,1)} %soft_weights.1.refs_0_, bf16[8,256,640]{2,1,0:T(8,128)(2,1)} %norm_tiles.1.refs_0_.refs_1_.refs_2_.refs_3_.refs_4_.refs_5_, ...), custom_call_target="tpu_custom_call" | custom-call | flops 5637144576 | bytes 17301504 | tf_op jit(solution)/shard_map/mix_values/pallas_call | solution.py:314
  355.5 55.5 %all_to_all.5.in_ref = bf16[32,32,768]{2,1,0:T(8,128)(2,1)} all-to-all(bf16[32,32,768]{2,1,0:T(8,128)(2,1)} %bitcast.19), channel_id=1, replica_groups=mesh['bal'=8,'seq'=4] {'bal','seq'}, dimensions={0} | all-to-all | bytes 3145728 | tf_op jit(solution)/shard_map/all_to_all | solution.py:518
  411.0 2.7 place_tiles.1
  (159 shorter events, 48.8 us)
Async XLA Ops:
  6.0 65.8 %collective-permute-start.14 = (bf16[6,640,256]{2,1,0:T(8,128)(2,1)S(1)}, bf16[6,640,256]{2,1,0:T(8,128)(2,1)S(1)}, u32[]{:S(2)}, u32[]{:S(2)}) collective-permute-start(bf16[6,640,256]{2,1,0:T(8,128)(2,1)S(1)} %slice.32), channel_id=1, source_target_pairs={{0,0},{1,4},{2,2},{3,6},{4,1},{5,5},{6,3},{7,7},{8,8},{9,12},{10,1... | collective-permute-start | bytes 5898248 | tf_op jit(solution)/shard_map/ppermute | solution.py:378
  6.8 10.2 %collective-permute-start.2 = (bf16[2,16,5120]{2,1,0:T(8,128)(2,1)S(1)}, bf16[2,16,5120]{2,1,0:T(8,128)(2,1)S(1)}, u32[]{:S(2)}, u32[]{:S(2)}) collective-permute-start(bf16[2,16,5120]{2,1,0:T(8,128)(2,1)S(1)} %copy-done.34), channel_id=1, source_target_pairs={{0,0},{1,4},{2,2},{3,6},{4,1},{5,5},{6,3},{7,7},{8,8},{9,12},{10,1... | collective-permute-start | bytes 983048 | tf_op jit(solution)/shard_map/ppermute | solution.py:378
  7.5 18.8 %collective-permute-start.3 = (bf16[2,16,5120]{2,1,0:T(8,128)(2,1)S(1)}, bf16[2,16,5120]{2,1,0:T(8,128)(2,1)S(1)}, u32[]{:S(2)}, u32[]{:S(2)}) collective-permute-start(bf16[2,16,5120]{2,1,0:T(8,128)(2,1)S(1)} %copy-done.33), channel_id=1, source_target_pairs={{0,1},{1,5},{2,3},{3,7},{4,8},{5,12},{6,10},{7,14},{8,9},{9,13},{1... | collective-permute-start | bytes 983048 | tf_op jit(solution)/shard_map/ppermute | solution.py:378
  13.0 36.6 %collective-permute-start.4 = (bf16[2,16,5120]{2,1,0:T(8,128)(2,1)S(1)}, bf16[2,16,5120]{2,1,0:T(8,128)(2,1)S(1)}, u32[]{:S(2)}, u32[]{:S(2)}) collective-permute-start(bf16[2,16,5120]{2,1,0:T(8,128)(2,1)S(1)} %copy-done.32), channel_id=1, source_target_pairs={{0,8},{1,12},{2,10},{3,14},{4,9},{5,13},{6,11},{7,15},{8,16},{9,20... | collective-permute-start | bytes 983048 | tf_op jit(solution)/shard_map/ppermute | solution.py:378
  14.6 38.3 %collective-permute-start.5 = (bf16[2,16,5120]{2,1,0:T(8,128)(2,1)S(1)}, bf16[2,16,5120]{2,1,0:T(8,128)(2,1)S(1)}, u32[]{:S(2)}, u32[]{:S(2)}) collective-permute-start(bf16[2,16,5120]{2,1,0:T(8,128)(2,1)S(1)} %copy-done.31), channel_id=1, source_target_pairs={{0,9},{1,13},{2,11},{3,15},{4,16},{5,20},{6,18},{7,22},{8,17},{9,2... | collective-permute-start | bytes 983048 | tf_op jit(solution)/shard_map/ppermute | solution.py:378
  17.0 35.9 %collective-permute-start.6 = (bf16[2,16,5120]{2,1,0:T(8,128)(2,1)S(1)}, bf16[2,16,5120]{2,1,0:T(8,128)(2,1)S(1)}, u32[]{:S(2)}, u32[]{:S(2)}) collective-permute-start(bf16[2,16,5120]{2,1,0:T(8,128)(2,1)S(1)} %copy-done.30), channel_id=1, source_target_pairs={{0,16},{1,20},{2,18},{3,22},{4,17},{5,21},{6,19},{7,23},{8,24},{9,... | collective-permute-start | bytes 983048 | tf_op jit(solution)/shard_map/ppermute | solution.py:378
  26.3 38.3 %collective-permute-start.7 = (bf16[2,16,5120]{2,1,0:T(8,128)(2,1)S(1)}, bf16[2,16,5120]{2,1,0:T(8,128)(2,1)S(1)}, u32[]{:S(2)}, u32[]{:S(2)}) collective-permute-start(bf16[2,16,5120]{2,1,0:T(8,128)(2,1)S(1)} %copy-done.29), channel_id=1, source_target_pairs={{0,17},{1,21},{2,19},{3,23},{4,24},{5,28},{6,26},{7,30},{8,25},{9,... | collective-permute-start | bytes 983048 | tf_op jit(solution)/shard_map/ppermute | solution.py:378
  49.7 15.2 %collective-permute-start.8 = (bf16[2,16,5120]{2,1,0:T(8,128)(2,1)S(1)}, bf16[2,16,5120]{2,1,0:T(8,128)(2,1)S(1)}, u32[]{:S(2)}, u32[]{:S(2)}) collective-permute-start(bf16[2,16,5120]{2,1,0:T(8,128)(2,1)S(1)} %copy-done.28), channel_id=1, source_target_pairs={{0,24},{1,28},{2,26},{3,30},{4,25},{5,29},{6,27},{7,31},{8,0},{9,4... | collective-permute-start | bytes 983048 | tf_op jit(solution)/shard_map/ppermute | solution.py:378
  52.9 18.9 %collective-permute-start.9 = (bf16[2,16,5120]{2,1,0:T(8,128)(2,1)S(1)}, bf16[2,16,5120]{2,1,0:T(8,128)(2,1)S(1)}, u32[]{:S(2)}, u32[]{:S(2)}) collective-permute-start(bf16[2,16,5120]{2,1,0:T(8,128)(2,1)S(1)} %copy-done.27), channel_id=1, source_target_pairs={{0,25},{1,29},{2,27},{3,31},{4,0},{5,4},{6,2},{7,6},{8,1},{9,5},{1... | collective-permute-start | bytes 983048 | tf_op jit(solution)/shard_map/ppermute | solution.py:378
  71.9 37.5 %collective-permute-start.16 = (bf16[6,640,256]{2,1,0:T(8,128)(2,1)S(1)}, bf16[6,640,256]{2,1,0:T(8,128)(2,1)}, u32[]{:S(2)}, u32[]{:S(2)}) collective-permute-start(bf16[6,640,256]{2,1,0:T(8,128)(2,1)S(1)} %collective-permute-done.14.refs_30_), channel_id=1, source_target_pairs={{8,16},{9,17},{10,18},{11,19},{12,20},{13,21},{14,22},{15,23},{16,... | collective-permute-start | bytes 5898248 | tf_op jit(solution)/shard_map/ppermute | solution.py:459
  73.9 53.6 %collective-permute-start.15 = (bf16[6,640,256]{2,1,0:T(8,128)(2,1)S(1)}, bf16[6,640,256]{2,1,0:T(8,128)(2,1)}, u32[]{:S(2)}, u32[]{:S(2)}) collective-permute-start(bf16[6,640,256]{2,1,0:T(8,128)(2,1)S(1)} %collective-permute-done.14.refs_30_), channel_id=1, source_target_pairs={{0,8},{1,9},{2,10},{3,11},{4,12},{5,13},{6,14},{7,15},{8,0},{9,1},... | collective-permute-start | bytes 5898248 | tf_op jit(solution)/shard_map/ppermute | solution.py:378
  98.2 76.4 %collective-permute-start.10 = (bf16[8,256,640]{2,1,0:T(8,128)(2,1)}, bf16[8,256,640]{2,1,0:T(8,128)(2,1)S(1)}, u32[]{:S(2)}, u32[]{:S(2)}) collective-permute-start(bf16[8,256,640]{2,1,0:T(8,128)(2,1)} %norm_tiles.1.refs_0_.refs_1_.refs_2_.refs_3_.refs_4_.refs_5_), channel_id=1, source_target_pairs={{0,4},{1,5},{2,6},{3,7},{4,0},{5,1},{6,2},{7,3},{8,12},{9,13},{10,... | collective-permute-start | bytes 7864328 | tf_op jit(solution)/shard_map/ppermute | solution.py:378
  107.8 75.6 %collective-permute-start.11 = (bf16[8,256,640]{2,1,0:T(8,128)(2,1)}, bf16[8,256,640]{2,1,0:T(8,128)(2,1)S(1)}, u32[]{:S(2)}, u32[]{:S(2)}) collective-permute-start(bf16[8,256,640]{2,1,0:T(8,128)(2,1)} %norm_tiles.1.refs_0_.refs_1_.refs_2_.refs_3_.refs_4_.refs_5_), channel_id=1, source_target_pairs={{0,2},{1,3},{2,0},{3,1},{4,6},{5,7},{6,4},{7,5},{8,10},{9,11},{10,... | collective-permute-start | bytes 7864328 | tf_op jit(solution)/shard_map/ppermute | solution.py:378
  109.3 61.9 %collective-permute-start.21 = (bf16[6,640,256]{2,1,0:T(8,128)(2,1)}, bf16[6,640,256]{2,1,0:T(8,128)(2,1)S(1)}, u32[]{:S(2)}, u32[]{:S(2)}) collective-permute-start(bf16[6,640,256]{2,1,0:T(8,128)(2,1)} %collective-permute-done.16), channel_id=1, source_target_pairs={{8,0},{9,1},{10,2},{11,3},{12,4},{13,5},{14,6},{15,7},{16,24},{17,... | collective-permute-start | bytes 5898248 | tf_op jit(solution)/shard_map/ppermute | solution.py:459
  112.1 17.4 %collective-permute-start.18 = (bf16[3,640,256]{2,1,0:T(8,128)(2,1)S(1)}, bf16[3,640,256]{2,1,0:T(8,128)(2,1)S(1)}, u32[]{:S(2)}, u32[]{:S(2)}) collective-permute-start(bf16[3,640,256]{2,1,0:T(8,128)(2,1)S(1)} %pad_maximum_fusion), channel_id=1, source_target_pairs={{0,0},{1,4},{2,2},{3,6},{4,1},{5,5},{6,3},{7,7},{8,8},{9,12},{10,1... | collective-permute-start | bytes 2949128 | tf_op jit(solution)/shard_map/ppermute | solution.py:378
  127.5 69.2 %collective-permute-start.19 = (bf16[6,640,256]{2,1,0:T(8,128)(2,1)S(1)}, bf16[6,640,256]{2,1,0:T(8,128)(2,1)S(1)}, u32[]{:S(2)}, u32[]{:S(2)}) collective-permute-start(bf16[6,640,256]{2,1,0:T(8,128)(2,1)S(1)} %collective-permute-done.14.refs_30_), channel_id=1, source_target_pairs={{0,1},{1,0},{2,3},{3,2},{4,5},{5,4},{6,7},{7,6},{8,9},{9,8},{10,11... | collective-permute-start | bytes 5898248 | tf_op jit(solution)/shard_map/ppermute | solution.py:378
  129.5 70.0 %collective-permute-start.17 = (bf16[6,640,256]{2,1,0:T(8,128)(2,1)}, bf16[6,640,256]{2,1,0:T(8,128)(2,1)}, u32[]{:S(2)}, u32[]{:S(2)}) collective-permute-start(bf16[6,640,256]{2,1,0:T(8,128)(2,1)} %collective-permute-done.15.refs_32_), channel_id=1, source_target_pairs={{8,16},{9,17},{10,18},{11,19},{12,20},{13,21},{14,22},{15,23},{16,... | collective-permute-start | bytes 5898248 | tf_op jit(solution)/shard_map/ppermute | solution.py:459
  171.2 18.5 %collective-permute-start.24 = (bf16[3,640,256]{2,1,0:T(8,128)(2,1)S(1)}, bf16[3,640,256]{2,1,0:T(8,128)(2,1)}, u32[]{:S(2)}, u32[]{:S(2)}) collective-permute-start(bf16[3,640,256]{2,1,0:T(8,128)(2,1)S(1)} %collective-permute-done.18.refs_20_), channel_id=1, source_target_pairs={{0,8},{1,9},{2,10},{3,11},{4,12},{5,13},{6,14},{7,15},{8,0},{9,1},... | collective-permute-start | bytes 2949128 | tf_op jit(solution)/shard_map/ppermute | solution.py:378
  174.7 53.3 %collective-permute-start.20 = (bf16[6,640,256]{2,1,0:T(8,128)(2,1)}, bf16[6,640,256]{2,1,0:T(8,128)(2,1)}, u32[]{:S(2)}, u32[]{:S(2)}) collective-permute-start(bf16[6,640,256]{2,1,0:T(8,128)(2,1)} %collective-permute-done.15.refs_32_), channel_id=1, source_target_pairs={{0,1},{1,0},{2,3},{3,2},{4,5},{5,4},{6,7},{7,6},{8,9},{9,8},{10,11... | collective-permute-start | bytes 5898248 | tf_op jit(solution)/shard_map/ppermute | solution.py:378
  183.4 44.5 %collective-permute-start.22 = (bf16[6,640,256]{2,1,0:T(8,128)(2,1)}, bf16[6,640,256]{2,1,0:T(8,128)(2,1)}, u32[]{:S(2)}, u32[]{:S(2)}) collective-permute-start(bf16[6,640,256]{2,1,0:T(8,128)(2,1)} %add.133.refs_34_), channel_id=1, source_target_pairs={{0,1},{1,0},{2,3},{3,2},{4,5},{5,4},{6,7},{7,6},{8,9},{9,8},{10,11... | collective-permute-start | bytes 5898248 | tf_op jit(solution)/shard_map/ppermute | solution.py:378
  189.7 36.6 %collective-permute-start.12 = (bf16[8,128,640]{2,1,0:T(8,128)(2,1)}, bf16[8,128,640]{2,1,0:T(8,128)(2,1)S(1)}, u32[]{:S(2)}, u32[]{:S(2)}) collective-permute-start(bf16[8,128,640]{2,1,0:T(8,128)(2,1)} %slice.36), channel_id=1, source_target_pairs={{0,4},{1,5},{2,6},{3,7},{4,0},{5,1},{6,2},{7,3},{8,12},{9,13},{10,... | collective-permute-start | bytes 3932168 | tf_op jit(solution)/shard_map/ppermute | solution.py:378
  197.9 30.0 %collective-permute-start.13 = (bf16[8,128,640]{2,1,0:T(8,128)(2,1)}, bf16[8,128,640]{2,1,0:T(8,128)(2,1)S(1)}, u32[]{:S(2)}, u32[]{:S(2)}) collective-permute-start(bf16[8,128,640]{2,1,0:T(8,128)(2,1)} %slice.37), channel_id=1, source_target_pairs={{0,2},{1,3},{2,0},{3,1},{4,6},{5,7},{6,4},{7,5},{8,10},{9,11},{10,... | collective-permute-start | bytes 3932168 | tf_op jit(solution)/shard_map/ppermute | solution.py:378
  199.4 59.7 %collective-permute-start.26 = (bf16[6,640,256]{2,1,0:T(8,128)(2,1)}, bf16[6,640,256]{2,1,0:T(8,128)(2,1)}, u32[]{:S(2)}, u32[]{:S(2)}) collective-permute-start(bf16[6,640,256]{2,1,0:T(8,128)(2,1)} %collective-permute-done.17), channel_id=1, source_target_pairs={{8,0},{9,1},{10,2},{11,3},{12,4},{13,5},{14,6},{15,7},{16,24},{17,... | collective-permute-start | bytes 5898248 | tf_op jit(solution)/shard_map/ppermute | solution.py:459
  226.3 23.1 %collective-permute-start.23 = (bf16[3,640,256]{2,1,0:T(8,128)(2,1)}, bf16[3,640,256]{2,1,0:T(8,128)(2,1)}, u32[]{:S(2)}, u32[]{:S(2)}) collective-permute-start(bf16[3,640,256]{2,1,0:T(8,128)(2,1)} %copy-done.9), channel_id=1, source_target_pairs={{0,1},{1,0},{2,3},{3,2},{4,5},{5,4},{6,7},{7,6},{8,9},{9,8},{10,11... | collective-permute-start | bytes 2949128 | tf_op jit(solution)/shard_map/ppermute | solution.py:378
  227.9 21.5 %collective-permute-start.25 = (bf16[3,640,256]{2,1,0:T(8,128)(2,1)}, bf16[3,640,256]{2,1,0:T(8,128)(2,1)}, u32[]{:S(2)}, u32[]{:S(2)}) collective-permute-start(bf16[3,640,256]{2,1,0:T(8,128)(2,1)} %collective-permute-done.24.refs_22_), channel_id=1, source_target_pairs={{0,1},{1,0},{2,3},{3,2},{4,5},{5,4},{6,7},{7,6},{8,9},{9,8},{10,11... | collective-permute-start | bytes 2949128 | tf_op jit(solution)/shard_map/ppermute | solution.py:378
  261.8 8.4 %collective-permute-start.27 = (bf16[6,640,256]{2,1,0:T(8,128)(2,1)S(1)}, bf16[6,640,256]{2,1,0:T(8,128)(2,1)}, u32[]{:S(2)}, u32[]{:S(2)}) collective-permute-start(bf16[6,640,256]{2,1,0:T(8,128)(2,1)S(1)} %add.134.refs_10_), channel_id=1, source_target_pairs={{0,1},{1,0},{2,3},{3,2},{4,5},{5,4},{6,7},{7,6},{8,9},{9,8},{10,11... | collective-permute-start | bytes 5898248 | tf_op jit(solution)/shard_map/ppermute | solution.py:378
  265.2 23.9 %collective-permute-start.31 = (f32[6,128]{1,0:T(8,128)S(1)}, f32[6,128]{1,0:T(8,128)S(1)}, u32[]{:S(2)}, u32[]{:S(2)}) collective-permute-start(f32[6,128]{1,0:T(8,128)S(1)} %copy-done.35), channel_id=1, source_target_pairs={{0,0},{1,4},{2,2},{3,6},{4,1},{5,5},{6,3},{7,7},{8,8},{9,12},{10,1... | collective-permute-start | bytes 9224 | tf_op jit(solution)/shard_map/ppermute | solution.py:378
  265.9 24.8 %collective-permute-start.32 = (f32[6,128]{1,0:T(8,128)S(1)}, f32[6,128]{1,0:T(8,128)S(1)}, u32[]{:S(2)}, u32[]{:S(2)}) collective-permute-start(f32[6,128]{1,0:T(8,128)S(1)} %copy-done.36), channel_id=1, source_target_pairs={{0,0},{1,4},{2,2},{3,6},{4,1},{5,5},{6,3},{7,7},{8,8},{9,12},{10,1... | collective-permute-start | bytes 9224 | tf_op jit(solution)/shard_map/ppermute | solution.py:378
  267.2 44.4 %collective-permute-start.34 = (bf16[3,640,256]{2,1,0:T(8,128)(2,1)}, bf16[3,640,256]{2,1,0:T(8,128)(2,1)}, u32[]{:S(2)}, u32[]{:S(2)}) collective-permute-start(bf16[3,640,256]{2,1,0:T(8,128)(2,1)} %collective-permute-done.33), channel_id=1, source_target_pairs={{8,0},{9,1},{10,2},{11,3},{12,4},{13,5},{14,6},{15,7},{16,24},{17,... | collective-permute-start | bytes 2949128 | tf_op jit(solution)/shard_map/ppermute | solution.py:459
  268.5 64.1 %collective-permute-start.37 = (bf16[3,640,256]{2,1,0:T(8,128)(2,1)}, bf16[3,640,256]{2,1,0:T(8,128)(2,1)S(1)}, u32[]{:S(2)}, u32[]{:S(2)}) collective-permute-start(bf16[3,640,256]{2,1,0:T(8,128)(2,1)} %collective-permute-done.36), channel_id=1, source_target_pairs={{8,0},{9,1},{10,2},{11,3},{12,4},{13,5},{14,6},{15,7},{16,24},{17,... | collective-permute-start | bytes 2949128 | tf_op jit(solution)/shard_map/ppermute | solution.py:459
  283.0 8.5 %collective-permute-start.28 = (f32[8,1024]{1,0:T(8,128)}, f32[8,1024]{1,0:T(8,128)S(1)}, u32[]{:S(2)}, u32[]{:S(2)}) collective-permute-start(f32[8,1024]{1,0:T(8,128)} %get-tuple-element.47.refs_2_), channel_id=1, source_target_pairs={{0,4},{1,5},{2,6},{3,7},{4,0},{5,1},{6,2},{7,3},{8,12},{9,13},{10,... | collective-permute-start | bytes 98312 | tf_op jit(solution)/shard_map/ppermute | solution.py:378
  313.4 21.5 %collective-permute-start.35 = (bf16[3,640,256]{2,1,0:T(8,128)(2,1)S(1)}, bf16[3,640,256]{2,1,0:T(8,128)(2,1)}, u32[]{:S(2)}, u32[]{:S(2)}) collective-permute-start(bf16[3,640,256]{2,1,0:T(8,128)(2,1)S(1)} %add.137.refs_21_), channel_id=1, source_target_pairs={{0,1},{1,0},{2,3},{3,2},{4,5},{5,4},{6,7},{7,6},{8,9},{9,8},{10,11... | collective-permute-start | bytes 2949128 | tf_op jit(solution)/shard_map/ppermute | solution.py:378
  (44 other events, 705.7 us)

commit v6 on v5

--- a/solution.py
+++ b/solution.py
@@ -265,7 +265,7 @@
     )(qk, qk, *partial_sums, *gains, bias)
 
 
-def mix_values(weights, values, xs, blocks, at, order, place, groups, capacity, piece):
+def mix_values(weights, values, xs, blocks, extra, at, order, place, groups, capacity, piece):
     parts, (count, total, _) = len(weights), weights[0].shape
     heads = parts * count
     packed, _, cols = values.shape
@@ -280,13 +280,17 @@
 
     def body(order_ref, place_ref, at_ref, *refs):
         weight_refs, x_refs, refs = refs[:parts], refs[parts : parts + m * k], refs[parts + m * k :]
-        w_refs, (acc_ref, out_ref, held, *staged) = refs[:k], refs[k:]
+        w_refs, e_refs, refs = refs[:k], refs[k : k + len(extra)], refs[k + len(extra) :]
+        acc_ref, out_ref, held, *staged = refs
         head = pl.program_id(0)
 
         @pl.when(head % share == 0)
         def _():
             left = [jnp.concatenate([x_refs[i * k + j][0] for j in range(k)], axis=1) for i in range(m)]
-            right = jnp.concatenate([ref[0] for ref in w_refs], axis=0)
+            sides = [ref[0] for ref in w_refs]
+            if extra:
+                sides = [side + ref[0] for side, ref in zip(sides, e_refs)]
+            right = jnp.concatenate(sides, axis=0)
             done = acc_ref[0] + jnp.dot(jnp.concatenate(left, axis=0), right, preferred_element_type=jnp.float32)
             for i in range(share):
                 held[i] = done[:, i * dim : (i + 1) * dim].astype(held.dtype)
@@ -319,7 +323,7 @@
             grid=(heads,),
             in_specs=[weight_block(i) for i in range(parts)]
             + [pl.BlockSpec((1, size, depth), lambda h, o, s, a, j=j: (a[j], 0, 0)) for size in sizes for j in range(k)]
-            + [pl.BlockSpec((1, depth, cols), lambda h, o, s, a: (h // share, 0, 0))] * k
+            + [pl.BlockSpec((1, depth, cols), lambda h, o, s, a: (h // share, 0, 0))] * (k + len(extra))
             + [pl.BlockSpec((1, total, cols), lambda h, o, s, a: (h // share, 0, 0))],
             out_specs=pl.BlockSpec((groups, n, capacity * piece, dim), lambda h, o, s, a: (0, 0, 0, h)),
             scratch_shapes=[pltpu.VMEM((share, total, dim), jnp.bfloat16)]
@@ -331,7 +335,7 @@
             transcendentals=0,
         ),
         name="mix_values",
-    )(order, place, at, *weights, *[x for x in xs for _ in range(k)], *blocks, values)
+    )(order, place, at, *weights, *[x for x in xs for _ in range(k)], *blocks, *extra, values)
 
 
 def place_tiles(returned, tile_owner, groups, n, capacity):
@@ -508,13 +512,16 @@
     bias = jnp.pad(bias, ((0, 0), (0, dim - TILES_OWN)))
     bias = jnp.tile(jnp.repeat(bias, piece, axis=0), (n, 1))
     weights = [soft_weights(qk, partial_sums, gains, after(bias, values), features, 0, heads)]
+    extra = []
     if planes == 4:
-        v_own.append(after(v_crossed, weights[0]) + v_passed[0])
-        v_own.append(after(v_crossed_next, weights[0]) + v_passed[1])
+        v_own += [v_crossed, v_crossed_next]
+        for passed in v_passed:
+            passed = after(passed, weights[0])
+            extra += [passed, other_core(passed)]
     else:
         v_own.append(ring(after(v_own[-1], sums)))
     blocks, at = blocks_of(v_own, range(split, planes))
-    mixed = mix_values(weights, values, pieces, blocks, at, order, place, groups, capacity, piece)
+    mixed = mix_values(weights, values, pieces, blocks, extra, at, order, place, groups, capacity, piece)
     returned = lax.all_to_all(
         mixed.reshape(groups * n, capacity * piece, heads * dim), AXES, split_axis=0, concat_axis=0, tiled=True
     )

time: 415 us -> 414 us (level)
    ppermute x31 -> x33, waiting for transfers between devices: 76.6 us -> 77.2 us  [send(): return lax.ppermute(value, AXES, pairs)]
    ppermute x31 -> x33, starting transfers between devices: 93.7 us -> 93.6 us  [send(): return lax.ppermute(value, AXES, pairs)]
  transfers between devices with their start and end apart: 39 -> 41, of which waited for: 14 -> 14; matrix products, arithmetic and copies ran while one was open for 4% -> 3% of each run, Pallas kernels for 16% -> 16%
where the time goes in v6:
time: 414 us; the launch traced here: 413 us
  waiting for transfers between devices  140 us (34%)
  starting transfers between devices  106 us (26%)
  Pallas kernels  90 us (22%)
  blocking collectives  55.2 us (13%)
  local copies, waits for them, and re-layouts  11.4 us (3%)
  other arithmetic  10.1 us (2%)
    ppermute x33, starting transfers between devices, send(): return lax.ppermute(value, AXES, pairs)  93.6 us
    ppermute x33, waiting for transfers between devices, send(): return lax.ppermute(value, AXES, pairs)  77.2 us
    ppermute x8, waiting for transfers between devices, send_some(): return lax.ppermute(value, AXES, pairs)  62.8 us
    all_to_all x1, blocking collectives, transposed(): lax.all_to_all(mixed.reshape(groups * n, capacity * piece, heads * dim),...  55.2 us
    pallas_call x3, Pallas kernels, project(): pl.pallas_call(body, out_shape=out_shape, grid_spec=pltpu.PrefetchScalarG...  42.8 us
    pallas_call x1, Pallas kernels, mix_values(): pl.pallas_call(body, out_shape=jax.ShapeDtypeStruct((groups, n, capacity...  19.1 us
    pallas_call x1, Pallas kernels, soft_weights(): pl.pallas_call(body, out_shape=jax.ShapeDtypeStruct((count, total, total)...  13.4 us
    ppermute x8, starting transfers between devices, send_some(): return lax.ppermute(value, AXES, pairs)  12.5 us
  transfers between devices with their start and end apart: 41, of which 14 were waited for; matrix products, arithmetic and copies ran while one was open for 3% of the time, Pallas kernels for 16%

profile of v6, /device:TPU:0, one launch (start us, length us, event | category | flops | bytes accessed | tf_op | source)
XLA Modules:
  0.0 413.3 jit_solution(560024355121527979)
XLA Ops:
  0.7 3.5 pick_tiles.1
  7.6 5.5 %collective-permute-start.3 = (bf16[2,16,5120]{2,1,0:T(8,128)(2,1)S(1)}, bf16[2,16,5120]{2,1,0:T(8,128)(2,1)S(1)}, u32[]{:S(2)}, u32[]{:S(2)}) collective-permute-start(bf16[2,16,5120]{2,1,0:T(8,128)(2,1)S(1)} %copy-done.33), channel_id=1, source_target_pairs={{0,1},{1,5},{2,3},{3,7},{4,8},{5,12},{6,10},{7,14},{8,9},{9,13},{1... | collective-permute-start | bytes 983048 | tf_op jit(solution)/shard_map/ppermute | solution.py:382
  14.7 2.4 collective-permute-start.5
  18.4 8.0 %collective-permute-done.3.rest_1_ = bf16[2,16,5120]{2,1,0:T(8,128)(2,1)S(1)} collective-permute-done((bf16[2,16,5120]{2,1,0:T(8,128)(2,1)S(1)}, bf16[2,16,5120]{2,1,0:T(8,128)(2,1)S(1)}, u32[]{:S(2)}, u32[]{:S(2)}) %collective-permute-start.3) | collective-permute-done | bytes 327712 | tf_op jit(solution)/shard_map/ppermute | solution.py:382
  26.4 23.3 %collective-permute-start.7 = (bf16[2,16,5120]{2,1,0:T(8,128)(2,1)S(1)}, bf16[2,16,5120]{2,1,0:T(8,128)(2,1)S(1)}, u32[]{:S(2)}, u32[]{:S(2)}) collective-permute-start(bf16[2,16,5120]{2,1,0:T(8,128)(2,1)S(1)} %copy-done.29), channel_id=1, source_target_pairs={{0,17},{1,21},{2,19},{3,23},{4,24},{5,28},{6,26},{7,30},{8,25},{9,... | collective-permute-start | bytes 983048 | tf_op jit(solution)/shard_map/ppermute | solution.py:382
  49.7 3.2 collective-permute-start.8
  53.0 11.7 %collective-permute-done.7.rest_5_ = bf16[2,16,5120]{2,1,0:T(8,128)(2,1)S(1)} collective-permute-done((bf16[2,16,5120]{2,1,0:T(8,128)(2,1)S(1)}, bf16[2,16,5120]{2,1,0:T(8,128)(2,1)S(1)}, u32[]{:S(2)}, u32[]{:S(2)}) %collective-permute-start.7) | collective-permute-done | bytes 327712 | tf_op jit(solution)/shard_map/ppermute | solution.py:382
  64.9 7.0 %collective-permute-done.9.rest_7_ = bf16[2,16,5120]{2,1,0:T(8,128)(2,1)S(1)} collective-permute-done((bf16[2,16,5120]{2,1,0:T(8,128)(2,1)S(1)}, bf16[2,16,5120]{2,1,0:T(8,128)(2,1)S(1)}, u32[]{:S(2)}, u32[]{:S(2)}) %collective-permute-start.9) | collective-permute-done | bytes 327712 | tf_op jit(solution)/shard_map/ppermute | solution.py:382
  73.9 11.9 %collective-permute-start.15 = (bf16[6,640,256]{2,1,0:T(8,128)(2,1)S(1)}, bf16[6,640,256]{2,1,0:T(8,128)(2,1)}, u32[]{:S(2)}, u32[]{:S(2)}) collective-permute-start(bf16[6,640,256]{2,1,0:T(8,128)(2,1)S(1)} %collective-permute-done.14.refs_30_), channel_id=1, source_target_pairs={{0,8},{1,9},{2,10},{3,11},{4,12},{5,13},{6,14},{7,15},{8,0},{9,1},... | collective-permute-start | bytes 5898248 | tf_op jit(solution)/shard_map/ppermute | solution.py:382
  89.7 8.5 %norm_tiles.1.refs_0_.refs_1_.refs_2_.refs_3_.refs_4_.refs_5_ = bf16[8,256,640]{2,1,0:T(8,128)(2,1)} custom-call(s32[16]{0:T(128)} %broadcast_maximum_fusion.1.member_ref, s32[16]{0:T(128)} %iota.28.place_ref, s32[2]{0:T(128)} %pad_add_fusion.3.ids_ref, f32[4,2,5120]{2,1,0:T(2,128)} %copy-done.20, bf16[2,16,5120]{2,1,0:T(8,128)(2,1)} %copy-done.12, ...), custom_call_target="tpu_custom_call" | custom-call | flops 15728640 | bytes 5242880 | tf_op jit(solution)/shard_map/norm_tiles/pallas_call | solution.py:117
  98.2 9.6 %collective-permute-start.10 = (bf16[8,256,640]{2,1,0:T(8,128)(2,1)}, bf16[8,256,640]{2,1,0:T(8,128)(2,1)S(1)}, u32[]{:S(2)}, u32[]{:S(2)}) collective-permute-start(bf16[8,256,640]{2,1,0:T(8,128)(2,1)} %norm_tiles.1.refs_0_.refs_1_.refs_2_.refs_3_.refs_4_.refs_5_), channel_id=1, source_target_pairs={{0,4},{1,5},{2,6},{3,7},{4,0},{5,1},{6,2},{7,3},{8,12},{9,13},{10,... | collective-permute-start | bytes 7864328 | tf_op jit(solution)/shard_map/ppermute | solution.py:382
  112.8 14.7 %collective-permute-done.15.refs_32_ = bf16[6,640,256]{2,1,0:T(8,128)(2,1)} collective-permute-done((bf16[6,640,256]{2,1,0:T(8,128)(2,1)S(1)}, bf16[6,640,256]{2,1,0:T(8,128)(2,1)}, u32[]{:S(2)}, u32[]{:S(2)}) %collective-permute-start.15) | collective-permute-done | bytes 1966112 | tf_op jit(solution)/shard_map/ppermute | solution.py:382
  127.5 2.0 collective-permute-start.19
  131.5 39.7 %collective-permute-done.21 = bf16[6,640,256]{2,1,0:T(8,128)(2,1)S(1)} collective-permute-done((bf16[6,640,256]{2,1,0:T(8,128)(2,1)}, bf16[6,640,256]{2,1,0:T(8,128)(2,1)S(1)}, u32[]{:S(2)}, u32[]{:S(2)}) %collective-permute-start.21) | collective-permute-done | bytes 1966112 | tf_op jit(solution)/shard_map/ppermute | solution.py:463
  171.3 3.4 add.127.refs_34_
  174.7 8.8 %collective-permute-start.20 = (bf16[6,640,256]{2,1,0:T(8,128)(2,1)}, bf16[6,640,256]{2,1,0:T(8,128)(2,1)}, u32[]{:S(2)}, u32[]{:S(2)}) collective-permute-start(bf16[6,640,256]{2,1,0:T(8,128)(2,1)} %collective-permute-done.15.refs_32_), channel_id=1, source_target_pairs={{0,1},{1,0},{2,3},{3,2},{4,5},{5,4},{6,7},{7,6},{8,9},{9,8},{10,11... | collective-permute-start | bytes 5898248 | tf_op jit(solution)/shard_map/ppermute | solution.py:382
  186.1 3.7 collective-permute-done.24.refs_22_
  189.7 7.0 %collective-permute-start.12 = (bf16[8,128,640]{2,1,0:T(8,128)(2,1)}, bf16[8,128,640]{2,1,0:T(8,128)(2,1)S(1)}, u32[]{:S(2)}, u32[]{:S(2)}) collective-permute-start(bf16[8,128,640]{2,1,0:T(8,128)(2,1)} %slice.36), channel_id=1, source_target_pairs={{0,4},{1,5},{2,6},{3,7},{4,0},{5,1},{6,2},{7,3},{8,12},{9,13},{10,... | collective-permute-start | bytes 3932168 | tf_op jit(solution)/shard_map/ppermute | solution.py:382
  202.0 24.3 %collective-permute-done.12.refs_18_.refs_19_.refs_20_.refs_21_.refs_22_.refs_23_.refs_12_.refs_13_.refs_14_.refs_15_.refs_6_.refs_7_.refs_16_ = bf16[8,128,640]{2,1,0:T(8,128)(2,1)S(1)} collective-permute-done((bf16[8,128,640]{2,1,0:T(8,128)(2,1)}, bf16[8,128,640]{2,1,0:T(8,128)(2,1)S(1)}, u32[]{:S(2)}, u32[]{:S(2)}) %collective-permute-start.12) | collective-permute-done | bytes 1310752 | tf_op jit(solution)/shard_map/ppermute | solution.py:382
  229.1 20.4 %project.3.refs_12_ = f32[6,1024,256]{2,1,0:T(8,128)} custom-call(s32[6]{0:T(128)} %stack.84.at_ref, bf16[8,256,640]{2,1,0:T(8,128)(2,1)} %norm_tiles.1.refs_0_.refs_1_.refs_2_.refs_3_.refs_4_.refs_5_, bf16[8,256,640]{2,1,0:T(8,128)(2,1)} %norm_tiles.1.refs_0_.refs_1_.refs_2_.refs_3_.refs_4_.refs_5_, ...), custom_call_target="tpu_custom_call" | custom-call | flops 12079595520 | bytes 32243712 | tf_op jit(solution)/shard_map/project/pallas_call | solution.py:187
  249.5 9.7 %project.4.refs_29_ = f32[3,1024,256]{2,1,0:T(8,128)} custom-call(s32[4]{0:T(128)} %pad_add_fusion.4.at_ref, bf16[8,256,640]{2,1,0:T(8,128)(2,1)} %norm_tiles.1.refs_0_.refs_1_.refs_2_.refs_3_.refs_4_.refs_5_, bf16[8,256,640]{2,1,0:T(8,128)(2,1)} %norm_tiles.1.refs_0_.refs_1_.refs_2_.refs_3_.refs_4_.refs_5_, ...), custom_call_target="tpu_custom_call" | custom-call | flops 4026531840 | bytes 15466496 | tf_op jit(solution)/shard_map/project/pallas_call | solution.py:187
  259.2 2.7 add.128.refs_10_
  270.3 12.7 %project.5 = (f32[6,1024,256]{2,1,0:T(8,128)}, f32[8,1024]{1,0:T(8,128)}) custom-call(s32[2]{0:T(128)} %pad_add_fusion.2.at_ref, bf16[8,256,640]{2,1,0:T(8,128)(2,1)} %norm_tiles.1.refs_0_.refs_1_.refs_2_.refs_3_.refs_4_.refs_5_, bf16[8,256,640]{2,1,0:T(8,128)(2,1)} %norm_tiles.1.refs_0_.refs_1_.refs_2_.refs_3_.refs_4_.refs_5_, ...), custom_call_target="tpu_custom_call", output_to_operand_aliasing={{0}: (13, {})} | custom-call | flops 4026531840 | bytes 19136512 | tf_op jit(solution)/shard_map/project/pallas_call | solution.py:187
  283.0 6.1 %collective-permute-start.28 = (f32[8,1024]{1,0:T(8,128)}, f32[8,1024]{1,0:T(8,128)S(1)}, u32[]{:S(2)}, u32[]{:S(2)}) collective-permute-start(f32[8,1024]{1,0:T(8,128)} %get-tuple-element.47.refs_2_), channel_id=1, source_target_pairs={{0,4},{1,5},{2,6},{3,7},{4,0},{5,1},{6,2},{7,3},{8,12},{9,13},{10,... | collective-permute-start | bytes 98312 | tf_op jit(solution)/shard_map/ppermute | solution.py:382
  291.6 2.0 collective-permute-done.29.refs_4_
  293.6 2.1 collective-permute-done.30.refs_5_
  296.3 13.4 %soft_weights.1.refs_0_ = bf16[6,1024,1024]{2,1,0:T(8,128)(2,1)} custom-call(f32[6,1024,256]{2,1,0:T(8,128)} %get-tuple-element.46.refs_0_.refs_1_, f32[6,1024,256]{2,1,0:T(8,128)} %get-tuple-element.46.refs_0_.refs_1_, f32[8,1024]{1,0:T(8,128)} %get-tuple-element.47.refs_2_, f32[8,1024]{1,0:T(8,128)} %copy-done.21, f32[8,1024]{1,0:T(8,128)} %copy-done.22, ...), custom_call_target="tpu_custom_call" | custom-call | flops 1660944384 | bytes 18874368 | tf_op jit(solution)/shard_map/soft_weights/pallas_call | solution.py:247
  311.6 21.2 %collective-permute-done.39.refs_27_ = bf16[3,640,256]{2,1,0:T(8,128)(2,1)} collective-permute-done((bf16[3,640,256]{2,1,0:T(8,128)(2,1)}, bf16[3,640,256]{2,1,0:T(8,128)(2,1)}, u32[]{:S(2)}, u32[]{:S(2)}) %collective-permute-start.39) | collective-permute-done | bytes 983072 | tf_op jit(solution)/shard_map/ppermute | solution.py:463
  333.4 2.3 collective-permute-done.40.refs_28_
  336.2 19.1 %mix_values.1 = bf16[8,4,32,768]{3,2,1,0:T(8,128)(2,1)} custom-call(s32[4]{0:T(128)} %get-tuple-element.67.order_ref, s32[16]{0:T(128)} %iota.27.place_ref, s32[4]{0:T(128)} %get-tuple-element.68.at_ref, bf16[6,1024,1024]{2,1,0:T(8,128)(2,1)} %soft_weights.1.refs_0_, bf16[8,256,640]{2,1,0:T(8,128)(2,1)} %norm_tiles.1.refs_0_.refs_1_.refs_2_.refs_3_.refs_4_.refs_5_, ...), custom_call_target="tpu_custom_call" | custom-call | flops 5637144576 | bytes 17301504 | tf_op jit(solution)/shard_map/mix_values/pallas_call | solution.py:318
  355.4 55.2 %all_to_all.5.in_ref = bf16[32,32,768]{2,1,0:T(8,128)(2,1)} all-to-all(bf16[32,32,768]{2,1,0:T(8,128)(2,1)} %bitcast.19), channel_id=1, replica_groups=mesh['bal'=8,'seq'=4] {'bal','seq'}, dimensions={0} | all-to-all | bytes 3145728 | tf_op jit(solution)/shard_map/all_to_all | solution.py:525
  410.6 2.7 place_tiles.1
  (161 shorter events, 45.0 us)
Async XLA Ops:
  6.1 65.8 %collective-permute-start.14 = (bf16[6,640,256]{2,1,0:T(8,128)(2,1)S(1)}, bf16[6,640,256]{2,1,0:T(8,128)(2,1)S(1)}, u32[]{:S(2)}, u32[]{:S(2)}) collective-permute-start(bf16[6,640,256]{2,1,0:T(8,128)(2,1)S(1)} %slice.32), channel_id=1, source_target_pairs={{0,0},{1,4},{2,2},{3,6},{4,1},{5,5},{6,3},{7,7},{8,8},{9,12},{10,1... | collective-permute-start | bytes 5898248 | tf_op jit(solution)/shard_map/ppermute | solution.py:382
  6.9 10.2 %collective-permute-start.2 = (bf16[2,16,5120]{2,1,0:T(8,128)(2,1)S(1)}, bf16[2,16,5120]{2,1,0:T(8,128)(2,1)S(1)}, u32[]{:S(2)}, u32[]{:S(2)}) collective-permute-start(bf16[2,16,5120]{2,1,0:T(8,128)(2,1)S(1)} %copy-done.34), channel_id=1, source_target_pairs={{0,0},{1,4},{2,2},{3,6},{4,1},{5,5},{6,3},{7,7},{8,8},{9,12},{10,1... | collective-permute-start | bytes 983048 | tf_op jit(solution)/shard_map/ppermute | solution.py:382
  7.6 18.8 %collective-permute-start.3 = (bf16[2,16,5120]{2,1,0:T(8,128)(2,1)S(1)}, bf16[2,16,5120]{2,1,0:T(8,128)(2,1)S(1)}, u32[]{:S(2)}, u32[]{:S(2)}) collective-permute-start(bf16[2,16,5120]{2,1,0:T(8,128)(2,1)S(1)} %copy-done.33), channel_id=1, source_target_pairs={{0,1},{1,5},{2,3},{3,7},{4,8},{5,12},{6,10},{7,14},{8,9},{9,13},{1... | collective-permute-start | bytes 983048 | tf_op jit(solution)/shard_map/ppermute | solution.py:382
  13.1 36.6 %collective-permute-start.4 = (bf16[2,16,5120]{2,1,0:T(8,128)(2,1)S(1)}, bf16[2,16,5120]{2,1,0:T(8,128)(2,1)S(1)}, u32[]{:S(2)}, u32[]{:S(2)}) collective-permute-start(bf16[2,16,5120]{2,1,0:T(8,128)(2,1)S(1)} %copy-done.32), channel_id=1, source_target_pairs={{0,8},{1,12},{2,10},{3,14},{4,9},{5,13},{6,11},{7,15},{8,16},{9,20... | collective-permute-start | bytes 983048 | tf_op jit(solution)/shard_map/ppermute | solution.py:382
  14.7 38.3 %collective-permute-start.5 = (bf16[2,16,5120]{2,1,0:T(8,128)(2,1)S(1)}, bf16[2,16,5120]{2,1,0:T(8,128)(2,1)S(1)}, u32[]{:S(2)}, u32[]{:S(2)}) collective-permute-start(bf16[2,16,5120]{2,1,0:T(8,128)(2,1)S(1)} %copy-done.31), channel_id=1, source_target_pairs={{0,9},{1,13},{2,11},{3,15},{4,16},{5,20},{6,18},{7,22},{8,17},{9,2... | collective-permute-start | bytes 983048 | tf_op jit(solution)/shard_map/ppermute | solution.py:382
  17.1 35.9 %collective-permute-start.6 = (bf16[2,16,5120]{2,1,0:T(8,128)(2,1)S(1)}, bf16[2,16,5120]{2,1,0:T(8,128)(2,1)S(1)}, u32[]{:S(2)}, u32[]{:S(2)}) collective-permute-start(bf16[2,16,5120]{2,1,0:T(8,128)(2,1)S(1)} %copy-done.30), channel_id=1, source_target_pairs={{0,16},{1,20},{2,18},{3,22},{4,17},{5,21},{6,19},{7,23},{8,24},{9,... | collective-permute-start | bytes 983048 | tf_op jit(solution)/shard_map/ppermute | solution.py:382
  26.4 38.3 %collective-permute-start.7 = (bf16[2,16,5120]{2,1,0:T(8,128)(2,1)S(1)}, bf16[2,16,5120]{2,1,0:T(8,128)(2,1)S(1)}, u32[]{:S(2)}, u32[]{:S(2)}) collective-permute-start(bf16[2,16,5120]{2,1,0:T(8,128)(2,1)S(1)} %copy-done.29), channel_id=1, source_target_pairs={{0,17},{1,21},{2,19},{3,23},{4,24},{5,28},{6,26},{7,30},{8,25},{9,... | collective-permute-start | bytes 983048 | tf_op jit(solution)/shard_map/ppermute | solution.py:382
  49.7 15.2 %collective-permute-start.8 = (bf16[2,16,5120]{2,1,0:T(8,128)(2,1)S(1)}, bf16[2,16,5120]{2,1,0:T(8,128)(2,1)S(1)}, u32[]{:S(2)}, u32[]{:S(2)}) collective-permute-start(bf16[2,16,5120]{2,1,0:T(8,128)(2,1)S(1)} %copy-done.28), channel_id=1, source_target_pairs={{0,24},{1,28},{2,26},{3,30},{4,25},{5,29},{6,27},{7,31},{8,0},{9,4... | collective-permute-start | bytes 983048 | tf_op jit(solution)/shard_map/ppermute | solution.py:382
  52.9 18.9 %collective-permute-start.9 = (bf16[2,16,5120]{2,1,0:T(8,128)(2,1)S(1)}, bf16[2,16,5120]{2,1,0:T(8,128)(2,1)S(1)}, u32[]{:S(2)}, u32[]{:S(2)}) collective-permute-start(bf16[2,16,5120]{2,1,0:T(8,128)(2,1)S(1)} %copy-done.27), channel_id=1, source_target_pairs={{0,25},{1,29},{2,27},{3,31},{4,0},{5,4},{6,2},{7,6},{8,1},{9,5},{1... | collective-permute-start | bytes 983048 | tf_op jit(solution)/shard_map/ppermute | solution.py:382
  71.9 37.4 %collective-permute-start.16 = (bf16[6,640,256]{2,1,0:T(8,128)(2,1)S(1)}, bf16[6,640,256]{2,1,0:T(8,128)(2,1)}, u32[]{:S(2)}, u32[]{:S(2)}) collective-permute-start(bf16[6,640,256]{2,1,0:T(8,128)(2,1)S(1)} %collective-permute-done.14.refs_30_), channel_id=1, source_target_pairs={{8,16},{9,17},{10,18},{11,19},{12,20},{13,21},{14,22},{15,23},{16,... | collective-permute-start | bytes 5898248 | tf_op jit(solution)/shard_map/ppermute | solution.py:463
  73.9 53.6 %collective-permute-start.15 = (bf16[6,640,256]{2,1,0:T(8,128)(2,1)S(1)}, bf16[6,640,256]{2,1,0:T(8,128)(2,1)}, u32[]{:S(2)}, u32[]{:S(2)}) collective-permute-start(bf16[6,640,256]{2,1,0:T(8,128)(2,1)S(1)} %collective-permute-done.14.refs_30_), channel_id=1, source_target_pairs={{0,8},{1,9},{2,10},{3,11},{4,12},{5,13},{6,14},{7,15},{8,0},{9,1},... | collective-permute-start | bytes 5898248 | tf_op jit(solution)/shard_map/ppermute | solution.py:382
  98.2 76.4 %collective-permute-start.10 = (bf16[8,256,640]{2,1,0:T(8,128)(2,1)}, bf16[8,256,640]{2,1,0:T(8,128)(2,1)S(1)}, u32[]{:S(2)}, u32[]{:S(2)}) collective-permute-start(bf16[8,256,640]{2,1,0:T(8,128)(2,1)} %norm_tiles.1.refs_0_.refs_1_.refs_2_.refs_3_.refs_4_.refs_5_), channel_id=1, source_target_pairs={{0,4},{1,5},{2,6},{3,7},{4,0},{5,1},{6,2},{7,3},{8,12},{9,13},{10,... | collective-permute-start | bytes 7864328 | tf_op jit(solution)/shard_map/ppermute | solution.py:382
  107.8 75.6 %collective-permute-start.11 = (bf16[8,256,640]{2,1,0:T(8,128)(2,1)}, bf16[8,256,640]{2,1,0:T(8,128)(2,1)S(1)}, u32[]{:S(2)}, u32[]{:S(2)}) collective-permute-start(bf16[8,256,640]{2,1,0:T(8,128)(2,1)} %norm_tiles.1.refs_0_.refs_1_.refs_2_.refs_3_.refs_4_.refs_5_), channel_id=1, source_target_pairs={{0,2},{1,3},{2,0},{3,1},{4,6},{5,7},{6,4},{7,5},{8,10},{9,11},{10,... | collective-permute-start | bytes 7864328 | tf_op jit(solution)/shard_map/ppermute | solution.py:382
  109.3 61.9 %collective-permute-start.21 = (bf16[6,640,256]{2,1,0:T(8,128)(2,1)}, bf16[6,640,256]{2,1,0:T(8,128)(2,1)S(1)}, u32[]{:S(2)}, u32[]{:S(2)}) collective-permute-start(bf16[6,640,256]{2,1,0:T(8,128)(2,1)} %collective-permute-done.16), channel_id=1, source_target_pairs={{8,0},{9,1},{10,2},{11,3},{12,4},{13,5},{14,6},{15,7},{16,24},{17,... | collective-permute-start | bytes 5898248 | tf_op jit(solution)/shard_map/ppermute | solution.py:463
  112.1 17.4 %collective-permute-start.18 = (bf16[3,640,256]{2,1,0:T(8,128)(2,1)S(1)}, bf16[3,640,256]{2,1,0:T(8,128)(2,1)S(1)}, u32[]{:S(2)}, u32[]{:S(2)}) collective-permute-start(bf16[3,640,256]{2,1,0:T(8,128)(2,1)S(1)} %pad_maximum_fusion), channel_id=1, source_target_pairs={{0,0},{1,4},{2,2},{3,6},{4,1},{5,5},{6,3},{7,7},{8,8},{9,12},{10,1... | collective-permute-start | bytes 2949128 | tf_op jit(solution)/shard_map/ppermute | solution.py:382
  127.5 69.2 %collective-permute-start.19 = (bf16[6,640,256]{2,1,0:T(8,128)(2,1)S(1)}, bf16[6,640,256]{2,1,0:T(8,128)(2,1)S(1)}, u32[]{:S(2)}, u32[]{:S(2)}) collective-permute-start(bf16[6,640,256]{2,1,0:T(8,128)(2,1)S(1)} %collective-permute-done.14.refs_30_), channel_id=1, source_target_pairs={{0,1},{1,0},{2,3},{3,2},{4,5},{5,4},{6,7},{7,6},{8,9},{9,8},{10,11... | collective-permute-start | bytes 5898248 | tf_op jit(solution)/shard_map/ppermute | solution.py:382
  129.5 70.0 %collective-permute-start.17 = (bf16[6,640,256]{2,1,0:T(8,128)(2,1)}, bf16[6,640,256]{2,1,0:T(8,128)(2,1)}, u32[]{:S(2)}, u32[]{:S(2)}) collective-permute-start(bf16[6,640,256]{2,1,0:T(8,128)(2,1)} %collective-permute-done.15.refs_32_), channel_id=1, source_target_pairs={{8,16},{9,17},{10,18},{11,19},{12,20},{13,21},{14,22},{15,23},{16,... | collective-permute-start | bytes 5898248 | tf_op jit(solution)/shard_map/ppermute | solution.py:463
  171.3 18.5 %collective-permute-start.24 = (bf16[3,640,256]{2,1,0:T(8,128)(2,1)S(1)}, bf16[3,640,256]{2,1,0:T(8,128)(2,1)}, u32[]{:S(2)}, u32[]{:S(2)}) collective-permute-start(bf16[3,640,256]{2,1,0:T(8,128)(2,1)S(1)} %collective-permute-done.18.refs_20_), channel_id=1, source_target_pairs={{0,8},{1,9},{2,10},{3,11},{4,12},{5,13},{6,14},{7,15},{8,0},{9,1},... | collective-permute-start | bytes 2949128 | tf_op jit(solution)/shard_map/ppermute | solution.py:382
  174.7 53.3 %collective-permute-start.20 = (bf16[6,640,256]{2,1,0:T(8,128)(2,1)}, bf16[6,640,256]{2,1,0:T(8,128)(2,1)}, u32[]{:S(2)}, u32[]{:S(2)}) collective-permute-start(bf16[6,640,256]{2,1,0:T(8,128)(2,1)} %collective-permute-done.15.refs_32_), channel_id=1, source_target_pairs={{0,1},{1,0},{2,3},{3,2},{4,5},{5,4},{6,7},{7,6},{8,9},{9,8},{10,11... | collective-permute-start | bytes 5898248 | tf_op jit(solution)/shard_map/ppermute | solution.py:382
  183.4 44.6 %collective-permute-start.22 = (bf16[6,640,256]{2,1,0:T(8,128)(2,1)}, bf16[6,640,256]{2,1,0:T(8,128)(2,1)}, u32[]{:S(2)}, u32[]{:S(2)}) collective-permute-start(bf16[6,640,256]{2,1,0:T(8,128)(2,1)} %add.127.refs_34_), channel_id=1, source_target_pairs={{0,1},{1,0},{2,3},{3,2},{4,5},{5,4},{6,7},{7,6},{8,9},{9,8},{10,11... | collective-permute-start | bytes 5898248 | tf_op jit(solution)/shard_map/ppermute | solution.py:382
  189.7 36.6 %collective-permute-start.12 = (bf16[8,128,640]{2,1,0:T(8,128)(2,1)}, bf16[8,128,640]{2,1,0:T(8,128)(2,1)S(1)}, u32[]{:S(2)}, u32[]{:S(2)}) collective-permute-start(bf16[8,128,640]{2,1,0:T(8,128)(2,1)} %slice.36), channel_id=1, source_target_pairs={{0,4},{1,5},{2,6},{3,7},{4,0},{5,1},{6,2},{7,3},{8,12},{9,13},{10,... | collective-permute-start | bytes 3932168 | tf_op jit(solution)/shard_map/ppermute | solution.py:382
  198.0 30.0 %collective-permute-start.13 = (bf16[8,128,640]{2,1,0:T(8,128)(2,1)}, bf16[8,128,640]{2,1,0:T(8,128)(2,1)S(1)}, u32[]{:S(2)}, u32[]{:S(2)}) collective-permute-start(bf16[8,128,640]{2,1,0:T(8,128)(2,1)} %slice.37), channel_id=1, source_target_pairs={{0,2},{1,3},{2,0},{3,1},{4,6},{5,7},{6,4},{7,5},{8,10},{9,11},{10,... | collective-permute-start | bytes 3932168 | tf_op jit(solution)/shard_map/ppermute | solution.py:382
  199.5 59.7 %collective-permute-start.26 = (bf16[6,640,256]{2,1,0:T(8,128)(2,1)}, bf16[6,640,256]{2,1,0:T(8,128)(2,1)}, u32[]{:S(2)}, u32[]{:S(2)}) collective-permute-start(bf16[6,640,256]{2,1,0:T(8,128)(2,1)} %collective-permute-done.17), channel_id=1, source_target_pairs={{8,0},{9,1},{10,2},{11,3},{12,4},{13,5},{14,6},{15,7},{16,24},{17,... | collective-permute-start | bytes 5898248 | tf_op jit(solution)/shard_map/ppermute | solution.py:463
  226.4 23.1 %collective-permute-start.23 = (bf16[3,640,256]{2,1,0:T(8,128)(2,1)}, bf16[3,640,256]{2,1,0:T(8,128)(2,1)}, u32[]{:S(2)}, u32[]{:S(2)}) collective-permute-start(bf16[3,640,256]{2,1,0:T(8,128)(2,1)} %copy-done.7), channel_id=1, source_target_pairs={{0,1},{1,0},{2,3},{3,2},{4,5},{5,4},{6,7},{7,6},{8,9},{9,8},{10,11... | collective-permute-start | bytes 2949128 | tf_op jit(solution)/shard_map/ppermute | solution.py:382
  228.0 21.5 %collective-permute-start.25 = (bf16[3,640,256]{2,1,0:T(8,128)(2,1)}, bf16[3,640,256]{2,1,0:T(8,128)(2,1)}, u32[]{:S(2)}, u32[]{:S(2)}) collective-permute-start(bf16[3,640,256]{2,1,0:T(8,128)(2,1)} %collective-permute-done.24.refs_22_), channel_id=1, source_target_pairs={{0,1},{1,0},{2,3},{3,2},{4,5},{5,4},{6,7},{7,6},{8,9},{9,8},{10,11... | collective-permute-start | bytes 2949128 | tf_op jit(solution)/shard_map/ppermute | solution.py:382
  265.2 24.0 %collective-permute-start.31 = (f32[6,128]{1,0:T(8,128)S(1)}, f32[6,128]{1,0:T(8,128)S(1)}, u32[]{:S(2)}, u32[]{:S(2)}) collective-permute-start(f32[6,128]{1,0:T(8,128)S(1)} %copy-done.35), channel_id=1, source_target_pairs={{0,0},{1,4},{2,2},{3,6},{4,1},{5,5},{6,3},{7,7},{8,8},{9,12},{10,1... | collective-permute-start | bytes 9224 | tf_op jit(solution)/shard_map/ppermute | solution.py:382
  265.9 24.8 %collective-permute-start.32 = (f32[6,128]{1,0:T(8,128)S(1)}, f32[6,128]{1,0:T(8,128)S(1)}, u32[]{:S(2)}, u32[]{:S(2)}) collective-permute-start(f32[6,128]{1,0:T(8,128)S(1)} %copy-done.36), channel_id=1, source_target_pairs={{0,0},{1,4},{2,2},{3,6},{4,1},{5,5},{6,3},{7,7},{8,8},{9,12},{10,1... | collective-permute-start | bytes 9224 | tf_op jit(solution)/shard_map/ppermute | solution.py:382
  267.3 44.3 %collective-permute-start.37 = (bf16[3,640,256]{2,1,0:T(8,128)(2,1)}, bf16[3,640,256]{2,1,0:T(8,128)(2,1)S(1)}, u32[]{:S(2)}, u32[]{:S(2)}) collective-permute-start(bf16[3,640,256]{2,1,0:T(8,128)(2,1)} %collective-permute-done.33.refs_21_), channel_id=1, source_target_pairs={{8,0},{9,1},{10,2},{11,3},{12,4},{13,5},{14,6},{15,7},{16,24},{17,... | collective-permute-start | bytes 2949128 | tf_op jit(solution)/shard_map/ppermute | solution.py:463
  268.6 64.2 %collective-permute-start.39 = (bf16[3,640,256]{2,1,0:T(8,128)(2,1)}, bf16[3,640,256]{2,1,0:T(8,128)(2,1)}, u32[]{:S(2)}, u32[]{:S(2)}) collective-permute-start(bf16[3,640,256]{2,1,0:T(8,128)(2,1)} %collective-permute-done.35.refs_23_), channel_id=1, source_target_pairs={{8,0},{9,1},{10,2},{11,3},{12,4},{13,5},{14,6},{15,7},{16,24},{17,... | collective-permute-start | bytes 2949128 | tf_op jit(solution)/shard_map/ppermute | solution.py:463
  291.6 41.8 %collective-permute-start.34 = (bf16[3,640,256]{2,1,0:T(8,128)(2,1)}, bf16[3,640,256]{2,1,0:T(8,128)(2,1)S(1)}, u32[]{:S(2)}, u32[]{:S(2)}) collective-permute-start(bf16[3,640,256]{2,1,0:T(8,128)(2,1)} %collective-permute-done.33.refs_21_), channel_id=1, source_target_pairs={{0,1},{1,0},{2,3},{3,2},{4,5},{5,4},{6,7},{7,6},{8,9},{9,8},{10,11... | collective-permute-start | bytes 2949128 | tf_op jit(solution)/shard_map/ppermute | solution.py:382
  293.6 39.8 %collective-permute-start.36 = (bf16[3,640,256]{2,1,0:T(8,128)(2,1)}, bf16[3,640,256]{2,1,0:T(8,128)(2,1)S(1)}, u32[]{:S(2)}, u32[]{:S(2)}) collective-permute-start(bf16[3,640,256]{2,1,0:T(8,128)(2,1)} %collective-permute-done.35.refs_23_), channel_id=1, source_target_pairs={{0,1},{1,0},{2,3},{3,2},{4,5},{5,4},{6,7},{7,6},{8,9},{9,8},{10,11... | collective-permute-start | bytes 2949128 | tf_op jit(solution)/shard_map/ppermute | solution.py:382
  311.6 21.8 %collective-permute-start.38 = (bf16[3,640,256]{2,1,0:T(8,128)(2,1)S(1)}, bf16[3,640,256]{2,1,0:T(8,128)(2,1)}, u32[]{:S(2)}, u32[]{:S(2)}) collective-permute-start(bf16[3,640,256]{2,1,0:T(8,128)(2,1)S(1)} %collective-permute-done.37.refs_25_), channel_id=1, source_target_pairs={{0,1},{1,0},{2,3},{3,2},{4,5},{5,4},{6,7},{7,6},{8,9},{9,8},{10,11... | collective-permute-start | bytes 2949128 | tf_op jit(solution)/shard_map/ppermute | solution.py:382
  (46 other events, 724.5 us)
